TPU v7x, 32 devices: a whole 2x2x4 slice. The times are simulated.
32 devices in a mesh: stn: 8 (over y, x, core), seg: 4 (over z).
Axes of the slice: x: 2, y: 2, z: 4, core: 2. Of those that a mesh axis runs over, the one named last changes fastest.
Arguments:
- spectra: bfloat16 [512, 5, 4, 2, 2048], P('stn', None, 'seg'), may hold values from -6 to 6
- segment_valid: int32 [512, 4], P('stn', 'seg'), may hold values 0 or 1
- pair_live: int32 [8, 5], P('stn'), may hold values 0 or 1
Outputs:
- cross: float32 [512, 5, 5, 2, 128], P(('stn', 'seg'))
All inputs are finite; a program needn't handle non-finite values. No bound on the sum of `segment_valid` or of `pair_live` on one device may be relied on, other than what follows from the above.
Results may differ from a plain program's by a relative error of at most 0.0003.
Values may be sent and summed in bfloat16 or wider, within the bound.
No kernel may reach another device: no remote copies, remote signals or barrier semaphores. Data moves between devices by JAX's collectives and lax.ppermute only.
A program may use at most 64 MiB of HBM per device.

v0:
```python
import math

import jax
import jax.numpy as jnp
from jax import lax
from jax.sharding import PartitionSpec as P

PAIRS = 5


def from_behind(block, axis, distance):
    devices = range(lax.axis_size(axis))
    route = [((i - distance) % len(devices), i) for i in devices]
    return lax.ppermute(block, axis, route)


def per_device(spectra, segment_valid, pair_live):
    block_rows, channels, seg_local, _, freq_len = spectra.shape
    masked = spectra * segment_valid.astype(jnp.bfloat16)[:, None, :, None, None]
    local_rows = masked.reshape(block_rows * channels, seg_local * 2 * freq_len)
    ref_rows = masked[:, 2:4]
    factor = 1.0 / math.sqrt(seg_local * lax.axis_size("seg") * freq_len)
    partial_terms = []
    for offset in range(PAIRS):
        if offset == 0:
            remote = ref_rows
        else:
            remote = from_behind(ref_rows, "stn", offset)
        rotated = jnp.stack([-remote[:, :, :, 1], remote[:, :, :, 0]], axis=3)
        stacked = jnp.stack([remote, rotated], axis=0).reshape(
            4 * block_rows, seg_local * 2 * freq_len
        )
        product = lax.dot_general(
            local_rows, stacked, (((1,), (1,)), ((), ())), preferred_element_type=jnp.float32
        )
        live_flag = pair_live[0, offset].astype(jnp.float32)
        pair_term = product.reshape(block_rows, channels, 2, 2 * block_rows) * (factor * live_flag)
        partial_terms.append(lax.psum_scatter(pair_term, "seg", scatter_dimension=0, tiled=True))
    return jnp.stack(partial_terms, axis=2)


def solution(mesh):
    return jax.shard_map(
        per_device,
        mesh=mesh,
        in_specs=(P("stn", None, "seg", None, None), P("stn", "seg"), P("stn", None)),
        out_specs=P(("stn", "seg"), None, None, None, None),
        check_vma=False,
    )
```

profile of v0, /device:TPU:0, one launch (start us, length us, event | category | flops | bytes accessed | tf_op | source)
XLA Modules:
  0.0 166.4 jit_solution(17446326762756376191)
XLA Ops:
  6.5 0.0 reduce-scatter.6.cloned.1.call-start
  6.5 0.7 convert_bitcast_fusion
  7.2 4.0 %broadcast_multiply_fusion = bf16[64,5,1,2,2048]{4,3,2,1,0:T(2,128)(2,1)S(1)} fusion(bf16[64,5,1,2,2048]{4,3,2,1,0:T(2,128)(2,1)} %param.3, bf16[64]{0:T(256)(128)(2,1)S(1)} %convert_bitcast_fusion), kind=kLoop, calls=%fused_computation.25 | loop fusion | flops 1310720 | bytes 5243008 | tf_op jit(solution)/shard_map/mul | solution.py:19
  11.2 2.2 %slice.66 = bf16[64,2,1,2,2048]{4,3,2,1,0:T(2,128)(2,1)} slice(bf16[64,5,1,2,2048]{4,3,2,1,0:T(2,128)(2,1)S(1)} %broadcast_multiply_fusion), slice={[0:64], [2:4], [0:1], [0:2], [0:2048]} | slice | bytes 2097152 | tf_op jit(solution)/shard_map/slice | solution.py:21
  13.4 0.5 collective-permute-start
  13.9 3.3 %slice_negate_fusion.4 = (bf16[64,2,1,1,2048]{4,3,2,1,0:T(2,128)(2,1)}, bf16[64,2,1,1,2048]{4,3,2,1,0:T(2,128)(2,1)}) fusion(bf16[64,5,1,2,2048]{4,3,2,1,0:T(2,128)(2,1)S(1)} %broadcast_multiply_fusion), kind=kLoop, calls=%fused_computation.35 | loop fusion | flops 262144 | bytes 2097152 | tf_op jit(solution)/shard_map/neg | solution.py:29
  17.2 2.6 %stack.83 = bf16[1,128,4096]{2,1,0:T(8,128)(2,1)} reshape(bf16[64,2,1,2,2048]{4,3,2,1,0:T(2,128)(2,1)} %slice.66) | data formatting | bytes 2097152 | tf_op jit(solution)/shard_map/stack | solution.py:30
  19.8 0.0 copy-start.1
  19.8 3.6 %copy.10 = bf16[64,5,1,2,2048]{4,3,0,1,2:T(2,128)(2,1)} copy(bf16[64,5,1,2,2048]{4,3,2,1,0:T(2,128)(2,1)S(1)} %broadcast_multiply_fusion) | data formatting | bytes 5242880 | tf_op jit(solution)/shard_map/mul | solution.py:19
  23.4 0.0 copy-done.1
  23.4 0.0 copy-done.2
  23.4 3.2 %pad_maximum_fusion = bf16[64,2,1,2,2048]{4,3,2,1,0:T(2,128)(2,1)} fusion(bf16[64,2,1,1,2048]{4,3,2,1,0:T(2,128)(2,1)S(1)} %copy-done.2, bf16[64,2,1,1,2048]{4,3,2,1,0:T(2,128)(2,1)S(1)} %copy-done.1), kind=kLoop, calls=%fused_computation.36 | loop fusion | flops 2097152 | bytes 2097152 | tf_op jit(solution)/shard_map/stack | solution.py:29
  26.6 2.6 %stack.85 = bf16[1,128,4096]{2,1,0:T(8,128)(2,1)} reshape(bf16[64,2,1,2,2048]{4,3,2,1,0:T(2,128)(2,1)} %pad_maximum_fusion) | data formatting | bytes 2097152 | tf_op jit(solution)/shard_map/stack | solution.py:30
  29.2 0.0 copy-done
  29.2 3.6 %reshape.84 = bf16[64,5,4096,1]{2,0,1,3:T(8,128)(2,1)} reshape(bf16[64,5,1,2,2048]{4,3,0,1,2:T(2,128)(2,1)S(1)} %copy-done) | data formatting | bytes 5242880 | tf_op jit(solution)/shard_map/dot_general | solution.py:33
  32.8 0.0 copy-done.3
  32.8 0.7 fusion.40
  34.2 3.9 %fusion.20 = f32[64,5,2,128]{3,0,2,1:T(8,128)} fusion(bf16[1,128,4096]{2,1,0:T(8,128)(2,1)} %stack.85, bf16[1,128,4096]{2,1,0:T(8,128)(2,1)} %stack.83, bf16[64,5,4096,1]{2,0,1,3:T(8,128)(2,1)} %reshape.84, f32[]{:T(128)} %bitcast.3), kind=kOutput, calls=%fused_computation.26 | convolution fusion | flops 675364864 | bytes 5046276 | tf_op jit(solution)/shard_map/dot_general | solution.py:33
  38.1 0.0 reduce-scatter.6.cloned.1.call-update
  38.1 0.0 reduce-scatter.8.cloned.1.call-start
  38.2 2.5 %collective-permute-start.1 = (bf16[64,2,1,2,2048]{4,3,2,1,0:T(2,128)(2,1)}, bf16[64,2,1,2,2048]{4,3,2,1,0:T(2,128)(2,1)S(1)}, u32[]{:S(2)}, u32[]{:S(2)}) collective-permute-start(bf16[64,2,1,2,2048]{4,3,2,1,0:T(2,128)(2,1)} %slice.66), channel_id=1, source_target_pairs={{24,0},{28,4},{0,8},{4,12},{8,16},{12,20},{16,24},{20,28},{25,1},{... | collective-permute-start | bytes 3145736 | tf_op jit(solution)/shard_map/ppermute | solution.py:14
  40.7 2.4 %collective-permute-start.2 = (bf16[64,2,1,2,2048]{4,3,2,1,0:T(2,128)(2,1)}, bf16[64,2,1,2,2048]{4,3,2,1,0:T(2,128)(2,1)S(1)}, u32[]{:S(2)}, u32[]{:S(2)}) collective-permute-start(bf16[64,2,1,2,2048]{4,3,2,1,0:T(2,128)(2,1)} %slice.66), channel_id=1, source_target_pairs={{20,0},{24,4},{28,8},{0,12},{4,16},{8,20},{12,24},{16,28},{21,1},{... | collective-permute-start | bytes 3145736 | tf_op jit(solution)/shard_map/ppermute | solution.py:14
  43.1 0.5 collective-permute-start.3
  46.1 14.7 %reduce-scatter.6.cloned.1.call-done = f32[16,5,2,128]{3,0,2,1:T(8,128)} async-done(((f32[64,5,2,128]{3,0,2,1:T(8,128)}), f32[16,5,2,128]{3,0,2,1:T(8,128)}) %reduce-scatter.6.cloned.1.call-update) | async-done | bytes 81936 | tf_op jit(solution)/shard_map/reduce_scatter | solution.py:38
  60.8 0.9 bitcast_dynamic-update-slice_fusion.4
  61.7 0.0 collective-permute-done
  61.7 3.9 %slice_negate_fusion.3 = (bf16[64,2,1,1,2048]{4,3,2,1,0:T(2,128)(2,1)S(1)}, bf16[64,2,1,1,2048]{4,3,2,1,0:T(2,128)(2,1)S(1)}) fusion(bf16[64,2,1,2,2048]{4,3,2,1,0:T(2,128)(2,1)} %collective-permute-done), kind=kLoop, calls=%fused_computation.34 | loop fusion | flops 262144 | bytes 2097152 | tf_op jit(solution)/shard_map/neg | solution.py:29
  65.6 3.2 %pad_maximum_fusion.1 = bf16[64,2,1,2,2048]{4,3,2,1,0:T(2,128)(2,1)} fusion(bf16[64,2,1,1,2048]{4,3,2,1,0:T(2,128)(2,1)S(1)} %get-tuple-element.14, bf16[64,2,1,1,2048]{4,3,2,1,0:T(2,128)(2,1)S(1)} %get-tuple-element.13), kind=kLoop, calls=%fused_computation.37 | loop fusion | flops 2097152 | bytes 2097152 | tf_op jit(solution)/shard_map/stack | solution.py:29
  68.8 2.6 %stack.90 = bf16[1,128,4096]{2,1,0:T(8,128)(2,1)} reshape(bf16[64,2,1,2,2048]{4,3,2,1,0:T(2,128)(2,1)} %pad_maximum_fusion.1) | data formatting | bytes 2097152 | tf_op jit(solution)/shard_map/stack | solution.py:30
  71.5 2.6 %stack.88 = bf16[1,128,4096]{2,1,0:T(8,128)(2,1)} reshape(bf16[64,2,1,2,2048]{4,3,2,1,0:T(2,128)(2,1)} %collective-permute-done) | data formatting | bytes 2097152 | tf_op jit(solution)/shard_map/stack | solution.py:30
  74.1 3.9 %fusion.23 = f32[64,5,2,128]{3,0,2,1:T(8,128)} fusion(bf16[1,128,4096]{2,1,0:T(8,128)(2,1)} %stack.90, bf16[1,128,4096]{2,1,0:T(8,128)(2,1)} %stack.88, bf16[64,5,4096,1]{2,0,1,3:T(8,128)(2,1)} %reshape.84, f32[]{:T(128)} %bitcast.6), kind=kOutput, calls=%fused_computation.27 | convolution fusion | flops 675364864 | bytes 5046276 | tf_op jit(solution)/shard_map/dot_general | solution.py:33
  78.0 0.0 reduce-scatter.8.cloned.1.call-update
  78.0 0.0 reduce-scatter.10.cloned.1.call-start
  78.1 0.0 collective-permute-done.1
  78.1 2.3 %slice_negate_fusion.2 = (bf16[64,2,1,1,2048]{4,3,2,1,0:T(2,128)(2,1)S(1)}, bf16[64,2,1,1,2048]{4,3,2,1,0:T(2,128)(2,1)S(1)}) fusion(bf16[64,2,1,2,2048]{4,3,2,1,0:T(2,128)(2,1)S(1)} %collective-permute-done.1), kind=kLoop, calls=%fused_computation.33 | loop fusion | flops 262144 | bytes 2097152 | tf_op jit(solution)/shard_map/neg | solution.py:29
  80.5 3.3 %pad_maximum_fusion.2 = bf16[64,2,1,2,2048]{4,3,2,1,0:T(2,128)(2,1)} fusion(bf16[64,2,1,1,2048]{4,3,2,1,0:T(2,128)(2,1)S(1)} %get-tuple-element.12, bf16[64,2,1,1,2048]{4,3,2,1,0:T(2,128)(2,1)S(1)} %get-tuple-element.11), kind=kLoop, calls=%fused_computation.38 | loop fusion | flops 2097152 | bytes 2097152 | tf_op jit(solution)/shard_map/stack | solution.py:29
  83.7 2.6 %stack.95 = bf16[1,128,4096]{2,1,0:T(8,128)(2,1)} reshape(bf16[64,2,1,2,2048]{4,3,2,1,0:T(2,128)(2,1)} %pad_maximum_fusion.2) | data formatting | bytes 2097152 | tf_op jit(solution)/shard_map/stack | solution.py:30
  86.3 1.6 stack.93
  88.0 4.0 %fusion.26 = f32[64,5,2,128]{3,0,2,1:T(8,128)} fusion(bf16[1,128,4096]{2,1,0:T(8,128)(2,1)} %stack.95, bf16[1,128,4096]{2,1,0:T(8,128)(2,1)} %stack.93, bf16[64,5,4096,1]{2,0,1,3:T(8,128)(2,1)} %reshape.84, f32[]{:T(128)} %bitcast.9), kind=kOutput, calls=%fused_computation.28 | convolution fusion | flops 675364864 | bytes 5046276 | tf_op jit(solution)/shard_map/dot_general | solution.py:33
  91.9 0.0 reduce-scatter.10.cloned.1.call-update
  92.0 0.3 reduce-scatter.12.cloned.1.call-start
  92.2 7.3 %collective-permute-done.2 = bf16[64,2,1,2,2048]{4,3,2,1,0:T(2,128)(2,1)S(1)} collective-permute-done((bf16[64,2,1,2,2048]{4,3,2,1,0:T(2,128)(2,1)}, bf16[64,2,1,2,2048]{4,3,2,1,0:T(2,128)(2,1)S(1)}, u32[]{:S(2)}, u32[]{:S(2)}) %collective-permute-start.2) | collective-permute-done | bytes 1048608 | tf_op jit(solution)/shard_map/ppermute | solution.py:14
  99.5 2.3 %slice_negate_fusion.1 = (bf16[64,2,1,1,2048]{4,3,2,1,0:T(2,128)(2,1)S(1)}, bf16[64,2,1,1,2048]{4,3,2,1,0:T(2,128)(2,1)S(1)}) fusion(bf16[64,2,1,2,2048]{4,3,2,1,0:T(2,128)(2,1)S(1)} %collective-permute-done.2), kind=kLoop, calls=%fused_computation.32 | loop fusion | flops 262144 | bytes 2097152 | tf_op jit(solution)/shard_map/neg | solution.py:29
  101.8 2.4 %pad_maximum_fusion.3 = bf16[64,2,1,2,2048]{4,3,2,1,0:T(2,128)(2,1)S(1)} fusion(bf16[64,2,1,1,2048]{4,3,2,1,0:T(2,128)(2,1)S(1)} %get-tuple-element.10, bf16[64,2,1,1,2048]{4,3,2,1,0:T(2,128)(2,1)S(1)} %get-tuple-element.9), kind=kLoop, calls=%fused_computation.39 | loop fusion | flops 2097152 | bytes 2097152 | tf_op jit(solution)/shard_map/stack | solution.py:29
  104.3 1.6 stack.100
  105.9 0.8 stack.98
  106.7 3.6 %fusion.29 = f32[64,5,2,128]{3,0,2,1:T(8,128)} fusion(bf16[1,128,4096]{2,1,0:T(8,128)(2,1)} %stack.100, bf16[1,128,4096]{2,1,0:T(8,128)(2,1)S(1)} %stack.98, bf16[64,5,4096,1]{2,0,1,3:T(8,128)(2,1)} %reshape.84, f32[]{:T(128)} %bitcast.12), kind=kOutput, calls=%fused_computation.29 | convolution fusion | flops 675364864 | bytes 5046276 | tf_op jit(solution)/shard_map/dot_general | solution.py:33
  110.3 0.0 reduce-scatter.12.cloned.1.call-update
  110.4 0.0 reduce-scatter.14.cloned.1.call-start
  110.4 0.0 collective-permute-done.3
  110.4 2.3 %slice_negate_fusion = (bf16[64,2,1,1,2048]{4,3,2,1,0:T(2,128)(2,1)S(1)}, bf16[64,2,1,1,2048]{4,3,2,1,0:T(2,128)(2,1)S(1)}) fusion(bf16[64,2,1,2,2048]{4,3,2,1,0:T(2,128)(2,1)S(1)} %collective-permute-done.3), kind=kLoop, calls=%fused_computation.31 | loop fusion | flops 262144 | bytes 2097152 | tf_op jit(solution)/shard_map/neg | solution.py:29
  112.8 2.4 %pad_maximum_fusion.4 = bf16[64,2,1,2,2048]{4,3,2,1,0:T(2,128)(2,1)S(1)} fusion(bf16[64,2,1,1,2048]{4,3,2,1,0:T(2,128)(2,1)S(1)} %get-tuple-element.8, bf16[64,2,1,1,2048]{4,3,2,1,0:T(2,128)(2,1)S(1)} %get-tuple-element.7), kind=kLoop, calls=%fused_computation.40 | loop fusion | flops 2097152 | bytes 2097152 | tf_op jit(solution)/shard_map/stack | solution.py:29
  115.2 0.8 stack.105
  116.1 0.8 stack.103
  116.9 3.4 %fusion.32 = f32[64,5,2,128]{3,0,2,1:T(8,128)} fusion(bf16[1,128,4096]{2,1,0:T(8,128)(2,1)S(1)} %stack.105, bf16[1,128,4096]{2,1,0:T(8,128)(2,1)S(1)} %stack.103, bf16[64,5,4096,1]{2,0,1,3:T(8,128)(2,1)} %reshape.84, f32[]{:T(128)} %bitcast.15), kind=kOutput, calls=%fused_computation.30 | convolution fusion | flops 675364864 | bytes 5046276 | tf_op jit(solution)/shard_map/dot_general | solution.py:33
  120.2 0.0 reduce-scatter.14.cloned.1.call-update
  120.3 0.0 reduce-scatter.8.cloned.1.call-done
  120.3 0.9 bitcast_dynamic-update-slice_fusion.3
  121.2 0.9 bitcast_dynamic-update-slice_fusion.2
  122.1 15.5 %reduce-scatter.12.cloned.1.call-done = f32[16,5,2,128]{3,0,2,1:T(8,128)} async-done(((f32[64,5,2,128]{3,0,2,1:T(8,128)}), f32[16,5,2,128]{3,0,2,1:T(8,128)}) %reduce-scatter.12.cloned.1.call-update) | async-done | bytes 81936 | tf_op jit(solution)/shard_map/reduce_scatter | solution.py:38
  137.6 0.9 bitcast_dynamic-update-slice_fusion.1
  138.5 19.5 %reduce-scatter.14.cloned.1.call-done = f32[16,5,2,128]{3,0,2,1:T(8,128)} async-done(((f32[64,5,2,128]{3,0,2,1:T(8,128)}), f32[16,5,2,128]{3,0,2,1:T(8,128)}) %reduce-scatter.14.cloned.1.call-update) | async-done | bytes 81936 | tf_op jit(solution)/shard_map/reduce_scatter | solution.py:38
  158.0 0.9 bitcast_dynamic-update-slice_fusion
  158.9 1.0 copy.11
  (4 shorter events, 0.0 us)
Async XLA Ops:
  6.5 54.3 %reduce-scatter.6.cloned.1.call-start = ((), (), s32[]{:S(2)}) async-start(), calls=%async_computation.5 | async-start | bytes 409600 | tf_op jit(solution)/shard_map/reduce_scatter | solution.py:38
  13.4 48.3 %collective-permute-start = (bf16[64,2,1,2,2048]{4,3,2,1,0:T(2,128)(2,1)}, bf16[64,2,1,2,2048]{4,3,2,1,0:T(2,128)(2,1)}, u32[]{:S(2)}, u32[]{:S(2)}) collective-permute-start(bf16[64,2,1,2,2048]{4,3,2,1,0:T(2,128)(2,1)} %slice.66), channel_id=1, source_target_pairs={{28,0},{0,4},{4,8},{8,12},{12,16},{16,20},{20,24},{24,28},{29,1},{... | collective-permute-start | bytes 3145736 | tf_op jit(solution)/shard_map/ppermute | solution.py:14
  19.8 3.6 %copy-start.1 = (bf16[64,2,1,1,2048]{4,3,2,1,0:T(2,128)(2,1)S(1)}, bf16[64,2,1,1,2048]{4,3,2,1,0:T(2,128)(2,1)}, u32[]{:S(2)}) copy-start(bf16[64,2,1,1,2048]{4,3,2,1,0:T(2,128)(2,1)} %get-tuple-element.5) | copy-start | bytes 1572868
  19.8 3.6 %copy-start.2 = (bf16[64,2,1,1,2048]{4,3,2,1,0:T(2,128)(2,1)S(1)}, bf16[64,2,1,1,2048]{4,3,2,1,0:T(2,128)(2,1)}, u32[]{:S(2)}) copy-start(bf16[64,2,1,1,2048]{4,3,2,1,0:T(2,128)(2,1)} %get-tuple-element.6) | copy-start | bytes 1572868
  23.4 5.8 %copy-start = (bf16[64,5,1,2,2048]{4,3,0,1,2:T(2,128)(2,1)S(1)}, bf16[64,5,1,2,2048]{4,3,0,1,2:T(2,128)(2,1)}, u32[]{:S(2)}) copy-start(bf16[64,5,1,2,2048]{4,3,0,1,2:T(2,128)(2,1)} %copy.10) | copy-start | bytes 7864324
  29.2 3.6 %copy-start.3 = (s32[1,5]{1,0:T(1,128)S(1)}, s32[1,5]{1,0:T(1,128)}, u32[]{:S(2)}) copy-start(s32[1,5]{1,0:T(1,128)} %param.5) | copy-start | bytes 64
  38.1 82.2 %reduce-scatter.8.cloned.1.call-start = ((), (), s32[]{:S(2)}) async-start(), calls=%async_computation.6 | async-start | bytes 409600 | tf_op jit(solution)/shard_map/reduce_scatter | solution.py:38
  38.2 39.9 %collective-permute-start.1 = (bf16[64,2,1,2,2048]{4,3,2,1,0:T(2,128)(2,1)}, bf16[64,2,1,2,2048]{4,3,2,1,0:T(2,128)(2,1)S(1)}, u32[]{:S(2)}, u32[]{:S(2)}) collective-permute-start(bf16[64,2,1,2,2048]{4,3,2,1,0:T(2,128)(2,1)} %slice.66), channel_id=1, source_target_pairs={{24,0},{28,4},{0,8},{4,12},{8,16},{12,20},{16,24},{20,28},{25,1},{... | collective-permute-start | bytes 3145736 | tf_op jit(solution)/shard_map/ppermute | solution.py:14
  40.7 58.8 %collective-permute-start.2 = (bf16[64,2,1,2,2048]{4,3,2,1,0:T(2,128)(2,1)}, bf16[64,2,1,2,2048]{4,3,2,1,0:T(2,128)(2,1)S(1)}, u32[]{:S(2)}, u32[]{:S(2)}) collective-permute-start(bf16[64,2,1,2,2048]{4,3,2,1,0:T(2,128)(2,1)} %slice.66), channel_id=1, source_target_pairs={{20,0},{24,4},{28,8},{0,12},{4,16},{8,20},{12,24},{16,28},{21,1},{... | collective-permute-start | bytes 3145736 | tf_op jit(solution)/shard_map/ppermute | solution.py:14
  43.1 67.3 %collective-permute-start.3 = (bf16[64,2,1,2,2048]{4,3,2,1,0:T(2,128)(2,1)}, bf16[64,2,1,2,2048]{4,3,2,1,0:T(2,128)(2,1)S(1)}, u32[]{:S(2)}, u32[]{:S(2)}) collective-permute-start(bf16[64,2,1,2,2048]{4,3,2,1,0:T(2,128)(2,1)} %slice.66), channel_id=1, source_target_pairs={{16,0},{20,4},{24,8},{28,12},{0,16},{4,20},{8,24},{12,28},{17,1},{... | collective-permute-start | bytes 3145736 | tf_op jit(solution)/shard_map/ppermute | solution.py:14
  78.0 43.1 %reduce-scatter.10.cloned.1.call-start = ((), (), s32[]{:S(2)}) async-start(), calls=%async_computation.7 | async-start | bytes 409600 | tf_op jit(solution)/shard_map/reduce_scatter | solution.py:38
  92.0 45.6 %reduce-scatter.12.cloned.1.call-start = ((), (), s32[]{:S(2)}) async-start(), calls=%async_computation.8 | async-start | bytes 409600 | tf_op jit(solution)/shard_map/reduce_scatter | solution.py:38
  110.4 47.6 %reduce-scatter.14.cloned.1.call-start = ((), (), s32[]{:S(2)}) async-start(), calls=%async_computation.9 | async-start | bytes 409600 | tf_op jit(solution)/shard_map/reduce_scatter | solution.py:38
Sparse Core Ops, SparseCore 0:
  38.2 22.5 reduce-scatter.5
  78.2 18.3 reduce-scatter.7
  98.8 18.2 reduce-scatter.9
  119.2 18.2 reduce-scatter.11
  139.7 18.2 reduce-scatter.13
where the time goes:
time: 167 us; the launch traced here: 166 us
  waiting for transfers between devices  57.1 us (34%)
  local copies, waits for them, and re-layouts  34.3 us (21%)
  other arithmetic  33.4 us (20%)
  matrix products  18.8 us (11%)
  between operations  16.4 us (10%)
  starting transfers between devices  6.31 us (4%)
    reduce_scatter x5, waiting for transfers between devices, per_device(): lax.psum_scatter(pair_term, 'seg', scatter_dimension=0, tiled=True)  49.7 us
    another operation x10, local copies, waits for them, and re-layouts, per_device(): jnp.stack([remote, rotated], axis=0)  18.8 us
    dot_general x5, matrix products, per_device(): lax.dot_general(local_rows, stacked, (((1,), (1,)), ((), ())), preferred_...  18.8 us
    another operation x5, other arithmetic, per_device(): rotated = jnp.stack([-remote[:, :, :, 1], remote[:, :, :, 0]], axis=3)  14.6 us
    neg x5, other arithmetic, per_device(): rotated = jnp.stack([-remote[:, :, :, 1], remote[:, :, :, 0]], axis=3)  14.2 us
    ppermute x4, waiting for transfers between devices, from_behind(): return lax.ppermute(block, axis, route)  7.27 us
    ppermute x4, starting transfers between devices, from_behind(): return lax.ppermute(block, axis, route)  5.92 us
    mul x2, other arithmetic, per_device(): spectra * segment_valid.astype(jnp.bfloat16)[:, None, :, None, None]  4.68 us
  transfers between devices with their start and end apart: 9, of which 4 were waited for; matrix products, arithmetic and copies ran while one was open for 47% of the time, Pallas kernels for 0%

commit v1 on v0

v1 whole, which is shorter than its diff:
```python
import functools
import math

import jax
import jax.numpy as jnp
from jax import lax
from jax.experimental import pallas as pl
from jax.experimental.pallas import tpu as pltpu
from jax.sharding import PartitionSpec as P

PAIRS = 5
CHUNKS = 4
LANES = 128
VMEM = pl.BlockSpec(memory_space=pltpu.VMEM)
HBM = pl.BlockSpec(memory_space=pl.ANY)
SMEM = pl.BlockSpec(memory_space=pltpu.SMEM)
F32 = jnp.float32
BF16 = jnp.bfloat16


def params(mib):
    return pltpu.CompilerParams(vmem_limit_bytes=mib * 2**20)


def iota(shape, dim):
    return lax.broadcasted_iota(jnp.int32, shape, dim)


def dot_t(a, b):
    return lax.dot_general(a, b, (((1,), (1,)), ((), ())), preferred_element_type=F32)


def extract_kernel(x_hbm, valid_ref, full_ref, *rest):
    *chunk_refs, buf, sem = rest
    copy = pltpu.make_async_copy(x_hbm.at[:, 2:4], buf, sem)
    copy.start()
    block = buf.shape[0]
    rows = 4 * block
    half = rows // 2
    spread = (iota((block, rows), 1) // 4 == iota((block, rows), 0)).astype(BF16)
    valid = jnp.broadcast_to(valid_ref[...], (8, block)).astype(F32).astype(BF16)
    valid = jnp.dot(valid, spread, preferred_element_type=F32)[:1]
    to, frm = iota((rows, rows), 0), iota((rows, rows), 1)
    source = jnp.where(to < half, 2 * to, 2 * (to - half) + 1)
    pick = jnp.where(frm == source, jnp.broadcast_to(valid, (rows, rows)), 0.0).astype(BF16)
    copy.wait()
    full = jnp.dot(pick, buf[...].reshape(rows, buf.shape[-1]), preferred_element_type=F32).astype(BF16)
    full_ref[...] = full
    width = half // len(chunk_refs)
    for k, chunk_ref in enumerate(chunk_refs):
        for part in range(2):
            at = part * half + k * width
            chunk_ref[part * width : (part + 1) * width] = full[at : at + width]


def store_tiles(g_ref, value):
    for tile in range(g_ref.shape[0]):
        g_ref[tile] = value[:, tile * LANES : (tile + 1) * LANES]


def combine(g_ref, out_keep, out_send, seg, members):
    tiles, rows = g_ref.shape[0], g_ref.shape[1] // members
    sign = jnp.where(iota((1, LANES), 1) < LANES // 2, 1.0, -1.0)
    for slot in range(members):
        at = pl.multiple_of((seg ^ slot) * rows, 8)
        out = out_send if slot % 2 else out_keep
        even = [g_ref[t, pl.ds(at, rows // 2, stride=2), :] for t in range(tiles)]
        odd = [g_ref[t, pl.ds(at + 1, rows // 2, stride=2), :] for t in range(tiles)]
        if tiles == 1:
            out[slot // 2] = pltpu.roll(odd[0], LANES // 2, 1) + sign * even[0]
        for t in range(tiles // 2):
            u = t + tiles // 2
            out[slot // 2, :, t * LANES : (t + 1) * LANES] = even[t] + odd[u]
            out[slot // 2, :, u * LANES : (u + 1) * LANES] = odd[t] - even[u]


def own_kernel(members, x_ref, valid_ref, full_ref, a_ref, keep_ref, send_ref, g_ref):
    block = x_ref.shape[0]
    rows = a_ref.shape[0]
    pick = (iota((rows, block), 0) // (rows // block) == iota((rows, block), 1)).astype(BF16)
    valid = jnp.broadcast_to(valid_ref[...], (8, block)).astype(F32).astype(BF16)
    valid = dot_t(pick, valid)[:, :1].astype(BF16)
    a_ref[...] = x_ref[...].reshape(a_ref.shape) * valid
    store_tiles(g_ref, dot_t(a_ref[...], full_ref[...]))
    combine(g_ref, keep_ref, send_ref, lax.axis_index("seg"), members)


def chunk_kernel(members, a_ref, sib_ref, own_ref, four_ref, low_ref, high_ref, keep_ref, send_ref, b_ref, g_ref):
    seg, stn = lax.axis_index("seg"), lax.axis_index("stn")
    first, odd = stn % 2 == 0, (stn // 2) % 2 == 1
    width = own_ref.shape[0] // 2

    def fill(which, column, ref):
        for part in range(2):
            at = (2 * part + column) * width
            b_ref[which, at : at + width] = ref[part * width : (part + 1) * width]

    def both(two_ref):
        fill(0, 0, two_ref)
        fill(0, 1, four_ref)

        @pl.when(first)
        def _():
            fill(1, 0, own_ref)
            fill(1, 1, two_ref)

        @pl.when(jnp.logical_not(first))
        def _():
            fill(1, 0, two_ref)
            fill(1, 1, four_ref)

    pl.when(odd)(lambda: both(low_ref))
    pl.when(jnp.logical_not(odd))(lambda: both(high_ref))
    store_tiles(g_ref.at[0], dot_t(a_ref[...], b_ref[0]))
    store_tiles(g_ref.at[1], dot_t(sib_ref[...], b_ref[1]))
    for which in range(2):
        combine(g_ref.at[which], keep_ref.at[which], send_ref.at[which], seg, members)


def add_kernel(keep_ref, got_ref, new_keep_ref, new_send_ref):
    for slot in range(keep_ref.shape[0]):
        out = new_send_ref if slot % 2 else new_keep_ref
        out[slot // 2] = keep_ref[slot] + got_ref[slot]


def add_last_kernel(keep_ref, got_ref, *out_refs):
    for which in range(2):
        for slot in range(2):
            out_refs[2 * which + slot][...] = keep_ref[which, slot] + got_ref[which, slot]


def final_kernel(factor, chunks, live_ref, *refs):
    *in_refs, out_ref = refs
    pairs = [in_refs[i][...] + in_refs[i + 1][...] for i in range(0, len(in_refs), 2)]
    own, mine, theirs = pairs[0], pairs[1 : 1 + chunks], pairs[1 + chunks :]
    rows = out_ref.shape[0] // (2 * PAIRS)
    lanes = out_ref.shape[1]
    for offset in range(PAIRS):
        scale = live_ref[0, offset].astype(F32) * factor
        for part in range(2):
            if offset == 0:
                value = own[:, part * lanes : (part + 1) * lanes]
            else:
                width = lanes // chunks
                at = (2 * part + (offset - 1) // 2) * width
                value = jnp.concatenate([t[:, at : at + width] for t in (theirs if offset % 2 else mine)], axis=1)
            out_ref[pl.ds(2 * offset + part, rows, stride=2 * PAIRS), :] = value * scale


def per_device(spectra, segment_valid, pair_live):
    block, channels, seg_local, _, freq = spectra.shape
    blocks, members = lax.axis_size("stn"), lax.axis_size("seg")
    factor = 1.0 / math.sqrt(seg_local * members * freq)
    valid = segment_valid.reshape(1, block)
    rows, per = 2 * block * channels, block * channels // members
    width = 2 * block // CHUNKS

    full, *own = pl.pallas_call(
        extract_kernel,
        in_specs=[HBM, VMEM],
        out_specs=[VMEM] * (1 + CHUNKS),
        out_shape=[jax.ShapeDtypeStruct((4 * block, freq), BF16)]
        + [jax.ShapeDtypeStruct((2 * width, freq), BF16)] * CHUNKS,
        scratch_shapes=[pltpu.VMEM((block, 2, 1, 2, freq), BF16), pltpu.SemaphoreType.DMA],
        compiler_params=params(12),
    )(spectra, valid)

    ids = range(blocks)
    four = [lax.ppermute(c, "stn", [((i - 4) % blocks, i) for i in ids]) for c in own]
    low = [lax.ppermute(c, "stn", [((i - 2) % blocks, i) for i in ids if i // 2 % 2 == 1]) for c in own]
    high = [lax.ppermute(c, "stn", [((i + 2) % blocks, i) for i in ids if i // 2 % 2 == 0]) for c in four]

    half = members // 2
    a, keep, send = pl.pallas_call(
        functools.partial(own_kernel, members),
        in_specs=[VMEM] * 3,
        out_specs=[VMEM] * 3,
        out_shape=[jax.ShapeDtypeStruct((rows, freq), BF16)]
        + [jax.ShapeDtypeStruct((half, per, 4 * block), F32)] * 2,
        scratch_shapes=[pltpu.VMEM((4 * block // LANES, rows, LANES), F32)],
        compiler_params=params(16),
    )(spectra, valid, full)
    sibling = lax.ppermute(a, "stn", [(i ^ 1, i) for i in ids])

    def to(distance):
        return [(i ^ distance, i) for i in range(members)]

    def halve(keep, send, distance, lead):
        got = lax.ppermute(send, "seg", to(distance))
        shape = (*lead, keep.shape[len(lead)] // 2, *keep.shape[len(lead) + 1 :])
        if lead:
            shape = (shape[0] * shape[1], *shape[2:])
        flat = lambda v: v.reshape((-1, *v.shape[-2:]))
        new = pl.pallas_call(
            add_kernel,
            in_specs=[VMEM] * 2,
            out_specs=[VMEM] * 2,
            out_shape=[jax.ShapeDtypeStruct(shape, F32)] * 2,
            compiler_params=params(8),
        )(flat(keep), flat(got))
        return [v.reshape((*lead, -1, *v.shape[-2:])) for v in new]

    distance = 1
    while 2 * distance < members:
        keep, send = halve(keep, send, distance, ())
        distance *= 2
    final = [keep.reshape(keep.shape[-2:]), lax.ppermute(send, "seg", to(distance)).reshape(keep.shape[-2:])]

    mine, theirs = [], []
    for k in range(CHUNKS):
        keep, send = pl.pallas_call(
            functools.partial(chunk_kernel, members),
            in_specs=[VMEM] * 6,
            out_specs=[VMEM] * 2,
            out_shape=[jax.ShapeDtypeStruct((2, half, per, 4 * width), F32)] * 2,
            scratch_shapes=[pltpu.VMEM((2, 4 * width, freq), BF16), pltpu.VMEM((2, 4 * width // LANES, rows, LANES), F32)],
            compiler_params=params(16),
        )(a, sibling, own[k], four[k], low[k], high[k])
        distance = 1
        while 4 * distance < members:
            keep, send = halve(keep, send, distance, (2,))
            distance *= 2
        got = lax.ppermute(send, "seg", to(distance))
        keep_own, send_own, keep_sib, send_sib = pl.pallas_call(
            add_last_kernel,
            in_specs=[VMEM] * 2,
            out_specs=[VMEM] * 4,
            out_shape=[jax.ShapeDtypeStruct((per, 4 * width), F32)] * 4,
            compiler_params=params(8),
        )(keep, got)
        distance *= 2
        got_own = lax.ppermute(send_own, "seg", to(distance))
        cross = [
            (i * members + j, (i ^ 1) * members + (j ^ distance)) for i in ids for j in range(members)
        ]
        got_sib = lax.ppermute(send_sib, ("stn", "seg"), cross)
        kept_sib = lax.ppermute(keep_sib, "stn", [(i ^ 1, i) for i in ids])
        mine += [keep_own, got_own]
        theirs += [kept_sib, got_sib]

    out = pl.pallas_call(
        functools.partial(final_kernel, factor, CHUNKS),
        in_specs=[SMEM] + [VMEM] * (2 + 4 * CHUNKS),
        out_specs=VMEM,
        out_shape=jax.ShapeDtypeStruct((2 * PAIRS * per, 2 * block), F32),
        compiler_params=params(12),
    )(pair_live, *final, *mine, *theirs)
    return out.reshape(block // members, channels, PAIRS, 2, 2 * block)


def solution(mesh):
    return jax.shard_map(
        per_device,
        mesh=mesh,
        in_specs=(P("stn", None, "seg", None, None), P("stn", "seg"), P("stn", None)),
        out_specs=P(("stn", "seg"), None, None, None, None),
        check_vma=False,
    )
```

time: 167 us -> 77.5 us (0.46)
  waiting for transfers between devices: 57.1 us -> 19 us
  starting transfers between devices: 6.31 us -> 43.5 us
  other arithmetic: 33.4 us -> 0 us
  local copies, waits for them, and re-layouts: 34.3 us -> 3.35 us
  matrix products: 18.8 us -> 0 us
  between operations: 16.4 us -> 0.2 us
  Pallas kernels: 0 us -> 11 us
    reduce_scatter x5 -> x0, waiting for transfers between devices: 49.7 us -> none  [per_device(): lax.psum_scatter(pair_term, 'seg', scatter_dimension=0, tiled=True)]
    ppermute x4 -> x31, starting transfers between devices: 5.92 us -> 43.5 us  [the longest x4 12.7 us: per_device(): lax.ppermute(c, 'stn', [((i - 2) % blocks, i) for i in ids if i // 2 % 2...]
    another operation x12 -> x0, local copies, waits for them, and re-layouts: 20.7 us -> none  [the longest x10 18.8 us: per_device(): jnp.stack([remote, rotated], axis=0)]
    dot_general x5 -> x0, matrix products: 18.8 us -> none  [per_device(): lax.dot_general(local_rows, stacked, (((1,), (1,)), ((), ())), preferred_...]
    another operation x5 -> x0, other arithmetic: 14.6 us -> none  [per_device(): rotated = jnp.stack([-remote[:, :, :, 1], remote[:, :, :, 0]], axis=3)]
    neg x5 -> x0, other arithmetic: 14.2 us -> none  [per_device(): rotated = jnp.stack([-remote[:, :, :, 1], remote[:, :, :, 0]], axis=3)]
    ppermute x4 -> x31, waiting for transfers between devices: 7.27 us -> 19 us  [the longest x4 5.29 us: per_device(): lax.ppermute(c, 'stn', [((i - 4) % blocks, i) for i in ids])]
    pallas_call x0 -> x12, Pallas kernels: none -> 11 us  [the longest x4 7.06 us: per_device(): pl.pallas_call(functools.partial(chunk_kernel, members), in_specs=[VMEM]...]
  transfers between devices with their start and end apart: 9 -> 31, of which waited for: 4 -> 15; matrix products, arithmetic and copies ran while one was open for 47% -> 0% of each run, Pallas kernels for 0% -> 9%
where the time goes in v1:
time: 77.5 us; the launch traced here: 77.1 us
  starting transfers between devices  43.5 us (56%)
  waiting for transfers between devices  19 us (25%)
  Pallas kernels  11 us (14%)
  local copies, waits for them, and re-layouts  3.35 us (4%)
    ppermute x4, starting transfers between devices, per_device(): lax.ppermute(c, 'stn', [((i - 2) % blocks, i) for i in ids if i // 2 % 2...  12.7 us
    pallas_call x4, Pallas kernels, per_device(): pl.pallas_call(functools.partial(chunk_kernel, members), in_specs=[VMEM]...  7.06 us
    ppermute x4, starting transfers between devices, per_device(): got_own = lax.ppermute(send_own, 'seg', to(distance))  5.8 us
    ppermute x4, starting transfers between devices, per_device(): lax.ppermute(c, 'stn', [((i - 4) % blocks, i) for i in ids])  5.69 us
    ppermute x4, waiting for transfers between devices, per_device(): lax.ppermute(c, 'stn', [((i - 4) % blocks, i) for i in ids])  5.29 us
    ppermute x4, starting transfers between devices, per_device(): lax.ppermute(c, 'stn', [((i + 2) % blocks, i) for i in ids if i // 2 % 2...  5.13 us
    ppermute x4, starting transfers between devices, per_device(): got = lax.ppermute(send, 'seg', to(distance))  5.04 us
    ppermute x4, waiting for transfers between devices, per_device(): got_sib = lax.ppermute(send_sib, ('stn', 'seg'), cross)  4.61 us
  transfers between devices with their start and end apart: 31, of which 15 were waited for; matrix products, arithmetic and copies ran while one was open for 0% of the time, Pallas kernels for 9%

profile of v1, /device:TPU:0, one launch (start us, length us, event | category | flops | bytes accessed | tf_op | source)
XLA Modules:
  0.0 77.1 jit_solution(11218537119604617956)
XLA Ops:
  0.0 1.7 %copy-done = bf16[64,5,1,2,2048]{4,3,2,1,0:T(2,128)(2,1)S(1)} copy-done((bf16[64,5,1,2,2048]{4,3,2,1,0:T(2,128)(2,1)S(1)}, bf16[64,5,1,2,2048]{4,3,2,1,0:T(2,128)(2,1)}, u32[]{:S(2)}) %copy-start) | copy-done | bytes 2621464
  1.7 0.7 copy-done.2
  2.4 0.8 %shard_map.37 = (bf16[256,2048]{1,0:T(8,128)(2,1)S(1)}, bf16[64,2048]{1,0:T(8,128)(2,1)S(1)}, bf16[64,2048]{1,0:T(8,128)(2,1)S(1)}, bf16[64,2048]{1,0:T(8,128)(2,1)S(1)}, bf16[64,2048]{1,0:T(8,128)(2,1)S(1)}) custom-call(bf16[64,5,1,2,2048]{4,3,2,1,0:T(2,128)(2,1)S(1)} %copy-done, s32[1,64]{1,0:T(1,128)S(1)} %bitcast.6), custom_call_target="tpu_custom_call" | custom-call | tf_op jit(solution)/shard_map/pallas_call | solution.py:158
  3.2 0.9 %copy-done.1 = bf16[64,5,1,2,2048]{4,3,2,1,0:T(2,128)(2,1)S(1)} copy-done((bf16[64,5,1,2,2048]{4,3,2,1,0:T(2,128)(2,1)S(1)}, bf16[64,5,1,2,2048]{4,3,2,1,0:T(2,128)(2,1)}, u32[]{:S(2)}) %copy-start.1) | copy-done | bytes 2621464
  4.1 1.5 %shard_map.38 = (bf16[640,2048]{1,0:T(8,128)(2,1)S(1)}, f32[2,80,256]{2,1,0:T(8,128)S(1)}, f32[2,80,256]{2,1,0:T(8,128)S(1)}) custom-call(bf16[64,5,1,2,2048]{4,3,2,1,0:T(2,128)(2,1)S(1)} %copy-done.1, s32[1,64]{1,0:T(1,128)S(1)} %bitcast.7, bf16[256,2048]{1,0:T(8,128)(2,1)S(1)} %get-tuple-element.39.full_ref), custom_call_target="tpu_custom_call" | custom-call | tf_op jit(solution)/shard_map/pallas_call | solution.py:174
  5.6 0.5 collective-permute-start.2
  6.1 2.6 %collective-permute-start.3 = (bf16[64,2048]{1,0:T(8,128)(2,1)S(1)}, bf16[64,2048]{1,0:T(8,128)(2,1)S(1)}, u32[]{:S(2)}, u32[]{:S(2)}) collective-permute-start(bf16[64,2048]{1,0:T(8,128)(2,1)S(1)} %get-tuple-element.45.own_ref), channel_id=1, source_target_pairs={{16,0},{20,4},{24,8},{28,12},{0,16},{4,20},{8,24},{12,28},{17,1},{... | collective-permute-start | bytes 786440 | tf_op jit(solution)/shard_map/ppermute | solution.py:169
  8.7 3.4 %collective-permute-start.4 = (bf16[64,2048]{1,0:T(8,128)(2,1)S(1)}, bf16[64,2048]{1,0:T(8,128)(2,1)S(1)}, u32[]{:S(2)}, u32[]{:S(2)}) collective-permute-start(bf16[64,2048]{1,0:T(8,128)(2,1)S(1)} %get-tuple-element.45.own_ref), channel_id=1, source_target_pairs={{0,8},{4,12},{16,24},{20,28},{1,9},{5,13},{17,25},{21,29},{2,10},{... | collective-permute-start | bytes 786440 | tf_op jit(solution)/shard_map/ppermute | solution.py:170
  12.1 0.6 collective-permute-start.8
  12.7 1.3 %collective-permute-start.9 = (bf16[64,2048]{1,0:T(8,128)(2,1)S(1)}, bf16[64,2048]{1,0:T(8,128)(2,1)S(1)}, u32[]{:S(2)}, u32[]{:S(2)}) collective-permute-start(bf16[64,2048]{1,0:T(8,128)(2,1)S(1)} %get-tuple-element.50.own_ref), channel_id=1, source_target_pairs={{0,8},{4,12},{16,24},{20,28},{1,9},{5,13},{17,25},{21,29},{2,10},{... | collective-permute-start | bytes 786440 | tf_op jit(solution)/shard_map/ppermute | solution.py:170
  14.0 1.9 %collective-permute-done.3.four_ref = bf16[64,2048]{1,0:T(8,128)(2,1)S(1)} collective-permute-done((bf16[64,2048]{1,0:T(8,128)(2,1)S(1)}, bf16[64,2048]{1,0:T(8,128)(2,1)S(1)}, u32[]{:S(2)}, u32[]{:S(2)}) %collective-permute-start.3) | collective-permute-done | bytes 262176 | tf_op jit(solution)/shard_map/ppermute | solution.py:169
  15.9 1.9 %collective-permute-start.13 = (bf16[64,2048]{1,0:T(8,128)(2,1)S(1)}, bf16[64,2048]{1,0:T(8,128)(2,1)S(1)}, u32[]{:S(2)}, u32[]{:S(2)}) collective-permute-start(bf16[64,2048]{1,0:T(8,128)(2,1)S(1)} %get-tuple-element.55.own_ref), channel_id=1, source_target_pairs={{16,0},{20,4},{24,8},{28,12},{0,16},{4,20},{8,24},{12,28},{17,1},{... | collective-permute-start | bytes 786440 | tf_op jit(solution)/shard_map/ppermute | solution.py:169
  17.8 0.9 %collective-permute-done.4.low_ref = bf16[64,2048]{1,0:T(8,128)(2,1)S(1)} collective-permute-done((bf16[64,2048]{1,0:T(8,128)(2,1)S(1)}, bf16[64,2048]{1,0:T(8,128)(2,1)S(1)}, u32[]{:S(2)}, u32[]{:S(2)}) %collective-permute-start.4) | collective-permute-done | bytes 262176 | tf_op jit(solution)/shard_map/ppermute | solution.py:170
  18.8 4.4 %collective-permute-start.14 = (bf16[64,2048]{1,0:T(8,128)(2,1)S(1)}, bf16[64,2048]{1,0:T(8,128)(2,1)S(1)}, u32[]{:S(2)}, u32[]{:S(2)}) collective-permute-start(bf16[64,2048]{1,0:T(8,128)(2,1)S(1)} %get-tuple-element.55.own_ref), channel_id=1, source_target_pairs={{0,8},{4,12},{16,24},{20,28},{1,9},{5,13},{17,25},{21,29},{2,10},{... | collective-permute-start | bytes 786440 | tf_op jit(solution)/shard_map/ppermute | solution.py:170
  23.1 0.0 collective-permute-done.8.four_ref
  23.2 0.6 collective-permute-start.18
  23.7 0.6 collective-permute-done.9.low_ref
  24.4 1.3 %collective-permute-start.5 = (bf16[64,2048]{1,0:T(8,128)(2,1)S(1)}, bf16[64,2048]{1,0:T(8,128)(2,1)S(1)}, u32[]{:S(2)}, u32[]{:S(2)}) collective-permute-start(bf16[64,2048]{1,0:T(8,128)(2,1)S(1)} %collective-permute-done.3.four_ref), channel_id=1, source_target_pairs={{8,0},{12,4},{24,16},{28,20},{9,1},{13,5},{25,17},{29,21},{10,2},{... | collective-permute-start | bytes 786440 | tf_op jit(solution)/shard_map/ppermute | solution.py:171
  25.7 1.4 %collective-permute-done.13.four_ref = bf16[64,2048]{1,0:T(8,128)(2,1)S(1)} collective-permute-done((bf16[64,2048]{1,0:T(8,128)(2,1)S(1)}, bf16[64,2048]{1,0:T(8,128)(2,1)S(1)}, u32[]{:S(2)}, u32[]{:S(2)}) %collective-permute-start.13) | collective-permute-done | bytes 262176 | tf_op jit(solution)/shard_map/ppermute | solution.py:169
  27.1 1.3 %collective-permute-start.10 = (bf16[64,2048]{1,0:T(8,128)(2,1)S(1)}, bf16[64,2048]{1,0:T(8,128)(2,1)S(1)}, u32[]{:S(2)}, u32[]{:S(2)}) collective-permute-start(bf16[64,2048]{1,0:T(8,128)(2,1)S(1)} %collective-permute-done.8.four_ref), channel_id=1, source_target_pairs={{8,0},{12,4},{24,16},{28,20},{9,1},{13,5},{25,17},{29,21},{10,2},{... | collective-permute-start | bytes 786440 | tf_op jit(solution)/shard_map/ppermute | solution.py:171
  28.4 0.8 %collective-permute-done.14.low_ref = bf16[64,2048]{1,0:T(8,128)(2,1)S(1)} collective-permute-done((bf16[64,2048]{1,0:T(8,128)(2,1)S(1)}, bf16[64,2048]{1,0:T(8,128)(2,1)S(1)}, u32[]{:S(2)}, u32[]{:S(2)}) %collective-permute-start.14) | collective-permute-done | bytes 262176 | tf_op jit(solution)/shard_map/ppermute | solution.py:170
  29.2 1.3 %collective-permute-start.15 = (bf16[64,2048]{1,0:T(8,128)(2,1)S(1)}, bf16[64,2048]{1,0:T(8,128)(2,1)S(1)}, u32[]{:S(2)}, u32[]{:S(2)}) collective-permute-start(bf16[64,2048]{1,0:T(8,128)(2,1)S(1)} %collective-permute-done.13.four_ref), channel_id=1, source_target_pairs={{8,0},{12,4},{24,16},{28,20},{9,1},{13,5},{25,17},{29,21},{10,2},{... | collective-permute-start | bytes 786440 | tf_op jit(solution)/shard_map/ppermute | solution.py:171
  30.5 2.0 %collective-permute-done.18.four_ref = bf16[64,2048]{1,0:T(8,128)(2,1)S(1)} collective-permute-done((bf16[64,2048]{1,0:T(8,128)(2,1)S(1)}, bf16[64,2048]{1,0:T(8,128)(2,1)S(1)}, u32[]{:S(2)}, u32[]{:S(2)}) %collective-permute-start.18) | collective-permute-done | bytes 262176 | tf_op jit(solution)/shard_map/ppermute | solution.py:169
  32.5 3.6 %collective-permute-start.19 = (bf16[64,2048]{1,0:T(8,128)(2,1)S(1)}, bf16[64,2048]{1,0:T(8,128)(2,1)S(1)}, u32[]{:S(2)}, u32[]{:S(2)}) collective-permute-start(bf16[64,2048]{1,0:T(8,128)(2,1)S(1)} %get-tuple-element.60.own_ref), channel_id=1, source_target_pairs={{0,8},{4,12},{16,24},{20,28},{1,9},{5,13},{17,25},{21,29},{2,10},{... | collective-permute-start | bytes 786440 | tf_op jit(solution)/shard_map/ppermute | solution.py:170
  36.1 1.3 %collective-permute-start.20 = (bf16[64,2048]{1,0:T(8,128)(2,1)S(1)}, bf16[64,2048]{1,0:T(8,128)(2,1)S(1)}, u32[]{:S(2)}, u32[]{:S(2)}) collective-permute-start(bf16[64,2048]{1,0:T(8,128)(2,1)S(1)} %collective-permute-done.18.four_ref), channel_id=1, source_target_pairs={{8,0},{12,4},{24,16},{28,20},{9,1},{13,5},{25,17},{29,21},{10,2},{... | collective-permute-start | bytes 786440 | tf_op jit(solution)/shard_map/ppermute | solution.py:171
  37.4 1.6 %collective-permute-start = (f32[2,80,256]{2,1,0:T(8,128)S(1)}, f32[2,80,256]{2,1,0:T(8,128)S(1)}, u32[]{:S(2)}, u32[]{:S(2)}) collective-permute-start(f32[2,80,256]{2,1,0:T(8,128)S(1)} %get-tuple-element.41), channel_id=1, source_target_pairs={{1,0},{0,1},{3,2},{2,3},{5,4},{4,5},{7,6},{6,7},{9,8},{8,9},{11,10... | collective-permute-start | bytes 491528 | tf_op jit(solution)/shard_map/ppermute | solution.py:189
  39.1 1.8 %shard_map.40 = (f32[2,2,80,128]{3,2,1,0:T(8,128)S(1)}, f32[2,2,80,128]{3,2,1,0:T(8,128)S(1)}) custom-call(bf16[640,2048]{1,0:T(8,128)(2,1)S(1)} %get-tuple-element.44.a_ref, bf16[640,2048]{1,0:T(8,128)(2,1)S(1)} %collective-permute-done.2.sib_ref, bf16[64,2048]{1,0:T(8,128)(2,1)S(1)} %get-tuple-element.45.own_ref, ...), custom_call_target="tpu_custom_call" | custom-call | tf_op jit(solution)/shard_map/pallas_call | solution.py:211
  40.8 0.0 collective-permute-done.10.high_ref
  40.9 1.4 %collective-permute-start.6 = (f32[2,2,80,128]{3,2,1,0:T(8,128)S(1)}, f32[2,2,80,128]{3,2,1,0:T(8,128)S(1)}, u32[]{:S(2)}, u32[]{:S(2)}) collective-permute-start(f32[2,2,80,128]{3,2,1,0:T(8,128)S(1)} %get-tuple-element.47), channel_id=1, source_target_pairs={{1,0},{0,1},{3,2},{2,3},{5,4},{4,5},{7,6},{6,7},{9,8},{8,9},{11,10... | collective-permute-start | bytes 491528 | tf_op jit(solution)/shard_map/ppermute | solution.py:223
  42.2 1.8 %shard_map.42 = (f32[2,2,80,128]{3,2,1,0:T(8,128)S(1)}, f32[2,2,80,128]{3,2,1,0:T(8,128)S(1)}) custom-call(bf16[640,2048]{1,0:T(8,128)(2,1)S(1)} %get-tuple-element.44.a_ref, bf16[640,2048]{1,0:T(8,128)(2,1)S(1)} %collective-permute-done.2.sib_ref, bf16[64,2048]{1,0:T(8,128)(2,1)S(1)} %get-tuple-element.50.own_ref, ...), custom_call_target="tpu_custom_call" | custom-call | tf_op jit(solution)/shard_map/pallas_call | solution.py:211
  44.0 2.3 %collective-permute-done.15.high_ref = bf16[64,2048]{1,0:T(8,128)(2,1)S(1)} collective-permute-done((bf16[64,2048]{1,0:T(8,128)(2,1)S(1)}, bf16[64,2048]{1,0:T(8,128)(2,1)S(1)}, u32[]{:S(2)}, u32[]{:S(2)}) %collective-permute-start.15) | collective-permute-done | bytes 262176 | tf_op jit(solution)/shard_map/ppermute | solution.py:171
  46.3 1.5 %collective-permute-start.11 = (f32[2,2,80,128]{3,2,1,0:T(8,128)S(1)}, f32[2,2,80,128]{3,2,1,0:T(8,128)S(1)}, u32[]{:S(2)}, u32[]{:S(2)}) collective-permute-start(f32[2,2,80,128]{3,2,1,0:T(8,128)S(1)} %get-tuple-element.52), channel_id=1, source_target_pairs={{1,0},{0,1},{3,2},{2,3},{5,4},{4,5},{7,6},{6,7},{9,8},{8,9},{11,10... | collective-permute-start | bytes 491528 | tf_op jit(solution)/shard_map/ppermute | solution.py:223
  47.8 1.8 %shard_map.44 = (f32[2,2,80,128]{3,2,1,0:T(8,128)S(1)}, f32[2,2,80,128]{3,2,1,0:T(8,128)S(1)}) custom-call(bf16[640,2048]{1,0:T(8,128)(2,1)S(1)} %get-tuple-element.44.a_ref, bf16[640,2048]{1,0:T(8,128)(2,1)S(1)} %collective-permute-done.2.sib_ref, bf16[64,2048]{1,0:T(8,128)(2,1)S(1)} %get-tuple-element.55.own_ref, ...), custom_call_target="tpu_custom_call" | custom-call | tf_op jit(solution)/shard_map/pallas_call | solution.py:211
  49.6 0.0 collective-permute-done.19.low_ref
  49.6 0.0 copy-start.3
  49.6 0.6 collective-permute-start.16
  50.2 1.8 %shard_map.46 = (f32[2,2,80,128]{3,2,1,0:T(8,128)S(1)}, f32[2,2,80,128]{3,2,1,0:T(8,128)S(1)}) custom-call(bf16[640,2048]{1,0:T(8,128)(2,1)S(1)} %get-tuple-element.44.a_ref, bf16[640,2048]{1,0:T(8,128)(2,1)S(1)} %collective-permute-done.2.sib_ref, bf16[64,2048]{1,0:T(8,128)(2,1)S(1)} %get-tuple-element.60.own_ref, ...), custom_call_target="tpu_custom_call" | custom-call | tf_op jit(solution)/shard_map/pallas_call | solution.py:211
  52.0 1.6 %collective-permute-start.21 = (f32[2,2,80,128]{3,2,1,0:T(8,128)S(1)}, f32[2,2,80,128]{3,2,1,0:T(8,128)S(1)}, u32[]{:S(2)}, u32[]{:S(2)}) collective-permute-start(f32[2,2,80,128]{3,2,1,0:T(8,128)S(1)} %get-tuple-element.62), channel_id=1, source_target_pairs={{1,0},{0,1},{3,2},{2,3},{5,4},{4,5},{7,6},{6,7},{9,8},{8,9},{11,10... | collective-permute-start | bytes 491528 | tf_op jit(solution)/shard_map/ppermute | solution.py:223
  53.6 2.7 %collective-permute-start.1 = (f32[1,80,256]{2,1,0:T(8,128)S(1)}, f32[1,80,256]{2,1,0:T(8,128)S(1)}, u32[]{:S(2)}, u32[]{:S(2)}) collective-permute-start(f32[1,80,256]{2,1,0:T(8,128)S(1)} %get-tuple-element.43), channel_id=1, source_target_pairs={{2,0},{3,1},{0,2},{1,3},{6,4},{7,5},{4,6},{5,7},{10,8},{11,9},{8,1... | collective-permute-start | bytes 245768 | tf_op jit(solution)/shard_map/ppermute | solution.py:207
  56.3 0.0 collective-permute-done.6.got_ref
  56.3 0.4 collective-permute-start.7
  56.7 0.0 collective-permute-done.11.got_ref
  56.7 2.7 %collective-permute-start.12 = (f32[80,128]{1,0:T(8,128)S(1)}, f32[80,128]{1,0:T(8,128)S(1)}, u32[]{:S(2)}, u32[]{:S(2)}) collective-permute-start(f32[80,128]{1,0:T(8,128)S(1)} %get-tuple-element.54), channel_id=1, source_target_pairs={{2,0},{3,1},{0,2},{1,3},{6,4},{7,5},{4,6},{5,7},{10,8},{11,9},{8,1... | collective-permute-start | bytes 122888 | tf_op jit(solution)/shard_map/ppermute | solution.py:232
  59.4 0.4 collective-permute-start.17
  59.8 0.6 collective-permute-done.21.got_ref
  60.5 2.4 %collective-permute-start.22 = (f32[80,128]{1,0:T(8,128)S(1)}, f32[80,128]{1,0:T(8,128)S(1)}, u32[]{:S(2)}, u32[]{:S(2)}) collective-permute-start(f32[80,128]{1,0:T(8,128)S(1)} %get-tuple-element.64), channel_id=1, source_target_pairs={{2,0},{3,1},{0,2},{1,3},{6,4},{7,5},{4,6},{5,7},{10,8},{11,9},{8,1... | collective-permute-start | bytes 122888 | tf_op jit(solution)/shard_map/ppermute | solution.py:232
  62.8 0.0 collective-permute-done.1
  62.8 0.0 collective-permute-start.23
  62.8 2.3 %collective-permute-done.7.refs_3_ = f32[80,128]{1,0:T(8,128)S(1)} collective-permute-done((f32[80,128]{1,0:T(8,128)S(1)}, f32[80,128]{1,0:T(8,128)S(1)}, u32[]{:S(2)}, u32[]{:S(2)}) %collective-permute-start.7) | collective-permute-done | bytes 40992 | tf_op jit(solution)/shard_map/ppermute | solution.py:232
  65.1 0.0 collective-permute-start.24
  65.1 1.0 %collective-permute-done.12.refs_5_ = f32[80,128]{1,0:T(8,128)S(1)} collective-permute-done((f32[80,128]{1,0:T(8,128)S(1)}, f32[80,128]{1,0:T(8,128)S(1)}, u32[]{:S(2)}, u32[]{:S(2)}) %collective-permute-start.12) | collective-permute-done | bytes 40992 | tf_op jit(solution)/shard_map/ppermute | solution.py:232
  66.2 0.4 collective-permute-done.17.refs_7_
  66.6 1.2 %collective-permute-start.26 = (f32[80,128]{1,0:T(8,128)S(1)}, f32[80,128]{1,0:T(8,128)S(1)}, u32[]{:S(2)}, u32[]{:S(2)}) collective-permute-start(f32[80,128]{1,0:T(8,128)S(1)} %get-tuple-element.68), channel_id=1, source_target_pairs={{0,6},{1,7},{2,4},{3,5},{4,2},{5,3},{6,0},{7,1},{8,14},{9,15},{10,... | collective-permute-start | bytes 122888 | tf_op jit(solution)/shard_map/ppermute | solution.py:236
  67.8 0.0 collective-permute-done.22.refs_9_
  67.8 0.4 collective-permute-start.27
  68.3 0.0 collective-permute-done.23.refs_10_
  68.3 1.0 %collective-permute-start.28 = (f32[80,128]{1,0:T(8,128)S(1)}, f32[80,128]{1,0:T(8,128)S(1)}, u32[]{:S(2)}, u32[]{:S(2)}) collective-permute-start(f32[80,128]{1,0:T(8,128)S(1)} %get-tuple-element.70), channel_id=1, source_target_pairs={{0,6},{1,7},{2,4},{3,5},{4,2},{5,3},{6,0},{7,1},{8,14},{9,15},{10,... | collective-permute-start | bytes 122888 | tf_op jit(solution)/shard_map/ppermute | solution.py:236
  69.3 0.1 collective-permute-done.24.refs_11_
  69.4 0.3 collective-permute-start.29
  69.8 1.2 %collective-permute-start.30 = (f32[80,128]{1,0:T(8,128)S(1)}, f32[80,128]{1,0:T(8,128)S(1)}, u32[]{:S(2)}, u32[]{:S(2)}) collective-permute-start(f32[80,128]{1,0:T(8,128)S(1)} %get-tuple-element.72), channel_id=1, source_target_pairs={{0,6},{1,7},{2,4},{3,5},{4,2},{5,3},{6,0},{7,1},{8,14},{9,15},{10,... | collective-permute-start | bytes 122888 | tf_op jit(solution)/shard_map/ppermute | solution.py:236
  71.0 0.1 collective-permute-done.26.refs_13_
  71.1 2.6 %collective-permute-done.28.refs_15_ = f32[80,128]{1,0:T(8,128)S(1)} collective-permute-done((f32[80,128]{1,0:T(8,128)S(1)}, f32[80,128]{1,0:T(8,128)S(1)}, u32[]{:S(2)}, u32[]{:S(2)}) %collective-permute-start.28) | collective-permute-done | bytes 40992 | tf_op jit(solution)/shard_map/ppermute | solution.py:236
  73.8 1.8 %collective-permute-done.30.refs_17_ = f32[80,128]{1,0:T(8,128)S(1)} collective-permute-done((f32[80,128]{1,0:T(8,128)S(1)}, f32[80,128]{1,0:T(8,128)S(1)}, u32[]{:S(2)}, u32[]{:S(2)}) %collective-permute-start.30) | collective-permute-done | bytes 40992 | tf_op jit(solution)/shard_map/ppermute | solution.py:236
  75.5 1.6 %shard_map.48 = f32[800,128]{1,0:T(8,128)} custom-call(s32[1,5]{1,0:T(1,128)S(1)} %copy-done.3, f32[80,256]{1,0:T(8,128)S(1)} %bitcast.4, f32[80,256]{1,0:T(8,128)S(1)} %bitcast.5, f32[80,128]{1,0:T(8,128)S(1)} %get-tuple-element.48.refs_2_, f32[80,128]{1,0:T(8,128)S(1)} %collective-permute-done.7.refs_3_, f32[80,128]{1,0:T(8,128)S(1)} %get-tuple-element.53.refs_4_, ...), custom_call_target="tpu_custom_call" | custom-call | tf_op jit(solution)/shard_map/pallas_call | solution.py:241
  (18 shorter events, 0.1 us)
Async XLA Ops:
  0.0 1.7 %copy-start = (bf16[64,5,1,2,2048]{4,3,2,1,0:T(2,128)(2,1)S(1)}, bf16[64,5,1,2,2048]{4,3,2,1,0:T(2,128)(2,1)}, u32[]{:S(2)}) copy-start(bf16[64,5,1,2,2048]{4,3,2,1,0:T(2,128)(2,1)} %x_ref.1) | copy-start | bytes 7864324
  1.7 0.7 copy-start.2
  2.4 1.7 %copy-start.1 = (bf16[64,5,1,2,2048]{4,3,2,1,0:T(2,128)(2,1)S(1)}, bf16[64,5,1,2,2048]{4,3,2,1,0:T(2,128)(2,1)}, u32[]{:S(2)}) copy-start(bf16[64,5,1,2,2048]{4,3,2,1,0:T(2,128)(2,1)} %x_ref.1) | copy-start | bytes 7864324
  5.6 31.8 %collective-permute-start.2 = (bf16[640,2048]{1,0:T(8,128)(2,1)S(1)}, bf16[640,2048]{1,0:T(8,128)(2,1)S(1)}, u32[]{:S(2)}, u32[]{:S(2)}) collective-permute-start(bf16[640,2048]{1,0:T(8,128)(2,1)S(1)} %get-tuple-element.44.a_ref), channel_id=1, source_target_pairs={{4,0},{0,4},{12,8},{8,12},{20,16},{16,20},{28,24},{24,28},{5,1},{1... | collective-permute-start | bytes 7864328 | tf_op jit(solution)/shard_map/ppermute | solution.py:183
  6.1 9.8 %collective-permute-start.3 = (bf16[64,2048]{1,0:T(8,128)(2,1)S(1)}, bf16[64,2048]{1,0:T(8,128)(2,1)S(1)}, u32[]{:S(2)}, u32[]{:S(2)}) collective-permute-start(bf16[64,2048]{1,0:T(8,128)(2,1)S(1)} %get-tuple-element.45.own_ref), channel_id=1, source_target_pairs={{16,0},{20,4},{24,8},{28,12},{0,16},{4,20},{8,24},{12,28},{17,1},{... | collective-permute-start | bytes 786440 | tf_op jit(solution)/shard_map/ppermute | solution.py:169
  8.7 10.0 %collective-permute-start.4 = (bf16[64,2048]{1,0:T(8,128)(2,1)S(1)}, bf16[64,2048]{1,0:T(8,128)(2,1)S(1)}, u32[]{:S(2)}, u32[]{:S(2)}) collective-permute-start(bf16[64,2048]{1,0:T(8,128)(2,1)S(1)} %get-tuple-element.45.own_ref), channel_id=1, source_target_pairs={{0,8},{4,12},{16,24},{20,28},{1,9},{5,13},{17,25},{21,29},{2,10},{... | collective-permute-start | bytes 786440 | tf_op jit(solution)/shard_map/ppermute | solution.py:170
  12.1 11.0 %collective-permute-start.8 = (bf16[64,2048]{1,0:T(8,128)(2,1)S(1)}, bf16[64,2048]{1,0:T(8,128)(2,1)S(1)}, u32[]{:S(2)}, u32[]{:S(2)}) collective-permute-start(bf16[64,2048]{1,0:T(8,128)(2,1)S(1)} %get-tuple-element.50.own_ref), channel_id=1, source_target_pairs={{16,0},{20,4},{24,8},{28,12},{0,16},{4,20},{8,24},{12,28},{17,1},{... | collective-permute-start | bytes 786440 | tf_op jit(solution)/shard_map/ppermute | solution.py:169
  12.7 11.7 %collective-permute-start.9 = (bf16[64,2048]{1,0:T(8,128)(2,1)S(1)}, bf16[64,2048]{1,0:T(8,128)(2,1)S(1)}, u32[]{:S(2)}, u32[]{:S(2)}) collective-permute-start(bf16[64,2048]{1,0:T(8,128)(2,1)S(1)} %get-tuple-element.50.own_ref), channel_id=1, source_target_pairs={{0,8},{4,12},{16,24},{20,28},{1,9},{5,13},{17,25},{21,29},{2,10},{... | collective-permute-start | bytes 786440 | tf_op jit(solution)/shard_map/ppermute | solution.py:170
  15.9 11.2 %collective-permute-start.13 = (bf16[64,2048]{1,0:T(8,128)(2,1)S(1)}, bf16[64,2048]{1,0:T(8,128)(2,1)S(1)}, u32[]{:S(2)}, u32[]{:S(2)}) collective-permute-start(bf16[64,2048]{1,0:T(8,128)(2,1)S(1)} %get-tuple-element.55.own_ref), channel_id=1, source_target_pairs={{16,0},{20,4},{24,8},{28,12},{0,16},{4,20},{8,24},{12,28},{17,1},{... | collective-permute-start | bytes 786440 | tf_op jit(solution)/shard_map/ppermute | solution.py:169
  18.8 10.5 %collective-permute-start.14 = (bf16[64,2048]{1,0:T(8,128)(2,1)S(1)}, bf16[64,2048]{1,0:T(8,128)(2,1)S(1)}, u32[]{:S(2)}, u32[]{:S(2)}) collective-permute-start(bf16[64,2048]{1,0:T(8,128)(2,1)S(1)} %get-tuple-element.55.own_ref), channel_id=1, source_target_pairs={{0,8},{4,12},{16,24},{20,28},{1,9},{5,13},{17,25},{21,29},{2,10},{... | collective-permute-start | bytes 786440 | tf_op jit(solution)/shard_map/ppermute | solution.py:170
  23.2 9.3 %collective-permute-start.18 = (bf16[64,2048]{1,0:T(8,128)(2,1)S(1)}, bf16[64,2048]{1,0:T(8,128)(2,1)S(1)}, u32[]{:S(2)}, u32[]{:S(2)}) collective-permute-start(bf16[64,2048]{1,0:T(8,128)(2,1)S(1)} %get-tuple-element.60.own_ref), channel_id=1, source_target_pairs={{16,0},{20,4},{24,8},{28,12},{0,16},{4,20},{8,24},{12,28},{17,1},{... | collective-permute-start | bytes 786440 | tf_op jit(solution)/shard_map/ppermute | solution.py:169
  24.4 11.7 %collective-permute-start.5 = (bf16[64,2048]{1,0:T(8,128)(2,1)S(1)}, bf16[64,2048]{1,0:T(8,128)(2,1)S(1)}, u32[]{:S(2)}, u32[]{:S(2)}) collective-permute-start(bf16[64,2048]{1,0:T(8,128)(2,1)S(1)} %collective-permute-done.3.four_ref), channel_id=1, source_target_pairs={{8,0},{12,4},{24,16},{28,20},{9,1},{13,5},{25,17},{29,21},{10,2},{... | collective-permute-start | bytes 786440 | tf_op jit(solution)/shard_map/ppermute | solution.py:171
  27.1 13.7 %collective-permute-start.10 = (bf16[64,2048]{1,0:T(8,128)(2,1)S(1)}, bf16[64,2048]{1,0:T(8,128)(2,1)S(1)}, u32[]{:S(2)}, u32[]{:S(2)}) collective-permute-start(bf16[64,2048]{1,0:T(8,128)(2,1)S(1)} %collective-permute-done.8.four_ref), channel_id=1, source_target_pairs={{8,0},{12,4},{24,16},{28,20},{9,1},{13,5},{25,17},{29,21},{10,2},{... | collective-permute-start | bytes 786440 | tf_op jit(solution)/shard_map/ppermute | solution.py:171
  29.2 17.1 %collective-permute-start.15 = (bf16[64,2048]{1,0:T(8,128)(2,1)S(1)}, bf16[64,2048]{1,0:T(8,128)(2,1)S(1)}, u32[]{:S(2)}, u32[]{:S(2)}) collective-permute-start(bf16[64,2048]{1,0:T(8,128)(2,1)S(1)} %collective-permute-done.13.four_ref), channel_id=1, source_target_pairs={{8,0},{12,4},{24,16},{28,20},{9,1},{13,5},{25,17},{29,21},{10,2},{... | collective-permute-start | bytes 786440 | tf_op jit(solution)/shard_map/ppermute | solution.py:171
  32.5 17.1 %collective-permute-start.19 = (bf16[64,2048]{1,0:T(8,128)(2,1)S(1)}, bf16[64,2048]{1,0:T(8,128)(2,1)S(1)}, u32[]{:S(2)}, u32[]{:S(2)}) collective-permute-start(bf16[64,2048]{1,0:T(8,128)(2,1)S(1)} %get-tuple-element.60.own_ref), channel_id=1, source_target_pairs={{0,8},{4,12},{16,24},{20,28},{1,9},{5,13},{17,25},{21,29},{2,10},{... | collective-permute-start | bytes 786440 | tf_op jit(solution)/shard_map/ppermute | solution.py:170
  36.1 14.1 %collective-permute-start.20 = (bf16[64,2048]{1,0:T(8,128)(2,1)S(1)}, bf16[64,2048]{1,0:T(8,128)(2,1)S(1)}, u32[]{:S(2)}, u32[]{:S(2)}) collective-permute-start(bf16[64,2048]{1,0:T(8,128)(2,1)S(1)} %collective-permute-done.18.four_ref), channel_id=1, source_target_pairs={{8,0},{12,4},{24,16},{28,20},{9,1},{13,5},{25,17},{29,21},{10,2},{... | collective-permute-start | bytes 786440 | tf_op jit(solution)/shard_map/ppermute | solution.py:171
  37.4 16.1 %collective-permute-start = (f32[2,80,256]{2,1,0:T(8,128)S(1)}, f32[2,80,256]{2,1,0:T(8,128)S(1)}, u32[]{:S(2)}, u32[]{:S(2)}) collective-permute-start(f32[2,80,256]{2,1,0:T(8,128)S(1)} %get-tuple-element.41), channel_id=1, source_target_pairs={{1,0},{0,1},{3,2},{2,3},{5,4},{4,5},{7,6},{6,7},{9,8},{8,9},{11,10... | collective-permute-start | bytes 491528 | tf_op jit(solution)/shard_map/ppermute | solution.py:189
  40.9 15.4 %collective-permute-start.6 = (f32[2,2,80,128]{3,2,1,0:T(8,128)S(1)}, f32[2,2,80,128]{3,2,1,0:T(8,128)S(1)}, u32[]{:S(2)}, u32[]{:S(2)}) collective-permute-start(f32[2,2,80,128]{3,2,1,0:T(8,128)S(1)} %get-tuple-element.47), channel_id=1, source_target_pairs={{1,0},{0,1},{3,2},{2,3},{5,4},{4,5},{7,6},{6,7},{9,8},{8,9},{11,10... | collective-permute-start | bytes 491528 | tf_op jit(solution)/shard_map/ppermute | solution.py:223
  46.3 10.4 %collective-permute-start.11 = (f32[2,2,80,128]{3,2,1,0:T(8,128)S(1)}, f32[2,2,80,128]{3,2,1,0:T(8,128)S(1)}, u32[]{:S(2)}, u32[]{:S(2)}) collective-permute-start(f32[2,2,80,128]{3,2,1,0:T(8,128)S(1)} %get-tuple-element.52), channel_id=1, source_target_pairs={{1,0},{0,1},{3,2},{2,3},{5,4},{4,5},{7,6},{6,7},{9,8},{8,9},{11,10... | collective-permute-start | bytes 491528 | tf_op jit(solution)/shard_map/ppermute | solution.py:223
  49.6 25.9 %copy-start.3 = (s32[1,5]{1,0:T(1,128)S(1)}, s32[1,5]{1,0:T(1,128)}, u32[]{:S(2)}) copy-start(s32[1,5]{1,0:T(1,128)} %live_ref.1) | copy-start | bytes 64
  49.6 9.8 %collective-permute-start.16 = (f32[2,2,80,128]{3,2,1,0:T(8,128)S(1)}, f32[2,2,80,128]{3,2,1,0:T(8,128)S(1)}, u32[]{:S(2)}, u32[]{:S(2)}) collective-permute-start(f32[2,2,80,128]{3,2,1,0:T(8,128)S(1)} %get-tuple-element.57), channel_id=1, source_target_pairs={{1,0},{0,1},{3,2},{2,3},{5,4},{4,5},{7,6},{6,7},{9,8},{8,9},{11,10... | collective-permute-start | bytes 491528 | tf_op jit(solution)/shard_map/ppermute | solution.py:223
  52.0 8.5 %collective-permute-start.21 = (f32[2,2,80,128]{3,2,1,0:T(8,128)S(1)}, f32[2,2,80,128]{3,2,1,0:T(8,128)S(1)}, u32[]{:S(2)}, u32[]{:S(2)}) collective-permute-start(f32[2,2,80,128]{3,2,1,0:T(8,128)S(1)} %get-tuple-element.62), channel_id=1, source_target_pairs={{1,0},{0,1},{3,2},{2,3},{5,4},{4,5},{7,6},{6,7},{9,8},{8,9},{11,10... | collective-permute-start | bytes 491528 | tf_op jit(solution)/shard_map/ppermute | solution.py:223
  53.6 9.2 %collective-permute-start.1 = (f32[1,80,256]{2,1,0:T(8,128)S(1)}, f32[1,80,256]{2,1,0:T(8,128)S(1)}, u32[]{:S(2)}, u32[]{:S(2)}) collective-permute-start(f32[1,80,256]{2,1,0:T(8,128)S(1)} %get-tuple-element.43), channel_id=1, source_target_pairs={{2,0},{3,1},{0,2},{1,3},{6,4},{7,5},{4,6},{5,7},{10,8},{11,9},{8,1... | collective-permute-start | bytes 245768 | tf_op jit(solution)/shard_map/ppermute | solution.py:207
  56.3 8.8 %collective-permute-start.7 = (f32[80,128]{1,0:T(8,128)S(1)}, f32[80,128]{1,0:T(8,128)S(1)}, u32[]{:S(2)}, u32[]{:S(2)}) collective-permute-start(f32[80,128]{1,0:T(8,128)S(1)} %get-tuple-element.49), channel_id=1, source_target_pairs={{2,0},{3,1},{0,2},{1,3},{6,4},{7,5},{4,6},{5,7},{10,8},{11,9},{8,1... | collective-permute-start | bytes 122888 | tf_op jit(solution)/shard_map/ppermute | solution.py:232
  56.7 9.4 %collective-permute-start.12 = (f32[80,128]{1,0:T(8,128)S(1)}, f32[80,128]{1,0:T(8,128)S(1)}, u32[]{:S(2)}, u32[]{:S(2)}) collective-permute-start(f32[80,128]{1,0:T(8,128)S(1)} %get-tuple-element.54), channel_id=1, source_target_pairs={{2,0},{3,1},{0,2},{1,3},{6,4},{7,5},{4,6},{5,7},{10,8},{11,9},{8,1... | collective-permute-start | bytes 122888 | tf_op jit(solution)/shard_map/ppermute | solution.py:232
  59.4 7.2 %collective-permute-start.17 = (f32[80,128]{1,0:T(8,128)S(1)}, f32[80,128]{1,0:T(8,128)S(1)}, u32[]{:S(2)}, u32[]{:S(2)}) collective-permute-start(f32[80,128]{1,0:T(8,128)S(1)} %get-tuple-element.59), channel_id=1, source_target_pairs={{2,0},{3,1},{0,2},{1,3},{6,4},{7,5},{4,6},{5,7},{10,8},{11,9},{8,1... | collective-permute-start | bytes 122888 | tf_op jit(solution)/shard_map/ppermute | solution.py:232
  60.5 7.4 %collective-permute-start.22 = (f32[80,128]{1,0:T(8,128)S(1)}, f32[80,128]{1,0:T(8,128)S(1)}, u32[]{:S(2)}, u32[]{:S(2)}) collective-permute-start(f32[80,128]{1,0:T(8,128)S(1)} %get-tuple-element.64), channel_id=1, source_target_pairs={{2,0},{3,1},{0,2},{1,3},{6,4},{7,5},{4,6},{5,7},{10,8},{11,9},{8,1... | collective-permute-start | bytes 122888 | tf_op jit(solution)/shard_map/ppermute | solution.py:232
  62.8 5.5 %collective-permute-start.23 = (f32[80,128]{1,0:T(8,128)S(1)}, f32[80,128]{1,0:T(8,128)S(1)}, u32[]{:S(2)}, u32[]{:S(2)}) collective-permute-start(f32[80,128]{1,0:T(8,128)S(1)} %get-tuple-element.65), channel_id=1, source_target_pairs={{4,0},{0,4},{12,8},{8,12},{20,16},{16,20},{28,24},{24,28},{5,1},{1... | collective-permute-start | bytes 122888 | tf_op jit(solution)/shard_map/ppermute | solution.py:237
  65.1 4.3 %collective-permute-start.24 = (f32[80,128]{1,0:T(8,128)S(1)}, f32[80,128]{1,0:T(8,128)S(1)}, u32[]{:S(2)}, u32[]{:S(2)}) collective-permute-start(f32[80,128]{1,0:T(8,128)S(1)} %get-tuple-element.66), channel_id=1, source_target_pairs={{0,6},{1,7},{2,4},{3,5},{4,2},{5,3},{6,0},{7,1},{8,14},{9,15},{10,... | collective-permute-start | bytes 122888 | tf_op jit(solution)/shard_map/ppermute | solution.py:236
  66.2 3.6 %collective-permute-start.25 = (f32[80,128]{1,0:T(8,128)S(1)}, f32[80,128]{1,0:T(8,128)S(1)}, u32[]{:S(2)}, u32[]{:S(2)}) collective-permute-start(f32[80,128]{1,0:T(8,128)S(1)} %get-tuple-element.67), channel_id=1, source_target_pairs={{4,0},{0,4},{12,8},{8,12},{20,16},{16,20},{28,24},{24,28},{5,1},{1... | collective-permute-start | bytes 122888 | tf_op jit(solution)/shard_map/ppermute | solution.py:237
  66.6 4.5 %collective-permute-start.26 = (f32[80,128]{1,0:T(8,128)S(1)}, f32[80,128]{1,0:T(8,128)S(1)}, u32[]{:S(2)}, u32[]{:S(2)}) collective-permute-start(f32[80,128]{1,0:T(8,128)S(1)} %get-tuple-element.68), channel_id=1, source_target_pairs={{0,6},{1,7},{2,4},{3,5},{4,2},{5,3},{6,0},{7,1},{8,14},{9,15},{10,... | collective-permute-start | bytes 122888 | tf_op jit(solution)/shard_map/ppermute | solution.py:236
  67.8 3.3 %collective-permute-start.27 = (f32[80,128]{1,0:T(8,128)S(1)}, f32[80,128]{1,0:T(8,128)S(1)}, u32[]{:S(2)}, u32[]{:S(2)}) collective-permute-start(f32[80,128]{1,0:T(8,128)S(1)} %get-tuple-element.69), channel_id=1, source_target_pairs={{4,0},{0,4},{12,8},{8,12},{20,16},{16,20},{28,24},{24,28},{5,1},{1... | collective-permute-start | bytes 122888 | tf_op jit(solution)/shard_map/ppermute | solution.py:237
  68.3 5.5 %collective-permute-start.28 = (f32[80,128]{1,0:T(8,128)S(1)}, f32[80,128]{1,0:T(8,128)S(1)}, u32[]{:S(2)}, u32[]{:S(2)}) collective-permute-start(f32[80,128]{1,0:T(8,128)S(1)} %get-tuple-element.70), channel_id=1, source_target_pairs={{0,6},{1,7},{2,4},{3,5},{4,2},{5,3},{6,0},{7,1},{8,14},{9,15},{10,... | collective-permute-start | bytes 122888 | tf_op jit(solution)/shard_map/ppermute | solution.py:236
  69.4 4.3 %collective-permute-start.29 = (f32[80,128]{1,0:T(8,128)S(1)}, f32[80,128]{1,0:T(8,128)S(1)}, u32[]{:S(2)}, u32[]{:S(2)}) collective-permute-start(f32[80,128]{1,0:T(8,128)S(1)} %get-tuple-element.71), channel_id=1, source_target_pairs={{4,0},{0,4},{12,8},{8,12},{20,16},{16,20},{28,24},{24,28},{5,1},{1... | collective-permute-start | bytes 122888 | tf_op jit(solution)/shard_map/ppermute | solution.py:237
  69.8 5.7 %collective-permute-start.30 = (f32[80,128]{1,0:T(8,128)S(1)}, f32[80,128]{1,0:T(8,128)S(1)}, u32[]{:S(2)}, u32[]{:S(2)}) collective-permute-start(f32[80,128]{1,0:T(8,128)S(1)} %get-tuple-element.72), channel_id=1, source_target_pairs={{0,6},{1,7},{2,4},{3,5},{4,2},{5,3},{6,0},{7,1},{8,14},{9,15},{10,... | collective-permute-start | bytes 122888 | tf_op jit(solution)/shard_map/ppermute | solution.py:236

commit v2 on v0

v2 whole, which is shorter than its diff:
```python
import functools
import math

import jax
import jax.numpy as jnp
from jax import lax
from jax.experimental import pallas as pl
from jax.experimental.pallas import tpu as pltpu
from jax.sharding import PartitionSpec as P

PAIRS = 5
CHUNKS = 4
UNITS = 2
STEPS = True
COST = None
LANES = 128
VMEM = pl.BlockSpec(memory_space=pltpu.VMEM)
HBM = pl.BlockSpec(memory_space=pltpu.HBM)
SMEM = pl.BlockSpec(memory_space=pltpu.SMEM)
F32 = jnp.float32
BF16 = jnp.bfloat16


def params(mib):
    return pltpu.CompilerParams(vmem_limit_bytes=mib * 2**20)


def iota(shape, dim):
    return lax.broadcasted_iota(jnp.int32, shape, dim)


def dot_t(a, b):
    return lax.dot_general(a, b, (((1,), (1,)), ((), ())), preferred_element_type=F32)


def extract_kernel(x_hbm, valid_hbm, full_ref, row_ref, *rest):
    *chunk_refs, buf, valid_buf, sems = rest
    copy = pltpu.make_async_copy(x_hbm.at[:, 2:4], buf, sems.at[0])
    copy.start()
    small = pltpu.make_async_copy(valid_hbm, valid_buf, sems.at[1])
    small.start()
    block = buf.shape[0]
    rows = 4 * block
    half = rows // 2
    spread = (iota((block, rows), 1) // 4 == iota((block, rows), 0)).astype(BF16)
    to, frm = iota((rows, rows), 0), iota((rows, rows), 1)
    source = jnp.where(to < half, 2 * to, 2 * (to - half) + 1)
    small.wait()
    valid = jnp.broadcast_to(valid_buf[...], row_ref.shape).astype(F32).astype(BF16)
    row_ref[...] = valid
    valid = jnp.dot(valid, spread, preferred_element_type=F32)[:1]
    pick = jnp.where(frm == source, jnp.broadcast_to(valid, (rows, rows)), 0.0).astype(BF16)
    copy.wait()
    full = jnp.dot(pick, buf[...].reshape(rows, buf.shape[-1]), preferred_element_type=F32).astype(BF16)
    full_ref[...] = full
    width = half // CHUNKS
    for k, chunk_ref in enumerate(chunk_refs):
        for part in range(2):
            at = part * half + k * width
            chunk_ref[part * width : (part + 1) * width] = full[at : at + width]


def store_tiles(g_ref, value):
    for tile in range(g_ref.shape[0]):
        g_ref[tile] = value[:, tile * LANES : (tile + 1) * LANES]


def combine(g_ref, out_keep, out_send, seg, members):
    tiles, rows = g_ref.shape[0], g_ref.shape[1] // members
    sign = jnp.where(iota((1, LANES), 1) < LANES // 2, 1.0, -1.0)
    for slot in range(members):
        at = pl.multiple_of((seg ^ slot) * rows, 8)
        out = out_send if slot % 2 else out_keep
        even = [g_ref[t, pl.ds(at, rows // 2, stride=2), :] for t in range(tiles)]
        odd = [g_ref[t, pl.ds(at + 1, rows // 2, stride=2), :] for t in range(tiles)]
        if tiles == 1:
            out[slot // 2] = pltpu.roll(odd[0], LANES // 2, 1) + sign * even[0]
        for t in range(tiles // 2):
            u = t + tiles // 2
            out[slot // 2, :, t * LANES : (t + 1) * LANES] = even[t] + odd[u]
            out[slot // 2, :, u * LANES : (u + 1) * LANES] = odd[t] - even[u]


def own_kernel(members, x_ref, valid_ref, full_ref, a_ref, keep_ref, send_ref, g_ref):
    block = x_ref.shape[0]
    rows = a_ref.shape[0]
    pick = (iota((rows, block), 0) // (rows // block) == iota((rows, block), 1)).astype(BF16)
    valid = dot_t(pick, valid_ref[...])[:, :1].astype(BF16)
    a_ref[...] = x_ref[...].reshape(a_ref.shape) * valid
    store_tiles(g_ref, dot_t(a_ref[...], full_ref[...]))
    combine(g_ref, keep_ref, send_ref, lax.axis_index("seg"), members)


def place(index):
    return (lax.axis_index("stn") >> index) & 1 == 1


def choose_kernel(own_ref, four_ref, out_ref):
    odd = place(1)

    @pl.when(odd)
    def _():
        out_ref[...] = four_ref[...]

    @pl.when(jnp.logical_not(odd))
    def _():
        out_ref[...] = own_ref[...]


def pair_kernel(members, at, early, a_ref, sib_ref, *refs):
    *piece_refs, full_ref, keep_ref, send_ref, b_ref, g_ref = refs
    seg = lax.axis_index("seg")
    width = piece_refs[0].shape[0] // 2
    half = b_ref.shape[1] // 2
    for i, piece_ref in enumerate(piece_refs):
        for part in range(2):
            to = part * half + i * width
            b_ref[0, to : to + width] = piece_ref[part * width : (part + 1) * width]
    if early:
        second = place(0)

        @pl.when(second)
        def _():
            b_ref[1] = b_ref[0]

        @pl.when(jnp.logical_not(second))
        def _():
            for part in range(2):
                frm = part * (full_ref.shape[0] // 2) + at
                b_ref[1, part * half : (part + 1) * half] = full_ref[frm : frm + half]

    store_tiles(g_ref.at[0], dot_t(a_ref[...], b_ref[0]))
    store_tiles(g_ref.at[1], dot_t(sib_ref[...], b_ref[1 if early else 0]))
    for which in range(2):
        combine(g_ref.at[which], keep_ref.at[which], send_ref.at[which], seg, members)


def add_kernel(keep_ref, got_ref, new_keep_ref, new_send_ref):
    for slot in range(keep_ref.shape[0]):
        out = new_send_ref if slot % 2 else new_keep_ref
        out[slot // 2] = keep_ref[slot] + got_ref[slot]


def home_kernel(*refs):
    *in_refs, out_ref = refs
    for k in range(out_ref.shape[0]):
        out_ref[k] = in_refs[2 * k][1] + in_refs[2 * k + 1][1]


def final_kernel(factor, live_ref, *refs):
    own_keep_ref, own_got_ref, *in_refs, early_ref, late_ref, out_ref = refs
    own = own_keep_ref[...] + own_got_ref[...]
    mine = [in_refs[i][0] + in_refs[i + 1][0] for i in range(0, len(in_refs), 2)]
    theirs = [r[i] for r in (early_ref, late_ref) for i in range(r.shape[0])]
    second = jnp.broadcast_to(lax.axis_index("stn") & 1, mine[0].shape) == 1
    by_offset = {
        4: mine[0::2],
        2: mine[1::2],
        1: [jnp.where(second, e, l) for e, l in zip(theirs[0::2], theirs[1::2])],
        3: [jnp.where(second, l, e) for e, l in zip(theirs[0::2], theirs[1::2])],
    }
    rows = out_ref.shape[0] // (2 * PAIRS)
    width = LANES // UNITS
    for offset in range(PAIRS):
        scale = live_ref[0, offset].astype(F32) * factor
        for part in range(2):
            if offset == 0:
                value = own[:, part * LANES : (part + 1) * LANES]
            else:
                value = jnp.concatenate([t[:, part * width : (part + 1) * width] for t in by_offset[offset]], axis=1)
            out_ref[pl.ds(2 * offset + part, rows, stride=2 * PAIRS), :] = value * scale


def tie(values, *others):
    return lax.optimization_barrier((values, others))[0]


def per_device(spectra, segment_valid, pair_live):
    block, channels, seg_local, _, freq = spectra.shape
    blocks, members = lax.axis_size("stn"), lax.axis_size("seg")
    factor = 1.0 / math.sqrt(seg_local * members * freq)
    rows, per, half = 2 * block * channels, block * channels // members, members // 2
    width = 2 * block // CHUNKS
    ids = range(blocks)

    def call(kernel, outs, operands, mib, scratch=(), specs=None, cost=COST):
        return pl.pallas_call(
            kernel,
            in_specs=specs or [VMEM] * len(operands),
            out_specs=[VMEM] * len(outs),
            out_shape=[jax.ShapeDtypeStruct(*out) for out in outs],
            scratch_shapes=list(scratch),
            compiler_params=params(mib),
            cost_estimate=cost and pl.CostEstimate(flops=cost, bytes_accessed=cost, transcendentals=0),
        )(*operands)

    full, valid, *own = call(
        extract_kernel,
        [((4 * block, freq), BF16), ((8, block), BF16)] + [((2 * width, freq), BF16)] * CHUNKS,
        [pltpu.with_memory_space_constraint(v, pltpu.HBM) for v in (spectra, segment_valid.reshape(1, block))],
        12,
        [
            pltpu.VMEM((block, 2, 1, 2, freq), BF16),
            pltpu.VMEM((1, block), jnp.int32),
            pltpu.SemaphoreType.DMA((2,)),
        ],
        [HBM] * 2,
    )

    def exchange(c, distance):
        return lax.ppermute(c, "stn", [(i ^ distance, i) for i in ids])

    def halve(keep, send, distance, kinds):
        got = lax.ppermute(send, "seg", [(i ^ distance, i) for i in range(members)])
        lead = (kinds,) if kinds else ()
        slots = keep.shape[len(lead)]
        if slots == 1:
            return keep.reshape(*lead, *keep.shape[-2:]), got.reshape(*lead, *keep.shape[-2:])
        shape = (max(kinds, 1) * slots // 2, *keep.shape[-2:])
        new = call(add_kernel, [(shape, F32)] * 2, [v.reshape(-1, *shape[1:]) for v in (keep, got)], 8)
        return [v.reshape(*lead, slots // 2, *shape[1:]) for v in new]

    def reduce(keep, send, kinds):
        steps = []
        distance = 1
        while distance < members:
            keep, send = halve(keep, send, distance, kinds)
            steps.append(keep if 2 * distance < members else send)
            distance *= 2
        return (keep, send), steps

    four = [lax.ppermute(c, "stn", [((i - 4) % blocks, i) for i in ids]) for c in own]
    two = []
    for k in range(CHUNKS):
        (c,) = call(choose_kernel, [((2 * width, freq), BF16)], [own[k], four[k]], 8)
        two.append(exchange(c, 2))

    a, keep, send = call(
        functools.partial(own_kernel, members),
        [((rows, freq), BF16)] + [((half, per, 4 * block), F32)] * 2,
        [spectra, valid, full],
        16,
        [pltpu.VMEM((4 * block // LANES, rows, LANES), F32)],
    )
    sibling = exchange(a, 1)
    (own_keep, own_got), own_steps = reduce(keep, send, 0)

    pieces, steps = [], [own_steps]
    size = 4 * block // UNITS
    for unit in range(2 * UNITS):
        early, which = unit % 2 == 0, unit // 2
        some = (four if early else two)[which * (CHUNKS // UNITS) : (which + 1) * (CHUNKS // UNITS)]
        waits = [s[i - 1] for i, s in enumerate(reversed(steps), 1) if i <= len(s)] if STEPS else []
        operand = tie(full, *waits) if waits else full
        keep, send = call(
            functools.partial(pair_kernel, members, which * (size // 2), early),
            [((2, half, per, size), F32)] * 2,
            [a, sibling, *some, operand],
            16,
            [pltpu.VMEM((2, size, freq), BF16), pltpu.VMEM((2, size // LANES, rows, LANES), F32)],
        )
        piece, new = reduce(keep, send, 2)
        pieces.append(piece)
        steps.append(new)

    early = [v for piece in pieces[:-1] for v in piece]
    (early_home,) = call(home_kernel, [((2 * UNITS - 1, per, size), F32)], early, 8)
    (late_home,) = call(home_kernel, [((1, per, size), F32)], pieces[-1], 8)
    sums = [v for piece in pieces for v in piece]
    operands = [pair_live, own_keep, own_got, *sums, exchange(early_home, 1), exchange(late_home, 1)]
    (out,) = call(
        functools.partial(final_kernel, factor),
        [((2 * PAIRS * per, 2 * block), F32)],
        operands,
        12,
        specs=[SMEM] + [VMEM] * (len(operands) - 1),
    )
    return out.reshape(block // members, channels, PAIRS, 2, 2 * block)


def solution(mesh):
    return jax.shard_map(
        per_device,
        mesh=mesh,
        in_specs=(P("stn", None, "seg", None, None), P("stn", "seg"), P("stn", None)),
        out_specs=P(("stn", "seg"), None, None, None, None),
        check_vma=False,
    )
```

time: 167 us -> 64.6 us (0.39)
  waiting for transfers between devices: 57.1 us -> 22.5 us
  local copies, waits for them, and re-layouts: 34.3 us -> 0.2 us
  other arithmetic: 33.4 us -> 0 us
  starting transfers between devices: 6.31 us -> 29.8 us
  matrix products: 18.8 us -> 0 us
  between operations: 16.4 us -> 0.17 us
  Pallas kernels: 0 us -> 11.8 us
    reduce_scatter x5 -> x0, waiting for transfers between devices: 49.7 us -> none  [per_device(): lax.psum_scatter(pair_term, 'seg', scatter_dimension=0, tiled=True)]
    ppermute x4 -> x21, starting transfers between devices: 5.92 us -> 29.8 us  [the longest x10 18.8 us: halve(): got = lax.ppermute(send, 'seg', [(i ^ distance, i) for i in range(members)])]
    another operation x12 -> x0, local copies, waits for them, and re-layouts: 20.7 us -> none  [the longest x10 18.8 us: per_device(): jnp.stack([remote, rotated], axis=0)]
    dot_general x5 -> x0, matrix products: 18.8 us -> none  [per_device(): lax.dot_general(local_rows, stacked, (((1,), (1,)), ((), ())), preferred_...]
    ppermute x4 -> x21, waiting for transfers between devices: 7.27 us -> 22.5 us  [the longest x10 11.5 us: halve(): got = lax.ppermute(send, 'seg', [(i ^ distance, i) for i in range(members)])]
    another operation x5 -> x0, other arithmetic: 14.6 us -> none  [per_device(): rotated = jnp.stack([-remote[:, :, :, 1], remote[:, :, :, 0]], axis=3)]
    neg x5 -> x0, other arithmetic: 14.2 us -> none  [per_device(): rotated = jnp.stack([-remote[:, :, :, 1], remote[:, :, :, 0]], axis=3)]
    pallas_call x0 -> x18, Pallas kernels: none -> 11.8 us  [call(): pl.pallas_call(kernel, in_specs=specs or [VMEM] * len(operands), out_spec...]
  transfers between devices with their start and end apart: 9 -> 21, of which waited for: 4 -> 10; matrix products, arithmetic and copies ran while one was open for 47% -> 0% of each run, Pallas kernels for 0% -> 11%
where the time goes in v2:
time: 64.6 us; the launch traced here: 64.5 us
  starting transfers between devices  29.8 us (46%)
  waiting for transfers between devices  22.5 us (35%)
  Pallas kernels  11.8 us (18%)
    ppermute x10, starting transfers between devices, halve(): got = lax.ppermute(send, 'seg', [(i ^ distance, i) for i in range(members)])  18.8 us
    pallas_call x18, Pallas kernels, call(): pl.pallas_call(kernel, in_specs=specs or [VMEM] * len(operands), out_spec...  11.8 us
    ppermute x10, waiting for transfers between devices, halve(): got = lax.ppermute(send, 'seg', [(i ^ distance, i) for i in range(members)])  11.5 us
    ppermute x4, waiting for transfers between devices, per_device(): lax.ppermute(c, 'stn', [((i - 4) % blocks, i) for i in ids])  9.47 us
    ppermute x4, starting transfers between devices, per_device(): lax.ppermute(c, 'stn', [((i - 4) % blocks, i) for i in ids])  6.15 us
    ppermute x7, starting transfers between devices, exchange(): return lax.ppermute(c, 'stn', [(i ^ distance, i) for i in ids])  4.78 us
    ppermute x7, waiting for transfers between devices, exchange(): return lax.ppermute(c, 'stn', [(i ^ distance, i) for i in ids])  1.54 us
  transfers between devices with their start and end apart: 21, of which 10 were waited for; matrix products, arithmetic and copies ran while one was open for 0% of the time, Pallas kernels for 11%

profile of v2, /device:TPU:0, one launch (start us, length us, event | category | flops | bytes accessed | tf_op | source)
XLA Modules:
  0.0 64.5 jit_solution(3918406257411722422)
XLA Ops:
  0.0 0.0 copy-start
  0.0 1.9 %shard_map.37 = (bf16[256,2048]{1,0:T(8,128)(2,1)S(1)}, bf16[8,64]{1,0:T(8,128)(2,1)S(1)}, bf16[64,2048]{1,0:T(8,128)(2,1)S(1)}, bf16[64,2048]{1,0:T(8,128)(2,1)...) custom-call(bf16[64,5,1,2,2048]{4,3,2,1,0:T(2,128)(2,1)} %x_ref.1, s32[1,64]{1,0:T(1,128)} %bitcast.42), custom_call_target="tpu_custom_call" | custom-call | tf_op jit(solution)/shard_map/pallas_call | solution.py:187
  1.9 0.2 copy-done
  2.1 1.4 %shard_map.38 = (bf16[640,2048]{1,0:T(8,128)(2,1)S(1)}, f32[2,80,256]{2,1,0:T(8,128)S(1)}, f32[2,80,256]{2,1,0:T(8,128)S(1)}) custom-call(bf16[64,5,1,2,2048]{4,3,2,1,0:T(2,128)(2,1)S(1)} %copy-done, bf16[8,64]{1,0:T(8,128)(2,1)S(1)} %get-tuple-element.36.valid_ref, bf16[256,2048]{1,0:T(8,128)(2,1)S(1)} %get-tuple-element.62.full_ref.refs_2_), custom_call_target="tpu_custom_call" | custom-call | tf_op jit(solution)/shard_map/pallas_call | solution.py:187
  3.5 0.5 collective-permute-start.2
  4.1 2.6 %collective-permute-start.3 = (bf16[64,2048]{1,0:T(8,128)(2,1)S(1)}, bf16[64,2048]{1,0:T(8,128)(2,1)S(1)}, u32[]{:S(2)}, u32[]{:S(2)}) collective-permute-start(bf16[64,2048]{1,0:T(8,128)(2,1)S(1)} %get-tuple-element.43.own_ref), channel_id=1, source_target_pairs={{16,0},{20,4},{24,8},{28,12},{0,16},{4,20},{8,24},{12,28},{17,1},{... | collective-permute-start | bytes 786440 | tf_op jit(solution)/shard_map/ppermute | solution.py:232
  6.6 0.1 collective-permute-start.4
  6.7 2.0 %collective-permute-start = (f32[2,80,256]{2,1,0:T(8,128)S(1)}, f32[2,80,256]{2,1,0:T(8,128)S(1)}, u32[]{:S(2)}, u32[]{:S(2)}) collective-permute-start(f32[2,80,256]{2,1,0:T(8,128)S(1)} %get-tuple-element.39), channel_id=1, source_target_pairs={{1,0},{0,1},{3,2},{2,3},{5,4},{4,5},{7,6},{6,7},{9,8},{8,9},{11,10... | collective-permute-start | bytes 491528 | tf_op jit(solution)/shard_map/ppermute | solution.py:214
  8.7 1.5 %collective-permute-start.11 = (bf16[64,2048]{1,0:T(8,128)(2,1)S(1)}, bf16[64,2048]{1,0:T(8,128)(2,1)S(1)}, u32[]{:S(2)}, u32[]{:S(2)}) collective-permute-start(bf16[64,2048]{1,0:T(8,128)(2,1)S(1)} %get-tuple-element.55.own_ref), channel_id=1, source_target_pairs={{16,0},{20,4},{24,8},{28,12},{0,16},{4,20},{8,24},{12,28},{17,1},{... | collective-permute-start | bytes 786440 | tf_op jit(solution)/shard_map/ppermute | solution.py:232
  10.3 3.6 %collective-permute-done.3.refs_0_.four_ref = bf16[64,2048]{1,0:T(8,128)(2,1)S(1)} collective-permute-done((bf16[64,2048]{1,0:T(8,128)(2,1)S(1)}, bf16[64,2048]{1,0:T(8,128)(2,1)S(1)}, u32[]{:S(2)}, u32[]{:S(2)}) %collective-permute-start.3) | collective-permute-done | bytes 262176 | tf_op jit(solution)/shard_map/ppermute | solution.py:232
  13.8 1.9 %collective-permute-start.12 = (bf16[64,2048]{1,0:T(8,128)(2,1)S(1)}, bf16[64,2048]{1,0:T(8,128)(2,1)S(1)}, u32[]{:S(2)}, u32[]{:S(2)}) collective-permute-start(bf16[64,2048]{1,0:T(8,128)(2,1)S(1)} %get-tuple-element.56.own_ref), channel_id=1, source_target_pairs={{16,0},{20,4},{24,8},{28,12},{0,16},{4,20},{8,24},{12,28},{17,1},{... | collective-permute-start | bytes 786440 | tf_op jit(solution)/shard_map/ppermute | solution.py:232
  15.8 3.6 %collective-permute-done.4.refs_1_.four_ref = bf16[64,2048]{1,0:T(8,128)(2,1)S(1)} collective-permute-done((bf16[64,2048]{1,0:T(8,128)(2,1)S(1)}, bf16[64,2048]{1,0:T(8,128)(2,1)S(1)}, u32[]{:S(2)}, u32[]{:S(2)}) %collective-permute-start.4) | collective-permute-done | bytes 262176 | tf_op jit(solution)/shard_map/ppermute | solution.py:232
  19.4 1.9 %collective-permute-start.7 = (bf16[64,2048]{1,0:T(8,128)(2,1)S(1)}, bf16[64,2048]{1,0:T(8,128)(2,1)S(1)}, u32[]{:S(2)}, u32[]{:S(2)}) collective-permute-start(bf16[64,2048]{1,0:T(8,128)(2,1)S(1)} %shard_map.42), channel_id=1, source_target_pairs={{8,0},{12,4},{0,8},{4,12},{24,16},{28,20},{16,24},{20,28},{9,1},{1... | collective-permute-start | bytes 786440 | tf_op jit(solution)/shard_map/ppermute | solution.py:211
  21.4 0.0 collective-permute-done.got_ref
  21.4 0.2 collective-permute-start.8
  21.6 0.0 collective-permute-done.2.sib_ref
  21.6 3.1 %collective-permute-start.1 = (f32[1,80,256]{2,1,0:T(8,128)S(1)}, f32[1,80,256]{2,1,0:T(8,128)S(1)}, u32[]{:S(2)}, u32[]{:S(2)}) collective-permute-start(f32[1,80,256]{2,1,0:T(8,128)S(1)} %get-tuple-element.41), channel_id=1, source_target_pairs={{2,0},{3,1},{0,2},{1,3},{6,4},{7,5},{4,6},{5,7},{10,8},{11,9},{8,1... | collective-permute-start | bytes 245768 | tf_op jit(solution)/shard_map/ppermute | solution.py:214
  24.7 1.8 %shard_map.40 = (f32[2,2,80,128]{3,2,1,0:T(8,128)S(1)}, f32[2,2,80,128]{3,2,1,0:T(8,128)S(1)}) custom-call(bf16[640,2048]{1,0:T(8,128)(2,1)S(1)} %get-tuple-element.42.a_ref, bf16[640,2048]{1,0:T(8,128)(2,1)S(1)} %collective-permute-done.2.sib_ref, bf16[64,2048]{1,0:T(8,128)(2,1)S(1)} %collective-permute-done.3.refs_0_.four_ref, ...), custom_call_target="tpu_custom_call" | custom-call | tf_op jit(solution)/shard_map/pallas_call | solution.py:187
  26.4 0.0 collective-permute-done.11.refs_0_.four_ref
  26.4 1.7 %collective-permute-start.5 = (f32[2,2,80,128]{3,2,1,0:T(8,128)S(1)}, f32[2,2,80,128]{3,2,1,0:T(8,128)S(1)}, u32[]{:S(2)}, u32[]{:S(2)}) collective-permute-start(f32[2,2,80,128]{3,2,1,0:T(8,128)S(1)} %get-tuple-element.47), channel_id=1, source_target_pairs={{1,0},{0,1},{3,2},{2,3},{5,4},{4,5},{7,6},{6,7},{9,8},{8,9},{11,10... | collective-permute-start | bytes 491528 | tf_op jit(solution)/shard_map/ppermute | solution.py:214
  28.1 2.3 %collective-permute-done.12.refs_1_.four_ref = bf16[64,2048]{1,0:T(8,128)(2,1)S(1)} collective-permute-done((bf16[64,2048]{1,0:T(8,128)(2,1)S(1)}, bf16[64,2048]{1,0:T(8,128)(2,1)S(1)}, u32[]{:S(2)}, u32[]{:S(2)}) %collective-permute-start.12) | collective-permute-done | bytes 262176 | tf_op jit(solution)/shard_map/ppermute | solution.py:232
  30.4 1.7 %collective-permute-start.15 = (bf16[64,2048]{1,0:T(8,128)(2,1)S(1)}, bf16[64,2048]{1,0:T(8,128)(2,1)S(1)}, u32[]{:S(2)}, u32[]{:S(2)}) collective-permute-start(bf16[64,2048]{1,0:T(8,128)(2,1)S(1)} %shard_map.48), channel_id=1, source_target_pairs={{8,0},{12,4},{0,8},{4,12},{24,16},{28,20},{16,24},{20,28},{9,1},{1... | collective-permute-start | bytes 786440 | tf_op jit(solution)/shard_map/ppermute | solution.py:211
  32.1 0.0 collective-permute-done.1
  32.2 0.4 collective-permute-start.16
  32.5 0.0 collective-permute-done.7.refs_0_
  32.5 0.3 collective-permute-done.8.refs_1_
  32.8 1.7 %shard_map.44 = (f32[2,2,80,128]{3,2,1,0:T(8,128)S(1)}, f32[2,2,80,128]{3,2,1,0:T(8,128)S(1)}) custom-call(bf16[640,2048]{1,0:T(8,128)(2,1)S(1)} %get-tuple-element.42.a_ref, bf16[640,2048]{1,0:T(8,128)(2,1)S(1)} %collective-permute-done.2.sib_ref, bf16[64,2048]{1,0:T(8,128)(2,1)S(1)} %collective-permute-done.7.refs_0_, ...), custom_call_target="tpu_custom_call" | custom-call | tf_op jit(solution)/shard_map/pallas_call | solution.py:187
  34.5 1.7 %collective-permute-start.9 = (f32[2,2,80,128]{3,2,1,0:T(8,128)S(1)}, f32[2,2,80,128]{3,2,1,0:T(8,128)S(1)}, u32[]{:S(2)}, u32[]{:S(2)}) collective-permute-start(f32[2,2,80,128]{3,2,1,0:T(8,128)S(1)} %get-tuple-element.52), channel_id=1, source_target_pairs={{1,0},{0,1},{3,2},{2,3},{5,4},{4,5},{7,6},{6,7},{9,8},{8,9},{11,10... | collective-permute-start | bytes 491528 | tf_op jit(solution)/shard_map/ppermute | solution.py:214
  36.2 0.0 collective-permute-done.5
  36.2 2.7 %collective-permute-start.6 = (f32[2,1,80,128]{3,2,0,1:T(8,128)S(1)}, f32[2,1,80,128]{3,2,0,1:T(8,128)S(1)}, u32[]{:S(2)}, u32[]{:S(2)}) collective-permute-start(f32[2,1,80,128]{3,2,0,1:T(8,128)S(1)} %bitcast.38), channel_id=1, source_target_pairs={{2,0},{3,1},{0,2},{1,3},{6,4},{7,5},{4,6},{5,7},{10,8},{11,9},{8,1... | collective-permute-start | bytes 245768 | tf_op jit(solution)/shard_map/ppermute | solution.py:214
  38.9 1.9 %collective-permute-done.9 = f32[2,2,80,128]{3,2,1,0:T(8,128)S(1)} collective-permute-done((f32[2,2,80,128]{3,2,1,0:T(8,128)S(1)}, f32[2,2,80,128]{3,2,1,0:T(8,128)S(1)}, u32[]{:S(2)}, u32[]{:S(2)}) %collective-permute-start.9) | collective-permute-done | bytes 163872 | tf_op jit(solution)/shard_map/ppermute | solution.py:214
  40.8 2.5 %collective-permute-start.10 = (f32[2,1,80,128]{3,2,0,1:T(8,128)S(1)}, f32[2,1,80,128]{3,2,0,1:T(8,128)S(1)}, u32[]{:S(2)}, u32[]{:S(2)}) collective-permute-start(f32[2,1,80,128]{3,2,0,1:T(8,128)S(1)} %bitcast.40), channel_id=1, source_target_pairs={{2,0},{3,1},{0,2},{1,3},{6,4},{7,5},{4,6},{5,7},{10,8},{11,9},{8,1... | collective-permute-start | bytes 245768 | tf_op jit(solution)/shard_map/ppermute | solution.py:214
  43.3 0.0 collective-permute-done.6
  43.3 1.8 %shard_map.46 = (f32[2,2,80,128]{3,2,1,0:T(8,128)S(1)}, f32[2,2,80,128]{3,2,1,0:T(8,128)S(1)}) custom-call(bf16[640,2048]{1,0:T(8,128)(2,1)S(1)} %get-tuple-element.42.a_ref, bf16[640,2048]{1,0:T(8,128)(2,1)S(1)} %collective-permute-done.2.sib_ref, bf16[64,2048]{1,0:T(8,128)(2,1)S(1)} %collective-permute-done.11.refs_0_.four_ref, ...), custom_call_target="tpu_custom_call" | custom-call | tf_op jit(solution)/shard_map/pallas_call | solution.py:187
  45.0 2.5 %collective-permute-start.13 = (f32[2,2,80,128]{3,2,1,0:T(8,128)S(1)}, f32[2,2,80,128]{3,2,1,0:T(8,128)S(1)}, u32[]{:S(2)}, u32[]{:S(2)}) collective-permute-start(f32[2,2,80,128]{3,2,1,0:T(8,128)S(1)} %get-tuple-element.59), channel_id=1, source_target_pairs={{1,0},{0,1},{3,2},{2,3},{5,4},{4,5},{7,6},{6,7},{9,8},{8,9},{11,10... | collective-permute-start | bytes 491528 | tf_op jit(solution)/shard_map/ppermute | solution.py:214
  47.6 0.0 collective-permute-done.10
  47.6 0.0 copy-start.1
  47.6 0.0 collective-permute-done.15.refs_0_
  47.6 0.0 collective-permute-done.16.refs_1_
  47.6 1.7 %shard_map.50 = (f32[2,2,80,128]{3,2,1,0:T(8,128)S(1)}, f32[2,2,80,128]{3,2,1,0:T(8,128)S(1)}) custom-call(bf16[640,2048]{1,0:T(8,128)(2,1)S(1)} %get-tuple-element.42.a_ref, bf16[640,2048]{1,0:T(8,128)(2,1)S(1)} %collective-permute-done.2.sib_ref, bf16[64,2048]{1,0:T(8,128)(2,1)S(1)} %collective-permute-done.15.refs_0_, ...), custom_call_target="tpu_custom_call" | custom-call | tf_op jit(solution)/shard_map/pallas_call | solution.py:187
  49.3 1.5 %collective-permute-start.17 = (f32[2,2,80,128]{3,2,1,0:T(8,128)S(1)}, f32[2,2,80,128]{3,2,1,0:T(8,128)S(1)}, u32[]{:S(2)}, u32[]{:S(2)}) collective-permute-start(f32[2,2,80,128]{3,2,1,0:T(8,128)S(1)} %get-tuple-element.64), channel_id=1, source_target_pairs={{1,0},{0,1},{3,2},{2,3},{5,4},{4,5},{7,6},{6,7},{9,8},{8,9},{11,10... | collective-permute-start | bytes 491528 | tf_op jit(solution)/shard_map/ppermute | solution.py:214
  50.8 2.5 %collective-permute-done.13 = f32[2,2,80,128]{3,2,1,0:T(8,128)S(1)} collective-permute-done((f32[2,2,80,128]{3,2,1,0:T(8,128)S(1)}, f32[2,2,80,128]{3,2,1,0:T(8,128)S(1)}, u32[]{:S(2)}, u32[]{:S(2)}) %collective-permute-start.13) | collective-permute-done | bytes 163872 | tf_op jit(solution)/shard_map/ppermute | solution.py:214
  53.4 0.1 collective-permute-start.14
  53.4 1.8 %collective-permute-done.17 = f32[2,2,80,128]{3,2,1,0:T(8,128)S(1)} collective-permute-done((f32[2,2,80,128]{3,2,1,0:T(8,128)S(1)}, f32[2,2,80,128]{3,2,1,0:T(8,128)S(1)}, u32[]{:S(2)}, u32[]{:S(2)}) %collective-permute-start.17) | collective-permute-done | bytes 163872 | tf_op jit(solution)/shard_map/ppermute | solution.py:214
  55.3 1.1 %collective-permute-start.18 = (f32[2,1,80,128]{3,2,0,1:T(8,128)S(1)}, f32[2,1,80,128]{3,2,0,1:T(8,128)S(1)}, u32[]{:S(2)}, u32[]{:S(2)}) collective-permute-start(f32[2,1,80,128]{3,2,0,1:T(8,128)S(1)} %bitcast.41), channel_id=1, source_target_pairs={{2,0},{3,1},{0,2},{1,3},{6,4},{7,5},{4,6},{5,7},{10,8},{11,9},{8,1... | collective-permute-start | bytes 245768 | tf_op jit(solution)/shard_map/ppermute | solution.py:214
  56.4 3.6 %collective-permute-done.14 = f32[2,1,80,128]{3,2,0,1:T(8,128)S(1)} collective-permute-done((f32[2,1,80,128]{3,2,0,1:T(8,128)S(1)}, f32[2,1,80,128]{3,2,0,1:T(8,128)S(1)}, u32[]{:S(2)}, u32[]{:S(2)}) %collective-permute-start.14) | collective-permute-done | bytes 81952 | tf_op jit(solution)/shard_map/ppermute | solution.py:214
  60.1 0.1 collective-permute-start.19
  60.1 1.7 %collective-permute-done.18 = f32[2,1,80,128]{3,2,0,1:T(8,128)S(1)} collective-permute-done((f32[2,1,80,128]{3,2,0,1:T(8,128)S(1)}, f32[2,1,80,128]{3,2,0,1:T(8,128)S(1)}, u32[]{:S(2)}, u32[]{:S(2)}) %collective-permute-start.18) | collective-permute-done | bytes 81952 | tf_op jit(solution)/shard_map/ppermute | solution.py:214
  61.8 0.0 collective-permute-start.20
  61.8 1.2 %collective-permute-done.20.refs_11_ = f32[1,80,128]{2,1,0:T(8,128)S(1)} collective-permute-done((f32[1,80,128]{2,1,0:T(8,128)S(1)}, f32[1,80,128]{2,1,0:T(8,128)S(1)}, u32[]{:S(2)}, u32[]{:S(2)}) %collective-permute-start.20) | collective-permute-done | bytes 40992 | tf_op jit(solution)/shard_map/ppermute | solution.py:211
  63.0 0.0 collective-permute-done.19.refs_10_
  63.0 0.0 copy-done.1
  63.0 1.5 %shard_map.54 = f32[800,128]{1,0:T(8,128)} custom-call(s32[1,5]{1,0:T(1,128)S(1)} %copy-done.1, f32[80,256]{1,0:T(8,128)S(1)} %bitcast.36, f32[80,256]{1,0:T(8,128)S(1)} %bitcast.37, f32[2,80,128]{2,1,0:T(8,128)S(1)} %get-tuple-element.48.refs_0_.refs_2_, f32[2,80,128]{2,1,0:T(8,128)S(1)} %bitcast.21, f32[2,80,128]{2,1,0:T(8,128)S(1)} %get-tuple-element.53.refs_2_.refs_4_, ...), custom_call_target="tpu_custom_call" | custom-call | tf_op jit(solution)/shard_map/pallas_call | solution.py:187
  (11 shorter events, 0.2 us)
Async XLA Ops:
  0.0 2.1 %copy-start = (bf16[64,5,1,2,2048]{4,3,2,1,0:T(2,128)(2,1)S(1)}, bf16[64,5,1,2,2048]{4,3,2,1,0:T(2,128)(2,1)}, u32[]{:S(2)}) copy-start(bf16[64,5,1,2,2048]{4,3,2,1,0:T(2,128)(2,1)} %x_ref.1) | copy-start | bytes 7864324
  3.5 18.0 %collective-permute-start.2 = (bf16[640,2048]{1,0:T(8,128)(2,1)S(1)}, bf16[640,2048]{1,0:T(8,128)(2,1)S(1)}, u32[]{:S(2)}, u32[]{:S(2)}) collective-permute-start(bf16[640,2048]{1,0:T(8,128)(2,1)S(1)} %get-tuple-element.42.a_ref), channel_id=1, source_target_pairs={{4,0},{0,4},{12,8},{8,12},{20,16},{16,20},{28,24},{24,28},{5,1},{1... | collective-permute-start | bytes 7864328 | tf_op jit(solution)/shard_map/ppermute | solution.py:211
  4.1 9.8 %collective-permute-start.3 = (bf16[64,2048]{1,0:T(8,128)(2,1)S(1)}, bf16[64,2048]{1,0:T(8,128)(2,1)S(1)}, u32[]{:S(2)}, u32[]{:S(2)}) collective-permute-start(bf16[64,2048]{1,0:T(8,128)(2,1)S(1)} %get-tuple-element.43.own_ref), channel_id=1, source_target_pairs={{16,0},{20,4},{24,8},{28,12},{0,16},{4,20},{8,24},{12,28},{17,1},{... | collective-permute-start | bytes 786440 | tf_op jit(solution)/shard_map/ppermute | solution.py:232
  6.6 12.8 %collective-permute-start.4 = (bf16[64,2048]{1,0:T(8,128)(2,1)S(1)}, bf16[64,2048]{1,0:T(8,128)(2,1)S(1)}, u32[]{:S(2)}, u32[]{:S(2)}) collective-permute-start(bf16[64,2048]{1,0:T(8,128)(2,1)S(1)} %get-tuple-element.44.own_ref), channel_id=1, source_target_pairs={{16,0},{20,4},{24,8},{28,12},{0,16},{4,20},{8,24},{12,28},{17,1},{... | collective-permute-start | bytes 786440 | tf_op jit(solution)/shard_map/ppermute | solution.py:232
  6.7 14.6 %collective-permute-start = (f32[2,80,256]{2,1,0:T(8,128)S(1)}, f32[2,80,256]{2,1,0:T(8,128)S(1)}, u32[]{:S(2)}, u32[]{:S(2)}) collective-permute-start(f32[2,80,256]{2,1,0:T(8,128)S(1)} %get-tuple-element.39), channel_id=1, source_target_pairs={{1,0},{0,1},{3,2},{2,3},{5,4},{4,5},{7,6},{6,7},{9,8},{8,9},{11,10... | collective-permute-start | bytes 491528 | tf_op jit(solution)/shard_map/ppermute | solution.py:214
  8.7 17.7 %collective-permute-start.11 = (bf16[64,2048]{1,0:T(8,128)(2,1)S(1)}, bf16[64,2048]{1,0:T(8,128)(2,1)S(1)}, u32[]{:S(2)}, u32[]{:S(2)}) collective-permute-start(bf16[64,2048]{1,0:T(8,128)(2,1)S(1)} %get-tuple-element.55.own_ref), channel_id=1, source_target_pairs={{16,0},{20,4},{24,8},{28,12},{0,16},{4,20},{8,24},{12,28},{17,1},{... | collective-permute-start | bytes 786440 | tf_op jit(solution)/shard_map/ppermute | solution.py:232
  13.8 16.6 %collective-permute-start.12 = (bf16[64,2048]{1,0:T(8,128)(2,1)S(1)}, bf16[64,2048]{1,0:T(8,128)(2,1)S(1)}, u32[]{:S(2)}, u32[]{:S(2)}) collective-permute-start(bf16[64,2048]{1,0:T(8,128)(2,1)S(1)} %get-tuple-element.56.own_ref), channel_id=1, source_target_pairs={{16,0},{20,4},{24,8},{28,12},{0,16},{4,20},{8,24},{12,28},{17,1},{... | collective-permute-start | bytes 786440 | tf_op jit(solution)/shard_map/ppermute | solution.py:232
  19.4 13.1 %collective-permute-start.7 = (bf16[64,2048]{1,0:T(8,128)(2,1)S(1)}, bf16[64,2048]{1,0:T(8,128)(2,1)S(1)}, u32[]{:S(2)}, u32[]{:S(2)}) collective-permute-start(bf16[64,2048]{1,0:T(8,128)(2,1)S(1)} %shard_map.42), channel_id=1, source_target_pairs={{8,0},{12,4},{0,8},{4,12},{24,16},{28,20},{16,24},{20,28},{9,1},{1... | collective-permute-start | bytes 786440 | tf_op jit(solution)/shard_map/ppermute | solution.py:211
  21.4 11.5 %collective-permute-start.8 = (bf16[64,2048]{1,0:T(8,128)(2,1)S(1)}, bf16[64,2048]{1,0:T(8,128)(2,1)S(1)}, u32[]{:S(2)}, u32[]{:S(2)}) collective-permute-start(bf16[64,2048]{1,0:T(8,128)(2,1)S(1)} %shard_map.43), channel_id=1, source_target_pairs={{8,0},{12,4},{0,8},{4,12},{24,16},{28,20},{16,24},{20,28},{9,1},{1... | collective-permute-start | bytes 786440 | tf_op jit(solution)/shard_map/ppermute | solution.py:211
  21.6 10.6 %collective-permute-start.1 = (f32[1,80,256]{2,1,0:T(8,128)S(1)}, f32[1,80,256]{2,1,0:T(8,128)S(1)}, u32[]{:S(2)}, u32[]{:S(2)}) collective-permute-start(f32[1,80,256]{2,1,0:T(8,128)S(1)} %get-tuple-element.41), channel_id=1, source_target_pairs={{2,0},{3,1},{0,2},{1,3},{6,4},{7,5},{4,6},{5,7},{10,8},{11,9},{8,1... | collective-permute-start | bytes 245768 | tf_op jit(solution)/shard_map/ppermute | solution.py:214
  26.4 9.8 %collective-permute-start.5 = (f32[2,2,80,128]{3,2,1,0:T(8,128)S(1)}, f32[2,2,80,128]{3,2,1,0:T(8,128)S(1)}, u32[]{:S(2)}, u32[]{:S(2)}) collective-permute-start(f32[2,2,80,128]{3,2,1,0:T(8,128)S(1)} %get-tuple-element.47), channel_id=1, source_target_pairs={{1,0},{0,1},{3,2},{2,3},{5,4},{4,5},{7,6},{6,7},{9,8},{8,9},{11,10... | collective-permute-start | bytes 491528 | tf_op jit(solution)/shard_map/ppermute | solution.py:214
  30.4 17.2 %collective-permute-start.15 = (bf16[64,2048]{1,0:T(8,128)(2,1)S(1)}, bf16[64,2048]{1,0:T(8,128)(2,1)S(1)}, u32[]{:S(2)}, u32[]{:S(2)}) collective-permute-start(bf16[64,2048]{1,0:T(8,128)(2,1)S(1)} %shard_map.48), channel_id=1, source_target_pairs={{8,0},{12,4},{0,8},{4,12},{24,16},{28,20},{16,24},{20,28},{9,1},{1... | collective-permute-start | bytes 786440 | tf_op jit(solution)/shard_map/ppermute | solution.py:211
  32.2 15.4 %collective-permute-start.16 = (bf16[64,2048]{1,0:T(8,128)(2,1)S(1)}, bf16[64,2048]{1,0:T(8,128)(2,1)S(1)}, u32[]{:S(2)}, u32[]{:S(2)}) collective-permute-start(bf16[64,2048]{1,0:T(8,128)(2,1)S(1)} %shard_map.49), channel_id=1, source_target_pairs={{8,0},{12,4},{0,8},{4,12},{24,16},{28,20},{16,24},{20,28},{9,1},{1... | collective-permute-start | bytes 786440 | tf_op jit(solution)/shard_map/ppermute | solution.py:211
  34.5 6.3 %collective-permute-start.9 = (f32[2,2,80,128]{3,2,1,0:T(8,128)S(1)}, f32[2,2,80,128]{3,2,1,0:T(8,128)S(1)}, u32[]{:S(2)}, u32[]{:S(2)}) collective-permute-start(f32[2,2,80,128]{3,2,1,0:T(8,128)S(1)} %get-tuple-element.52), channel_id=1, source_target_pairs={{1,0},{0,1},{3,2},{2,3},{5,4},{4,5},{7,6},{6,7},{9,8},{8,9},{11,10... | collective-permute-start | bytes 491528 | tf_op jit(solution)/shard_map/ppermute | solution.py:214
  36.2 7.0 %collective-permute-start.6 = (f32[2,1,80,128]{3,2,0,1:T(8,128)S(1)}, f32[2,1,80,128]{3,2,0,1:T(8,128)S(1)}, u32[]{:S(2)}, u32[]{:S(2)}) collective-permute-start(f32[2,1,80,128]{3,2,0,1:T(8,128)S(1)} %bitcast.38), channel_id=1, source_target_pairs={{2,0},{3,1},{0,2},{1,3},{6,4},{7,5},{4,6},{5,7},{10,8},{11,9},{8,1... | collective-permute-start | bytes 245768 | tf_op jit(solution)/shard_map/ppermute | solution.py:214
  40.8 6.8 %collective-permute-start.10 = (f32[2,1,80,128]{3,2,0,1:T(8,128)S(1)}, f32[2,1,80,128]{3,2,0,1:T(8,128)S(1)}, u32[]{:S(2)}, u32[]{:S(2)}) collective-permute-start(f32[2,1,80,128]{3,2,0,1:T(8,128)S(1)} %bitcast.40), channel_id=1, source_target_pairs={{2,0},{3,1},{0,2},{1,3},{6,4},{7,5},{4,6},{5,7},{10,8},{11,9},{8,1... | collective-permute-start | bytes 245768 | tf_op jit(solution)/shard_map/ppermute | solution.py:214
  45.0 8.3 %collective-permute-start.13 = (f32[2,2,80,128]{3,2,1,0:T(8,128)S(1)}, f32[2,2,80,128]{3,2,1,0:T(8,128)S(1)}, u32[]{:S(2)}, u32[]{:S(2)}) collective-permute-start(f32[2,2,80,128]{3,2,1,0:T(8,128)S(1)} %get-tuple-element.59), channel_id=1, source_target_pairs={{1,0},{0,1},{3,2},{2,3},{5,4},{4,5},{7,6},{6,7},{9,8},{8,9},{11,10... | collective-permute-start | bytes 491528 | tf_op jit(solution)/shard_map/ppermute | solution.py:214
  47.6 15.4 %copy-start.1 = (s32[1,5]{1,0:T(1,128)S(1)}, s32[1,5]{1,0:T(1,128)}, u32[]{:S(2)}) copy-start(s32[1,5]{1,0:T(1,128)} %live_ref.1) | copy-start | bytes 64
  49.3 6.0 %collective-permute-start.17 = (f32[2,2,80,128]{3,2,1,0:T(8,128)S(1)}, f32[2,2,80,128]{3,2,1,0:T(8,128)S(1)}, u32[]{:S(2)}, u32[]{:S(2)}) collective-permute-start(f32[2,2,80,128]{3,2,1,0:T(8,128)S(1)} %get-tuple-element.64), channel_id=1, source_target_pairs={{1,0},{0,1},{3,2},{2,3},{5,4},{4,5},{7,6},{6,7},{9,8},{8,9},{11,10... | collective-permute-start | bytes 491528 | tf_op jit(solution)/shard_map/ppermute | solution.py:214
  53.4 6.7 %collective-permute-start.14 = (f32[2,1,80,128]{3,2,0,1:T(8,128)S(1)}, f32[2,1,80,128]{3,2,0,1:T(8,128)S(1)}, u32[]{:S(2)}, u32[]{:S(2)}) collective-permute-start(f32[2,1,80,128]{3,2,0,1:T(8,128)S(1)} %bitcast.39), channel_id=1, source_target_pairs={{2,0},{3,1},{0,2},{1,3},{6,4},{7,5},{4,6},{5,7},{10,8},{11,9},{8,1... | collective-permute-start | bytes 245768 | tf_op jit(solution)/shard_map/ppermute | solution.py:214
  55.3 6.5 %collective-permute-start.18 = (f32[2,1,80,128]{3,2,0,1:T(8,128)S(1)}, f32[2,1,80,128]{3,2,0,1:T(8,128)S(1)}, u32[]{:S(2)}, u32[]{:S(2)}) collective-permute-start(f32[2,1,80,128]{3,2,0,1:T(8,128)S(1)} %bitcast.41), channel_id=1, source_target_pairs={{2,0},{3,1},{0,2},{1,3},{6,4},{7,5},{4,6},{5,7},{10,8},{11,9},{8,1... | collective-permute-start | bytes 245768 | tf_op jit(solution)/shard_map/ppermute | solution.py:214
  60.1 3.0 %collective-permute-start.19 = (f32[3,80,128]{2,1,0:T(8,128)S(1)}, f32[3,80,128]{2,1,0:T(8,128)S(1)}, u32[]{:S(2)}, u32[]{:S(2)}) collective-permute-start(f32[3,80,128]{2,1,0:T(8,128)S(1)} %shard_map.52), channel_id=1, source_target_pairs={{4,0},{0,4},{12,8},{8,12},{20,16},{16,20},{28,24},{24,28},{5,1},{1... | collective-permute-start | bytes 368648 | tf_op jit(solution)/shard_map/ppermute | solution.py:211
  61.8 1.2 %collective-permute-start.20 = (f32[1,80,128]{2,1,0:T(8,128)S(1)}, f32[1,80,128]{2,1,0:T(8,128)S(1)}, u32[]{:S(2)}, u32[]{:S(2)}) collective-permute-start(f32[1,80,128]{2,1,0:T(8,128)S(1)} %shard_map.53), channel_id=1, source_target_pairs={{4,0},{0,4},{12,8},{8,12},{20,16},{16,20},{28,24},{24,28},{5,1},{1... | collective-permute-start | bytes 122888 | tf_op jit(solution)/shard_map/ppermute | solution.py:211

commit v3 on v2

--- a/solution.py
+++ b/solution.py
@@ -10,8 +10,19 @@
 
 PAIRS = 5
 CHUNKS = 4
-UNITS = 2
-STEPS = True
+ORDER = ("F0", "F1", "U", "F2", "F3", "X0", "X1", "F0F1", "X2", "X0X1", "X3", "F2F3", "X2X3")
+TIES = {
+    "F0F1b": ("X1",),
+    "F2": ("Ua",),
+    "F2F3": ("F0F1b",),
+    "F3": ("F1", "S"),
+    "X0": ("S", "Ua"),
+    "X0X1": ("F0F1k", "F3", "Ub"),
+    "X0X1b": ("F3",),
+    "X2": ("F0F1k",),
+    "X2X3": ("X0X1a",),
+    "X3": ("F0F1a", "Ub", "X1"),
+}
 COST = None
 LANES = 128
 VMEM = pl.BlockSpec(memory_space=pltpu.VMEM)
@@ -65,20 +76,24 @@
         g_ref[tile] = value[:, tile * LANES : (tile + 1) * LANES]
 
 
-def combine(g_ref, out_keep, out_send, seg, members):
-    tiles, rows = g_ref.shape[0], g_ref.shape[1] // members
-    sign = jnp.where(iota((1, LANES), 1) < LANES // 2, 1.0, -1.0)
+def combine(even, odd, span):
+    part = iota((1, LANES), 1) // span % 2
+    swapped = pltpu.roll(odd, span, 1)
+    if 2 * span < LANES:
+        swapped = jnp.where(part == 0, pltpu.roll(odd, LANES - span, 1), swapped)
+    return swapped + jnp.where(part == 0, 1.0, -1.0) * even
+
+
+def scatter(g_ref, out_keep, out_send, seg, members, finish):
+    rows = g_ref.shape[-2] // members
     for slot in range(members):
         at = pl.multiple_of((seg ^ slot) * rows, 8)
-        out = out_send if slot % 2 else out_keep
-        even = [g_ref[t, pl.ds(at, rows // 2, stride=2), :] for t in range(tiles)]
-        odd = [g_ref[t, pl.ds(at + 1, rows // 2, stride=2), :] for t in range(tiles)]
-        if tiles == 1:
-            out[slot // 2] = pltpu.roll(odd[0], LANES // 2, 1) + sign * even[0]
-        for t in range(tiles // 2):
-            u = t + tiles // 2
-            out[slot // 2, :, t * LANES : (t + 1) * LANES] = even[t] + odd[u]
-            out[slot // 2, :, u * LANES : (u + 1) * LANES] = odd[t] - even[u]
+        finish(
+            [g_ref[t, pl.ds(at, rows // 2, stride=2), :] for t in range(g_ref.shape[0])],
+            [g_ref[t, pl.ds(at + 1, rows // 2, stride=2), :] for t in range(g_ref.shape[0])],
+            out_send if slot % 2 else out_keep,
+            slot // 2,
+        )
 
 
 def own_kernel(members, x_ref, valid_ref, full_ref, a_ref, keep_ref, send_ref, g_ref):
@@ -88,7 +103,12 @@
     valid = dot_t(pick, valid_ref[...])[:, :1].astype(BF16)
     a_ref[...] = x_ref[...].reshape(a_ref.shape) * valid
     store_tiles(g_ref, dot_t(a_ref[...], full_ref[...]))
-    combine(g_ref, keep_ref, send_ref, lax.axis_index("seg"), members)
+
+    def finish(even, odd, out, slot):
+        out[slot, :, :LANES] = even[0] + odd[1]
+        out[slot, :, LANES:] = odd[0] - even[1]
+
+    scatter(g_ref, keep_ref, send_ref, lax.axis_index("seg"), members, finish)
 
 
 def place(index):
@@ -107,32 +127,33 @@
         out_ref[...] = own_ref[...]
 
 
-def pair_kernel(members, at, early, a_ref, sib_ref, *refs):
-    *piece_refs, full_ref, keep_ref, send_ref, b_ref, g_ref = refs
-    seg = lax.axis_index("seg")
+def unit_kernel(members, kinds, a_ref, sib_ref, *refs):
+    count = len(kinds)
+    piece_refs, own_refs = refs[:count], refs[count : 2 * count]
+    _, keep_ref, send_ref, b_ref, g_ref = refs[2 * count :]
     width = piece_refs[0].shape[0] // 2
-    half = b_ref.shape[1] // 2
-    for i, piece_ref in enumerate(piece_refs):
+    second = place(0)
+
+    def fill(which, i, ref):
         for part in range(2):
-            to = part * half + i * width
-            b_ref[0, to : to + width] = piece_ref[part * width : (part + 1) * width]
-    if early:
-        second = place(0)
-
-        @pl.when(second)
-        def _():
-            b_ref[1] = b_ref[0]
-
-        @pl.when(jnp.logical_not(second))
-        def _():
-            for part in range(2):
-                frm = part * (full_ref.shape[0] // 2) + at
-                b_ref[1, part * half : (part + 1) * half] = full_ref[frm : frm + half]
-
-    store_tiles(g_ref.at[0], dot_t(a_ref[...], b_ref[0]))
-    store_tiles(g_ref.at[1], dot_t(sib_ref[...], b_ref[1 if early else 0]))
-    for which in range(2):
-        combine(g_ref.at[which], keep_ref.at[which], send_ref.at[which], seg, members)
+            to = (part * count + i) * width
+            b_ref[which, to : to + width] = ref[part * width : (part + 1) * width]
+
+    for i, kind in enumerate(kinds):
+        fill(0, i, piece_refs[i])
+        if kind == "F":
+            pl.when(second)(functools.partial(fill, 1, i, piece_refs[i]))
+            pl.when(jnp.logical_not(second))(functools.partial(fill, 1, i, own_refs[i]))
+        else:
+            fill(1, i, piece_refs[i])
+    mine, theirs = dot_t(a_ref[...], b_ref[0]), dot_t(sib_ref[...], b_ref[1])
+    store_tiles(g_ref, jnp.concatenate([mine, theirs], axis=1))
+
+    def finish(even, odd, out, slot):
+        for t in range(len(even)):
+            out[t, slot] = combine(even[t], odd[t], count * width)
+
+    scatter(g_ref, keep_ref, send_ref, lax.axis_index("seg"), members, finish)
 
 
 def add_kernel(keep_ref, got_ref, new_keep_ref, new_send_ref):
@@ -144,35 +165,47 @@
 def home_kernel(*refs):
     *in_refs, out_ref = refs
     for k in range(out_ref.shape[0]):
-        out_ref[k] = in_refs[2 * k][1] + in_refs[2 * k + 1][1]
-
-
-def final_kernel(factor, live_ref, *refs):
+        last = in_refs[2 * k].shape[0] - 1
+        out_ref[k] = in_refs[2 * k][last] + in_refs[2 * k + 1][last]
+
+
+def final_kernel(factor, units, live_ref, *refs):
     own_keep_ref, own_got_ref, *in_refs, early_ref, late_ref, out_ref = refs
     own = own_keep_ref[...] + own_got_ref[...]
-    mine = [in_refs[i][0] + in_refs[i + 1][0] for i in range(0, len(in_refs), 2)]
+    second = jnp.broadcast_to(lax.axis_index("stn") & 1, own[:, :LANES].shape) == 1
     theirs = [r[i] for r in (early_ref, late_ref) for i in range(r.shape[0])]
-    second = jnp.broadcast_to(lax.axis_index("stn") & 1, mine[0].shape) == 1
-    by_offset = {
-        4: mine[0::2],
-        2: mine[1::2],
-        1: [jnp.where(second, e, l) for e, l in zip(theirs[0::2], theirs[1::2])],
-        3: [jnp.where(second, l, e) for e, l in zip(theirs[0::2], theirs[1::2])],
-    }
+    width = LANES // CHUNKS
+    columns = {}
+    for u, unit in enumerate(units):
+        tiles = in_refs[2 * u].shape[0]
+        mine = in_refs[2 * u][0] + in_refs[2 * u + 1][0]
+        for i, (kind, k) in enumerate(unit):
+            for part in range(2):
+                at = (part * len(unit) + i) * width
+                columns[kind, k, part] = mine[:, at : at + width]
+                at += LANES // 2 if tiles == 1 else 0
+                columns[kind + "s", k, part] = theirs[u][:, at : at + width]
     rows = out_ref.shape[0] // (2 * PAIRS)
-    width = LANES // UNITS
-    for offset in range(PAIRS):
-        scale = live_ref[0, offset].astype(F32) * factor
-        for part in range(2):
-            if offset == 0:
-                value = own[:, part * LANES : (part + 1) * LANES]
-            else:
-                value = jnp.concatenate([t[:, part * width : (part + 1) * width] for t in by_offset[offset]], axis=1)
+
+    def joined(kind, part):
+        return jnp.concatenate([columns[kind, k, part] for k in range(CHUNKS)], axis=1)
+
+    for part in range(2):
+        four, two = joined("Fs", part), joined("Xs", part)
+        values = [
+            own[:, part * LANES : (part + 1) * LANES],
+            jnp.where(second, four, two),
+            joined("X", part),
+            jnp.where(second, two, four),
+            joined("F", part),
+        ]
+        for offset, value in enumerate(values):
+            scale = live_ref[0, offset].astype(F32) * factor
             out_ref[pl.ds(2 * offset + part, rows, stride=2 * PAIRS), :] = value * scale
 
 
 def tie(values, *others):
-    return lax.optimization_barrier((values, others))[0]
+    return lax.optimization_barrier((values, others))[0] if others else values
 
 
 def per_device(spectra, segment_valid, pair_live):
@@ -220,20 +253,15 @@
         new = call(add_kernel, [(shape, F32)] * 2, [v.reshape(-1, *shape[1:]) for v in (keep, got)], 8)
         return [v.reshape(*lead, slots // 2, *shape[1:]) for v in new]
 
-    def reduce(keep, send, kinds):
-        steps = []
+    def reduce(keep, send, kinds, name):
         distance = 1
         while distance < members:
+            if 2 * distance == members:
+                send = tie(send, *after(name + "b"))
             keep, send = halve(keep, send, distance, kinds)
-            steps.append(keep if 2 * distance < members else send)
+            done[name + ("a" if distance == 1 else "b")] = keep if 2 * distance < members else send
             distance *= 2
-        return (keep, send), steps
-
-    four = [lax.ppermute(c, "stn", [((i - 4) % blocks, i) for i in ids]) for c in own]
-    two = []
-    for k in range(CHUNKS):
-        (c,) = call(choose_kernel, [((2 * width, freq), BF16)], [own[k], four[k]], 8)
-        two.append(exchange(c, 2))
+        return keep, send
 
     a, keep, send = call(
         functools.partial(own_kernel, members),
@@ -243,33 +271,62 @@
         [pltpu.VMEM((4 * block // LANES, rows, LANES), F32)],
     )
     sibling = exchange(a, 1)
-    (own_keep, own_got), own_steps = reduce(keep, send, 0)
-
-    pieces, steps = [], [own_steps]
-    size = 4 * block // UNITS
-    for unit in range(2 * UNITS):
-        early, which = unit % 2 == 0, unit // 2
-        some = (four if early else two)[which * (CHUNKS // UNITS) : (which + 1) * (CHUNKS // UNITS)]
-        waits = [s[i - 1] for i, s in enumerate(reversed(steps), 1) if i <= len(s)] if STEPS else []
-        operand = tie(full, *waits) if waits else full
+    done = {}
+
+    def after(name):
+        return [done[n] for n in TIES.get(name, ())]
+
+    sibling = exchange(tie(a, *after("S")), 1)
+    done["S"] = sibling
+
+    def four_of(k):
+        value = tie(own[k], *after("F%d" % k))
+        done["F%d" % k] = lax.ppermute(value, "stn", [((i - 4) % blocks, i) for i in ids])
+        return done["F%d" % k]
+
+    def two_of(k):
+        value = tie(own[k], *after("X%d" % k))
+        (c,) = call(choose_kernel, [((2 * width, freq), BF16)], [value, four[k]], 8)
+        done["X%d" % k] = exchange(c, 2)
+        return done["X%d" % k]
+
+    def unit(name):
+        pieces = [(name[i], int(name[i + 1])) for i in range(0, len(name), 2)]
+        columns = 2 * width * len(pieces)
+        tiles = max(1, 2 * columns // LANES)
         keep, send = call(
-            functools.partial(pair_kernel, members, which * (size // 2), early),
-            [((2, half, per, size), F32)] * 2,
-            [a, sibling, *some, operand],
+            functools.partial(unit_kernel, members, [p[0] for p in pieces]),
+            [((tiles, half, per, LANES), F32)] * 2,
+            [a, sibling]
+            + [(four if kind == "F" else two)[k] for kind, k in pieces]
+            + [own[k] for _, k in pieces]
+            + [tie(valid, *after(name))],
             16,
-            [pltpu.VMEM((2, size, freq), BF16), pltpu.VMEM((2, size // LANES, rows, LANES), F32)],
+            [pltpu.VMEM((2, columns, freq), BF16), pltpu.VMEM((tiles, rows, LANES), F32)],
         )
-        piece, new = reduce(keep, send, 2)
-        pieces.append(piece)
-        steps.append(new)
-
+        done[name + "k"] = keep
+        return pieces, reduce(keep, send, tiles, name)
+
+    four, two = [], []
+    units = []
+    for name in ORDER:
+        if name == "U":
+            own_keep, own_got = reduce(keep, send, 0, "U")
+        elif len(name) == 2 and name[0] == "F" and len(four) <= int(name[1]):
+            four.append(four_of(int(name[1])))
+        elif len(name) == 2 and name[0] == "X" and len(two) <= int(name[1]):
+            two.append(two_of(int(name[1])))
+        else:
+            units.append(unit(name))
+    pieces = [piece for _, piece in units]
+    units = [names for names, _ in units]
     early = [v for piece in pieces[:-1] for v in piece]
-    (early_home,) = call(home_kernel, [((2 * UNITS - 1, per, size), F32)], early, 8)
-    (late_home,) = call(home_kernel, [((1, per, size), F32)], pieces[-1], 8)
+    (early_home,) = call(home_kernel, [((len(pieces) - 1, per, LANES), F32)], early, 8)
+    (late_home,) = call(home_kernel, [((1, per, LANES), F32)], pieces[-1], 8)
     sums = [v for piece in pieces for v in piece]
     operands = [pair_live, own_keep, own_got, *sums, exchange(early_home, 1), exchange(late_home, 1)]
     (out,) = call(
-        functools.partial(final_kernel, factor),
+        functools.partial(final_kernel, factor, units),
         [((2 * PAIRS * per, 2 * block), F32)],
         operands,
         12,

time: 64.6 us -> 60.2 us (0.932)
  waiting for transfers between devices: 22.5 us -> 15.8 us
  starting transfers between devices: 29.8 us -> 32 us
    ppermute x4, waiting for transfers between devices: 9.47 us -> 4.36 us  [four_of(): lax.ppermute(value, 'stn', [((i - 4) % blocks, i) for i in ids])]
    ppermute x7, starting transfers between devices: 4.78 us -> 7.35 us  [exchange(): return lax.ppermute(c, 'stn', [(i ^ distance, i) for i in ids])]
    ppermute x10, waiting for transfers between devices: 11.5 us -> 10.2 us  [halve(): got = lax.ppermute(send, 'seg', [(i ^ distance, i) for i in range(members)])]
    ppermute x4, starting transfers between devices: 6.15 us -> 5.12 us  [four_of(): lax.ppermute(value, 'stn', [((i - 4) % blocks, i) for i in ids])]
    ppermute x10, starting transfers between devices: 18.8 us -> 19.5 us  [halve(): got = lax.ppermute(send, 'seg', [(i ^ distance, i) for i in range(members)])]
  transfers between devices with their start and end apart: 21 -> 21, of which waited for: 10 -> 11; matrix products, arithmetic and copies ran while one was open for 0% -> 0% of each run, Pallas kernels for 11% -> 12%
where the time goes in v3:
time: 60.2 us; the launch traced here: 60 us
  starting transfers between devices  32 us (53%)
  waiting for transfers between devices  15.8 us (26%)
  Pallas kernels  11.9 us (20%)
    ppermute x10, starting transfers between devices, halve(): got = lax.ppermute(send, 'seg', [(i ^ distance, i) for i in range(members)])  19.5 us
    pallas_call x18, Pallas kernels, call(): pl.pallas_call(kernel, in_specs=specs or [VMEM] * len(operands), out_spec...  11.9 us
    ppermute x10, waiting for transfers between devices, halve(): got = lax.ppermute(send, 'seg', [(i ^ distance, i) for i in range(members)])  10.2 us
    ppermute x7, starting transfers between devices, exchange(): return lax.ppermute(c, 'stn', [(i ^ distance, i) for i in ids])  7.35 us
    ppermute x4, starting transfers between devices, four_of(): lax.ppermute(value, 'stn', [((i - 4) % blocks, i) for i in ids])  5.12 us
    ppermute x4, waiting for transfers between devices, four_of(): lax.ppermute(value, 'stn', [((i - 4) % blocks, i) for i in ids])  4.36 us
    ppermute x7, waiting for transfers between devices, exchange(): return lax.ppermute(c, 'stn', [(i ^ distance, i) for i in ids])  1.22 us
  transfers between devices with their start and end apart: 21, of which 11 were waited for; matrix products, arithmetic and copies ran while one was open for 0% of the time, Pallas kernels for 12%

profile of v3, /device:TPU:0, one launch (start us, length us, event | category | flops | bytes accessed | tf_op | source)
XLA Modules:
  0.0 60.0 jit_solution(9501699633167189731)
XLA Ops:
  0.0 0.0 copy-start
  0.0 1.9 %shard_map.37 = (bf16[256,2048]{1,0:T(8,128)(2,1)S(1)}, bf16[8,64]{1,0:T(8,128)(2,1)S(1)}, bf16[64,2048]{1,0:T(8,128)(2,1)S(1)}, bf16[64,2048]{1,0:T(8,128)(2,1)...) custom-call(bf16[64,5,1,2,2048]{4,3,2,1,0:T(2,128)(2,1)} %x_ref.1, s32[1,64]{1,0:T(1,128)} %bitcast.42), custom_call_target="tpu_custom_call" | custom-call | tf_op jit(solution)/shard_map/pallas_call | solution.py:220
  1.9 0.2 copy-done
  2.1 1.5 %shard_map.38 = (bf16[640,2048]{1,0:T(8,128)(2,1)S(1)}, f32[2,80,256]{2,1,0:T(8,128)S(1)}, f32[2,80,256]{2,1,0:T(8,128)S(1)}) custom-call(bf16[64,5,1,2,2048]{4,3,2,1,0:T(2,128)(2,1)S(1)} %copy-done, bf16[8,64]{1,0:T(8,128)(2,1)S(1)} %get-tuple-element.66.valid_ref.refs_4_, bf16[256,2048]{1,0:T(8,128)(2,1)S(1)} %get-tuple-element.42.full_ref), custom_call_target="tpu_custom_call" | custom-call | tf_op jit(solution)/shard_map/pallas_call | solution.py:220
  3.5 0.5 collective-permute-start.2
  4.1 2.6 %collective-permute-start.4 = (bf16[64,2048]{1,0:T(8,128)(2,1)S(1)}, bf16[64,2048]{1,0:T(8,128)(2,1)S(1)}, u32[]{:S(2)}, u32[]{:S(2)}) collective-permute-start(bf16[64,2048]{1,0:T(8,128)(2,1)S(1)} %get-tuple-element.49.refs_3_.own_ref), channel_id=1, source_target_pairs={{16,0},{20,4},{24,8},{28,12},{0,16},{4,20},{8,24},{12,28},{17,1},{... | collective-permute-start | bytes 786440 | tf_op jit(solution)/shard_map/ppermute | solution.py:284
  6.7 1.6 %collective-permute-start = (f32[2,80,256]{2,1,0:T(8,128)S(1)}, f32[2,80,256]{2,1,0:T(8,128)S(1)}, u32[]{:S(2)}, u32[]{:S(2)}) collective-permute-start(f32[2,80,256]{2,1,0:T(8,128)S(1)} %get-tuple-element.44), channel_id=1, source_target_pairs={{1,0},{0,1},{3,2},{2,3},{5,4},{4,5},{7,6},{6,7},{9,8},{8,9},{11,10... | collective-permute-start | bytes 491528 | tf_op jit(solution)/shard_map/ppermute | solution.py:247
  8.2 0.5 collective-permute-start.3
  8.7 4.2 %collective-permute-done.got_ref = f32[2,80,256]{2,1,0:T(8,128)S(1)} collective-permute-done((f32[2,80,256]{2,1,0:T(8,128)S(1)}, f32[2,80,256]{2,1,0:T(8,128)S(1)}, u32[]{:S(2)}, u32[]{:S(2)}) %collective-permute-start) | collective-permute-done | bytes 163872 | tf_op jit(solution)/shard_map/ppermute | solution.py:247
  13.0 0.9 %collective-permute-done.4.refs_1_.four_ref = bf16[64,2048]{1,0:T(8,128)(2,1)S(1)} collective-permute-done((bf16[64,2048]{1,0:T(8,128)(2,1)S(1)}, bf16[64,2048]{1,0:T(8,128)(2,1)S(1)}, u32[]{:S(2)}, u32[]{:S(2)}) %collective-permute-start.4) | collective-permute-done | bytes 262176 | tf_op jit(solution)/shard_map/ppermute | solution.py:284
  13.8 2.0 %collective-permute-start.6 = (bf16[64,2048]{1,0:T(8,128)(2,1)S(1)}, bf16[64,2048]{1,0:T(8,128)(2,1)S(1)}, u32[]{:S(2)}, u32[]{:S(2)}) collective-permute-start(bf16[64,2048]{1,0:T(8,128)(2,1)S(1)} %shard_map.42), channel_id=1, source_target_pairs={{8,0},{12,4},{0,8},{4,12},{24,16},{28,20},{16,24},{20,28},{9,1},{1... | collective-permute-start | bytes 786440 | tf_op jit(solution)/shard_map/ppermute | solution.py:244
  15.8 1.5 %collective-permute-start.12 = (bf16[64,2048]{1,0:T(8,128)(2,1)S(1)}, bf16[64,2048]{1,0:T(8,128)(2,1)S(1)}, u32[]{:S(2)}, u32[]{:S(2)}) collective-permute-start(bf16[64,2048]{1,0:T(8,128)(2,1)S(1)} %get-tuple-element.71.refs_2_.own_ref), channel_id=1, source_target_pairs={{16,0},{20,4},{24,8},{28,12},{0,16},{4,20},{8,24},{12,28},{17,1},{... | collective-permute-start | bytes 786440 | tf_op jit(solution)/shard_map/ppermute | solution.py:284
  17.3 0.0 collective-permute-done.2.sib_ref
  17.4 0.5 collective-permute-start.9
  17.9 2.6 %collective-permute-start.1 = (f32[1,80,256]{2,1,0:T(8,128)S(1)}, f32[1,80,256]{2,1,0:T(8,128)S(1)}, u32[]{:S(2)}, u32[]{:S(2)}) collective-permute-start(f32[1,80,256]{2,1,0:T(8,128)S(1)} %get-tuple-element.46), channel_id=1, source_target_pairs={{2,0},{3,1},{0,2},{1,3},{6,4},{7,5},{4,6},{5,7},{10,8},{11,9},{8,1... | collective-permute-start | bytes 245768 | tf_op jit(solution)/shard_map/ppermute | solution.py:247
  20.4 0.0 collective-permute-done.3.refs_0_.four_ref
  20.5 1.0 %collective-permute-start.8 = (bf16[64,2048]{1,0:T(8,128)(2,1)S(1)}, bf16[64,2048]{1,0:T(8,128)(2,1)S(1)}, u32[]{:S(2)}, u32[]{:S(2)}) collective-permute-start(bf16[64,2048]{1,0:T(8,128)(2,1)S(1)} %shard_map.43), channel_id=1, source_target_pairs={{8,0},{12,4},{0,8},{4,12},{24,16},{28,20},{16,24},{20,28},{9,1},{1... | collective-permute-start | bytes 786440 | tf_op jit(solution)/shard_map/ppermute | solution.py:244
  21.4 1.8 %shard_map.40 = (f32[2,2,80,128]{3,2,1,0:T(8,128)S(1)}, f32[2,2,80,128]{3,2,1,0:T(8,128)S(1)}) custom-call(bf16[640,2048]{1,0:T(8,128)(2,1)S(1)} %get-tuple-element.47.a_ref, bf16[640,2048]{1,0:T(8,128)(2,1)S(1)} %collective-permute-done.2.sib_ref, bf16[64,2048]{1,0:T(8,128)(2,1)S(1)} %collective-permute-done.3.refs_0_.four_ref, ...), custom_call_target="tpu_custom_call" | custom-call | tf_op jit(solution)/shard_map/pallas_call | solution.py:220
  23.2 0.0 collective-permute-done.1
  23.3 1.6 %collective-permute-start.5 = (f32[2,2,80,128]{3,2,1,0:T(8,128)S(1)}, f32[2,2,80,128]{3,2,1,0:T(8,128)S(1)}, u32[]{:S(2)}, u32[]{:S(2)}) collective-permute-start(f32[2,2,80,128]{3,2,1,0:T(8,128)S(1)} %get-tuple-element.51), channel_id=1, source_target_pairs={{1,0},{0,1},{3,2},{2,3},{5,4},{4,5},{7,6},{6,7},{9,8},{8,9},{11,10... | collective-permute-start | bytes 491528 | tf_op jit(solution)/shard_map/ppermute | solution.py:247
  24.9 0.0 collective-permute-done.6.refs_1_
  24.9 0.1 collective-permute-done.12.refs_0_.four_ref
  25.1 2.0 %collective-permute-start.15 = (bf16[64,2048]{1,0:T(8,128)(2,1)S(1)}, bf16[64,2048]{1,0:T(8,128)(2,1)S(1)}, u32[]{:S(2)}, u32[]{:S(2)}) collective-permute-start(bf16[64,2048]{1,0:T(8,128)(2,1)S(1)} %shard_map.48), channel_id=1, source_target_pairs={{8,0},{12,4},{0,8},{4,12},{24,16},{28,20},{16,24},{20,28},{9,1},{1... | collective-permute-start | bytes 786440 | tf_op jit(solution)/shard_map/ppermute | solution.py:244
  27.1 3.3 %collective-permute-done.9.refs_1_.four_ref = bf16[64,2048]{1,0:T(8,128)(2,1)S(1)} collective-permute-done((bf16[64,2048]{1,0:T(8,128)(2,1)S(1)}, bf16[64,2048]{1,0:T(8,128)(2,1)S(1)}, u32[]{:S(2)}, u32[]{:S(2)}) %collective-permute-start.9) | collective-permute-done | bytes 262176 | tf_op jit(solution)/shard_map/ppermute | solution.py:284
  30.4 1.8 %collective-permute-start.16 = (bf16[64,2048]{1,0:T(8,128)(2,1)S(1)}, bf16[64,2048]{1,0:T(8,128)(2,1)S(1)}, u32[]{:S(2)}, u32[]{:S(2)}) collective-permute-start(bf16[64,2048]{1,0:T(8,128)(2,1)S(1)} %shard_map.49), channel_id=1, source_target_pairs={{8,0},{12,4},{0,8},{4,12},{24,16},{28,20},{16,24},{20,28},{9,1},{1... | collective-permute-start | bytes 786440 | tf_op jit(solution)/shard_map/ppermute | solution.py:244
  32.2 0.0 collective-permute-done.5
  32.3 2.7 %collective-permute-start.7 = (f32[2,1,80,128]{3,2,0,1:T(8,128)S(1)}, f32[2,1,80,128]{3,2,0,1:T(8,128)S(1)}, u32[]{:S(2)}, u32[]{:S(2)}) collective-permute-start(f32[2,1,80,128]{3,2,0,1:T(8,128)S(1)} %bitcast.41), channel_id=1, source_target_pairs={{2,0},{3,1},{0,2},{1,3},{6,4},{7,5},{4,6},{5,7},{10,8},{11,9},{8,1... | collective-permute-start | bytes 245768 | tf_op jit(solution)/shard_map/ppermute | solution.py:247
  34.9 0.0 collective-permute-done.8.refs_0_
  34.9 1.7 %shard_map.44 = (f32[2,2,80,128]{3,2,1,0:T(8,128)S(1)}, f32[2,2,80,128]{3,2,1,0:T(8,128)S(1)}) custom-call(bf16[640,2048]{1,0:T(8,128)(2,1)S(1)} %get-tuple-element.47.a_ref, bf16[640,2048]{1,0:T(8,128)(2,1)S(1)} %collective-permute-done.2.sib_ref, bf16[64,2048]{1,0:T(8,128)(2,1)S(1)} %collective-permute-done.8.refs_0_, ...), custom_call_target="tpu_custom_call" | custom-call | tf_op jit(solution)/shard_map/pallas_call | solution.py:220
  36.6 1.7 %collective-permute-start.10 = (f32[2,2,80,128]{3,2,1,0:T(8,128)S(1)}, f32[2,2,80,128]{3,2,1,0:T(8,128)S(1)}, u32[]{:S(2)}, u32[]{:S(2)}) collective-permute-start(f32[2,2,80,128]{3,2,1,0:T(8,128)S(1)} %get-tuple-element.60), channel_id=1, source_target_pairs={{1,0},{0,1},{3,2},{2,3},{5,4},{4,5},{7,6},{6,7},{9,8},{8,9},{11,10... | collective-permute-start | bytes 491528 | tf_op jit(solution)/shard_map/ppermute | solution.py:247
  38.3 0.2 collective-permute-done.7
  38.5 1.8 %shard_map.46 = (f32[2,2,80,128]{3,2,1,0:T(8,128)S(1)}, f32[2,2,80,128]{3,2,1,0:T(8,128)S(1)}) custom-call(bf16[640,2048]{1,0:T(8,128)(2,1)S(1)} %get-tuple-element.47.a_ref, bf16[640,2048]{1,0:T(8,128)(2,1)S(1)} %collective-permute-done.2.sib_ref, bf16[64,2048]{1,0:T(8,128)(2,1)S(1)} %collective-permute-done.12.refs_0_.four_ref, ...), custom_call_target="tpu_custom_call" | custom-call | tf_op jit(solution)/shard_map/pallas_call | solution.py:220
  40.3 0.0 copy-start.1
  40.3 1.4 %collective-permute-start.13 = (f32[2,2,80,128]{3,2,1,0:T(8,128)S(1)}, f32[2,2,80,128]{3,2,1,0:T(8,128)S(1)}, u32[]{:S(2)}, u32[]{:S(2)}) collective-permute-start(f32[2,2,80,128]{3,2,1,0:T(8,128)S(1)} %get-tuple-element.68), channel_id=1, source_target_pairs={{1,0},{0,1},{3,2},{2,3},{5,4},{4,5},{7,6},{6,7},{9,8},{8,9},{11,10... | collective-permute-start | bytes 491528 | tf_op jit(solution)/shard_map/ppermute | solution.py:247
  41.7 0.0 collective-permute-done.15.refs_0_
  41.7 0.0 collective-permute-done.16.refs_1_
  41.7 1.7 %shard_map.50 = (f32[2,2,80,128]{3,2,1,0:T(8,128)S(1)}, f32[2,2,80,128]{3,2,1,0:T(8,128)S(1)}) custom-call(bf16[640,2048]{1,0:T(8,128)(2,1)S(1)} %get-tuple-element.47.a_ref, bf16[640,2048]{1,0:T(8,128)(2,1)S(1)} %collective-permute-done.2.sib_ref, bf16[64,2048]{1,0:T(8,128)(2,1)S(1)} %collective-permute-done.15.refs_0_, ...), custom_call_target="tpu_custom_call" | custom-call | tf_op jit(solution)/shard_map/pallas_call | solution.py:220
  43.4 0.8 %collective-permute-start.17 = (f32[2,2,80,128]{3,2,1,0:T(8,128)S(1)}, f32[2,2,80,128]{3,2,1,0:T(8,128)S(1)}, u32[]{:S(2)}, u32[]{:S(2)}) collective-permute-start(f32[2,2,80,128]{3,2,1,0:T(8,128)S(1)} %get-tuple-element.74), channel_id=1, source_target_pairs={{1,0},{0,1},{3,2},{2,3},{5,4},{4,5},{7,6},{6,7},{9,8},{8,9},{11,10... | collective-permute-start | bytes 491528 | tf_op jit(solution)/shard_map/ppermute | solution.py:247
  44.1 0.0 collective-permute-done.10
  44.1 2.5 %collective-permute-start.11 = (f32[2,1,80,128]{3,2,0,1:T(8,128)S(1)}, f32[2,1,80,128]{3,2,0,1:T(8,128)S(1)}, u32[]{:S(2)}, u32[]{:S(2)}) collective-permute-start(f32[2,1,80,128]{3,2,0,1:T(8,128)S(1)} %bitcast.38), channel_id=1, source_target_pairs={{2,0},{3,1},{0,2},{1,3},{6,4},{7,5},{4,6},{5,7},{10,8},{11,9},{8,1... | collective-permute-start | bytes 245768 | tf_op jit(solution)/shard_map/ppermute | solution.py:247
  46.6 1.5 %collective-permute-done.13 = f32[2,2,80,128]{3,2,1,0:T(8,128)S(1)} collective-permute-done((f32[2,2,80,128]{3,2,1,0:T(8,128)S(1)}, f32[2,2,80,128]{3,2,1,0:T(8,128)S(1)}, u32[]{:S(2)}, u32[]{:S(2)}) %collective-permute-start.13) | collective-permute-done | bytes 163872 | tf_op jit(solution)/shard_map/ppermute | solution.py:247
  48.1 2.8 %collective-permute-start.14 = (f32[2,1,80,128]{3,2,0,1:T(8,128)S(1)}, f32[2,1,80,128]{3,2,0,1:T(8,128)S(1)}, u32[]{:S(2)}, u32[]{:S(2)}) collective-permute-start(f32[2,1,80,128]{3,2,0,1:T(8,128)S(1)} %bitcast.39), channel_id=1, source_target_pairs={{2,0},{3,1},{0,2},{1,3},{6,4},{7,5},{4,6},{5,7},{10,8},{11,9},{8,1... | collective-permute-start | bytes 245768 | tf_op jit(solution)/shard_map/ppermute | solution.py:247
  50.9 0.6 collective-permute-done.17
  51.5 2.0 %collective-permute-start.18 = (f32[2,1,80,128]{3,2,0,1:T(8,128)S(1)}, f32[2,1,80,128]{3,2,0,1:T(8,128)S(1)}, u32[]{:S(2)}, u32[]{:S(2)}) collective-permute-start(f32[2,1,80,128]{3,2,0,1:T(8,128)S(1)} %bitcast.40), channel_id=1, source_target_pairs={{2,0},{3,1},{0,2},{1,3},{6,4},{7,5},{4,6},{5,7},{10,8},{11,9},{8,1... | collective-permute-start | bytes 245768 | tf_op jit(solution)/shard_map/ppermute | solution.py:247
  53.5 0.0 collective-permute-done.11
  53.5 3.0 %collective-permute-done.14 = f32[2,1,80,128]{3,2,0,1:T(8,128)S(1)} collective-permute-done((f32[2,1,80,128]{3,2,0,1:T(8,128)S(1)}, f32[2,1,80,128]{3,2,0,1:T(8,128)S(1)}, u32[]{:S(2)}, u32[]{:S(2)}) %collective-permute-start.14) | collective-permute-done | bytes 81952 | tf_op jit(solution)/shard_map/ppermute | solution.py:247
  56.5 0.1 collective-permute-start.19
  56.6 0.8 %collective-permute-done.18 = f32[2,1,80,128]{3,2,0,1:T(8,128)S(1)} collective-permute-done((f32[2,1,80,128]{3,2,0,1:T(8,128)S(1)}, f32[2,1,80,128]{3,2,0,1:T(8,128)S(1)}, u32[]{:S(2)}, u32[]{:S(2)}) %collective-permute-start.18) | collective-permute-done | bytes 81952 | tf_op jit(solution)/shard_map/ppermute | solution.py:247
  57.4 0.0 collective-permute-start.20
  57.4 0.5 collective-permute-done.19.refs_10_
  57.9 0.7 %collective-permute-done.20.refs_11_ = f32[1,80,128]{2,1,0:T(8,128)S(1)} collective-permute-done((f32[1,80,128]{2,1,0:T(8,128)S(1)}, f32[1,80,128]{2,1,0:T(8,128)S(1)}, u32[]{:S(2)}, u32[]{:S(2)}) %collective-permute-start.20) | collective-permute-done | bytes 40992 | tf_op jit(solution)/shard_map/ppermute | solution.py:244
  58.6 0.0 copy-done.1
  58.6 1.4 %shard_map.54 = f32[800,128]{1,0:T(8,128)} custom-call(s32[1,5]{1,0:T(1,128)S(1)} %copy-done.1, f32[80,256]{1,0:T(8,128)S(1)} %bitcast.36, f32[80,256]{1,0:T(8,128)S(1)} %bitcast.37, f32[2,80,128]{2,1,0:T(8,128)S(1)} %get-tuple-element.52.refs_0_.refs_2_, f32[2,80,128]{2,1,0:T(8,128)S(1)} %bitcast.21, f32[2,80,128]{2,1,0:T(8,128)S(1)} %get-tuple-element.61.refs_2_.refs_4_, ...), custom_call_target="tpu_custom_call" | custom-call | tf_op jit(solution)/shard_map/pallas_call | solution.py:220
  (11 shorter events, 0.2 us)
Async XLA Ops:
  0.0 2.1 %copy-start = (bf16[64,5,1,2,2048]{4,3,2,1,0:T(2,128)(2,1)S(1)}, bf16[64,5,1,2,2048]{4,3,2,1,0:T(2,128)(2,1)}, u32[]{:S(2)}) copy-start(bf16[64,5,1,2,2048]{4,3,2,1,0:T(2,128)(2,1)} %x_ref.1) | copy-start | bytes 7864324
  3.5 13.8 %collective-permute-start.2 = (bf16[640,2048]{1,0:T(8,128)(2,1)S(1)}, bf16[640,2048]{1,0:T(8,128)(2,1)S(1)}, u32[]{:S(2)}, u32[]{:S(2)}) collective-permute-start(bf16[640,2048]{1,0:T(8,128)(2,1)S(1)} %get-tuple-element.47.a_ref), channel_id=1, source_target_pairs={{4,0},{0,4},{12,8},{8,12},{20,16},{16,20},{28,24},{24,28},{5,1},{1... | collective-permute-start | bytes 7864328 | tf_op jit(solution)/shard_map/ppermute | solution.py:244
  4.1 9.7 %collective-permute-start.4 = (bf16[64,2048]{1,0:T(8,128)(2,1)S(1)}, bf16[64,2048]{1,0:T(8,128)(2,1)S(1)}, u32[]{:S(2)}, u32[]{:S(2)}) collective-permute-start(bf16[64,2048]{1,0:T(8,128)(2,1)S(1)} %get-tuple-element.49.refs_3_.own_ref), channel_id=1, source_target_pairs={{16,0},{20,4},{24,8},{28,12},{0,16},{4,20},{8,24},{12,28},{17,1},{... | collective-permute-start | bytes 786440 | tf_op jit(solution)/shard_map/ppermute | solution.py:284
  6.7 6.3 %collective-permute-start = (f32[2,80,256]{2,1,0:T(8,128)S(1)}, f32[2,80,256]{2,1,0:T(8,128)S(1)}, u32[]{:S(2)}, u32[]{:S(2)}) collective-permute-start(f32[2,80,256]{2,1,0:T(8,128)S(1)} %get-tuple-element.44), channel_id=1, source_target_pairs={{1,0},{0,1},{3,2},{2,3},{5,4},{4,5},{7,6},{6,7},{9,8},{8,9},{11,10... | collective-permute-start | bytes 491528 | tf_op jit(solution)/shard_map/ppermute | solution.py:247
  8.2 12.2 %collective-permute-start.3 = (bf16[64,2048]{1,0:T(8,128)(2,1)S(1)}, bf16[64,2048]{1,0:T(8,128)(2,1)S(1)}, u32[]{:S(2)}, u32[]{:S(2)}) collective-permute-start(bf16[64,2048]{1,0:T(8,128)(2,1)S(1)} %get-tuple-element.55.refs_2_.own_ref), channel_id=1, source_target_pairs={{16,0},{20,4},{24,8},{28,12},{0,16},{4,20},{8,24},{12,28},{17,1},{... | collective-permute-start | bytes 786440 | tf_op jit(solution)/shard_map/ppermute | solution.py:284
  13.8 11.1 %collective-permute-start.6 = (bf16[64,2048]{1,0:T(8,128)(2,1)S(1)}, bf16[64,2048]{1,0:T(8,128)(2,1)S(1)}, u32[]{:S(2)}, u32[]{:S(2)}) collective-permute-start(bf16[64,2048]{1,0:T(8,128)(2,1)S(1)} %shard_map.42), channel_id=1, source_target_pairs={{8,0},{12,4},{0,8},{4,12},{24,16},{28,20},{16,24},{20,28},{9,1},{1... | collective-permute-start | bytes 786440 | tf_op jit(solution)/shard_map/ppermute | solution.py:244
  15.8 9.2 %collective-permute-start.12 = (bf16[64,2048]{1,0:T(8,128)(2,1)S(1)}, bf16[64,2048]{1,0:T(8,128)(2,1)S(1)}, u32[]{:S(2)}, u32[]{:S(2)}) collective-permute-start(bf16[64,2048]{1,0:T(8,128)(2,1)S(1)} %get-tuple-element.71.refs_2_.own_ref), channel_id=1, source_target_pairs={{16,0},{20,4},{24,8},{28,12},{0,16},{4,20},{8,24},{12,28},{17,1},{... | collective-permute-start | bytes 786440 | tf_op jit(solution)/shard_map/ppermute | solution.py:284
  17.4 13.1 %collective-permute-start.9 = (bf16[64,2048]{1,0:T(8,128)(2,1)S(1)}, bf16[64,2048]{1,0:T(8,128)(2,1)S(1)}, u32[]{:S(2)}, u32[]{:S(2)}) collective-permute-start(bf16[64,2048]{1,0:T(8,128)(2,1)S(1)} %get-tuple-element.72.refs_3_.own_ref), channel_id=1, source_target_pairs={{16,0},{20,4},{24,8},{28,12},{0,16},{4,20},{8,24},{12,28},{17,1},{... | collective-permute-start | bytes 786440 | tf_op jit(solution)/shard_map/ppermute | solution.py:284
  17.9 5.4 %collective-permute-start.1 = (f32[1,80,256]{2,1,0:T(8,128)S(1)}, f32[1,80,256]{2,1,0:T(8,128)S(1)}, u32[]{:S(2)}, u32[]{:S(2)}) collective-permute-start(f32[1,80,256]{2,1,0:T(8,128)S(1)} %get-tuple-element.46), channel_id=1, source_target_pairs={{2,0},{3,1},{0,2},{1,3},{6,4},{7,5},{4,6},{5,7},{10,8},{11,9},{8,1... | collective-permute-start | bytes 245768 | tf_op jit(solution)/shard_map/ppermute | solution.py:247
  20.5 14.4 %collective-permute-start.8 = (bf16[64,2048]{1,0:T(8,128)(2,1)S(1)}, bf16[64,2048]{1,0:T(8,128)(2,1)S(1)}, u32[]{:S(2)}, u32[]{:S(2)}) collective-permute-start(bf16[64,2048]{1,0:T(8,128)(2,1)S(1)} %shard_map.43), channel_id=1, source_target_pairs={{8,0},{12,4},{0,8},{4,12},{24,16},{28,20},{16,24},{20,28},{9,1},{1... | collective-permute-start | bytes 786440 | tf_op jit(solution)/shard_map/ppermute | solution.py:244
  23.3 9.0 %collective-permute-start.5 = (f32[2,2,80,128]{3,2,1,0:T(8,128)S(1)}, f32[2,2,80,128]{3,2,1,0:T(8,128)S(1)}, u32[]{:S(2)}, u32[]{:S(2)}) collective-permute-start(f32[2,2,80,128]{3,2,1,0:T(8,128)S(1)} %get-tuple-element.51), channel_id=1, source_target_pairs={{1,0},{0,1},{3,2},{2,3},{5,4},{4,5},{7,6},{6,7},{9,8},{8,9},{11,10... | collective-permute-start | bytes 491528 | tf_op jit(solution)/shard_map/ppermute | solution.py:247
  25.1 16.6 %collective-permute-start.15 = (bf16[64,2048]{1,0:T(8,128)(2,1)S(1)}, bf16[64,2048]{1,0:T(8,128)(2,1)S(1)}, u32[]{:S(2)}, u32[]{:S(2)}) collective-permute-start(bf16[64,2048]{1,0:T(8,128)(2,1)S(1)} %shard_map.48), channel_id=1, source_target_pairs={{8,0},{12,4},{0,8},{4,12},{24,16},{28,20},{16,24},{20,28},{9,1},{1... | collective-permute-start | bytes 786440 | tf_op jit(solution)/shard_map/ppermute | solution.py:244
  30.4 11.2 %collective-permute-start.16 = (bf16[64,2048]{1,0:T(8,128)(2,1)S(1)}, bf16[64,2048]{1,0:T(8,128)(2,1)S(1)}, u32[]{:S(2)}, u32[]{:S(2)}) collective-permute-start(bf16[64,2048]{1,0:T(8,128)(2,1)S(1)} %shard_map.49), channel_id=1, source_target_pairs={{8,0},{12,4},{0,8},{4,12},{24,16},{28,20},{16,24},{20,28},{9,1},{1... | collective-permute-start | bytes 786440 | tf_op jit(solution)/shard_map/ppermute | solution.py:244
  32.3 6.2 %collective-permute-start.7 = (f32[2,1,80,128]{3,2,0,1:T(8,128)S(1)}, f32[2,1,80,128]{3,2,0,1:T(8,128)S(1)}, u32[]{:S(2)}, u32[]{:S(2)}) collective-permute-start(f32[2,1,80,128]{3,2,0,1:T(8,128)S(1)} %bitcast.41), channel_id=1, source_target_pairs={{2,0},{3,1},{0,2},{1,3},{6,4},{7,5},{4,6},{5,7},{10,8},{11,9},{8,1... | collective-permute-start | bytes 245768 | tf_op jit(solution)/shard_map/ppermute | solution.py:247
  36.6 7.5 %collective-permute-start.10 = (f32[2,2,80,128]{3,2,1,0:T(8,128)S(1)}, f32[2,2,80,128]{3,2,1,0:T(8,128)S(1)}, u32[]{:S(2)}, u32[]{:S(2)}) collective-permute-start(f32[2,2,80,128]{3,2,1,0:T(8,128)S(1)} %get-tuple-element.60), channel_id=1, source_target_pairs={{1,0},{0,1},{3,2},{2,3},{5,4},{4,5},{7,6},{6,7},{9,8},{8,9},{11,10... | collective-permute-start | bytes 491528 | tf_op jit(solution)/shard_map/ppermute | solution.py:247
  40.3 18.3 %copy-start.1 = (s32[1,5]{1,0:T(1,128)S(1)}, s32[1,5]{1,0:T(1,128)}, u32[]{:S(2)}) copy-start(s32[1,5]{1,0:T(1,128)} %live_ref.1) | copy-start | bytes 64
  40.3 7.9 %collective-permute-start.13 = (f32[2,2,80,128]{3,2,1,0:T(8,128)S(1)}, f32[2,2,80,128]{3,2,1,0:T(8,128)S(1)}, u32[]{:S(2)}, u32[]{:S(2)}) collective-permute-start(f32[2,2,80,128]{3,2,1,0:T(8,128)S(1)} %get-tuple-element.68), channel_id=1, source_target_pairs={{1,0},{0,1},{3,2},{2,3},{5,4},{4,5},{7,6},{6,7},{9,8},{8,9},{11,10... | collective-permute-start | bytes 491528 | tf_op jit(solution)/shard_map/ppermute | solution.py:247
  43.4 8.1 %collective-permute-start.17 = (f32[2,2,80,128]{3,2,1,0:T(8,128)S(1)}, f32[2,2,80,128]{3,2,1,0:T(8,128)S(1)}, u32[]{:S(2)}, u32[]{:S(2)}) collective-permute-start(f32[2,2,80,128]{3,2,1,0:T(8,128)S(1)} %get-tuple-element.74), channel_id=1, source_target_pairs={{1,0},{0,1},{3,2},{2,3},{5,4},{4,5},{7,6},{6,7},{9,8},{8,9},{11,10... | collective-permute-start | bytes 491528 | tf_op jit(solution)/shard_map/ppermute | solution.py:247
  44.1 9.4 %collective-permute-start.11 = (f32[2,1,80,128]{3,2,0,1:T(8,128)S(1)}, f32[2,1,80,128]{3,2,0,1:T(8,128)S(1)}, u32[]{:S(2)}, u32[]{:S(2)}) collective-permute-start(f32[2,1,80,128]{3,2,0,1:T(8,128)S(1)} %bitcast.38), channel_id=1, source_target_pairs={{2,0},{3,1},{0,2},{1,3},{6,4},{7,5},{4,6},{5,7},{10,8},{11,9},{8,1... | collective-permute-start | bytes 245768 | tf_op jit(solution)/shard_map/ppermute | solution.py:247
  48.1 8.3 %collective-permute-start.14 = (f32[2,1,80,128]{3,2,0,1:T(8,128)S(1)}, f32[2,1,80,128]{3,2,0,1:T(8,128)S(1)}, u32[]{:S(2)}, u32[]{:S(2)}) collective-permute-start(f32[2,1,80,128]{3,2,0,1:T(8,128)S(1)} %bitcast.39), channel_id=1, source_target_pairs={{2,0},{3,1},{0,2},{1,3},{6,4},{7,5},{4,6},{5,7},{10,8},{11,9},{8,1... | collective-permute-start | bytes 245768 | tf_op jit(solution)/shard_map/ppermute | solution.py:247
  51.5 5.8 %collective-permute-start.18 = (f32[2,1,80,128]{3,2,0,1:T(8,128)S(1)}, f32[2,1,80,128]{3,2,0,1:T(8,128)S(1)}, u32[]{:S(2)}, u32[]{:S(2)}) collective-permute-start(f32[2,1,80,128]{3,2,0,1:T(8,128)S(1)} %bitcast.40), channel_id=1, source_target_pairs={{2,0},{3,1},{0,2},{1,3},{6,4},{7,5},{4,6},{5,7},{10,8},{11,9},{8,1... | collective-permute-start | bytes 245768 | tf_op jit(solution)/shard_map/ppermute | solution.py:247
  56.5 1.4 %collective-permute-start.19 = (f32[3,80,128]{2,1,0:T(8,128)S(1)}, f32[3,80,128]{2,1,0:T(8,128)S(1)}, u32[]{:S(2)}, u32[]{:S(2)}) collective-permute-start(f32[3,80,128]{2,1,0:T(8,128)S(1)} %shard_map.52), channel_id=1, source_target_pairs={{4,0},{0,4},{12,8},{8,12},{20,16},{16,20},{28,24},{24,28},{5,1},{1... | collective-permute-start | bytes 368648 | tf_op jit(solution)/shard_map/ppermute | solution.py:244
  57.4 1.2 %collective-permute-start.20 = (f32[1,80,128]{2,1,0:T(8,128)S(1)}, f32[1,80,128]{2,1,0:T(8,128)S(1)}, u32[]{:S(2)}, u32[]{:S(2)}) collective-permute-start(f32[1,80,128]{2,1,0:T(8,128)S(1)} %shard_map.53), channel_id=1, source_target_pairs={{4,0},{0,4},{12,8},{8,12},{20,16},{16,20},{28,24},{24,28},{5,1},{1... | collective-permute-start | bytes 122888 | tf_op jit(solution)/shard_map/ppermute | solution.py:244

commit v4 on v3

--- a/solution.py
+++ b/solution.py
@@ -10,6 +10,7 @@
 
 PAIRS = 5
 CHUNKS = 4
+STEPS = 5
 ORDER = ("F0", "F1", "U", "F2", "F3", "X0", "X1", "F0F1", "X2", "X0X1", "X3", "F2F3", "X2X3")
 TIES = {
     "F0F1b": ("X1",),
@@ -17,13 +18,12 @@
     "F2F3": ("F0F1b",),
     "F3": ("F1", "S"),
     "X0": ("S", "Ua"),
-    "X0X1": ("F0F1k", "F3", "Ub"),
+    "X0X1": ("F0F1k", "F2", "Ub"),
     "X0X1b": ("F3",),
     "X2": ("F0F1k",),
     "X2X3": ("X0X1a",),
-    "X3": ("F0F1a", "Ub", "X1"),
+    "X3": ("F0F1a", "Ub", "X0X1k"),
 }
-COST = None
 LANES = 128
 VMEM = pl.BlockSpec(memory_space=pltpu.VMEM)
 HBM = pl.BlockSpec(memory_space=pltpu.HBM)
@@ -42,33 +42,6 @@
 
 def dot_t(a, b):
     return lax.dot_general(a, b, (((1,), (1,)), ((), ())), preferred_element_type=F32)
-
-
-def extract_kernel(x_hbm, valid_hbm, full_ref, row_ref, *rest):
-    *chunk_refs, buf, valid_buf, sems = rest
-    copy = pltpu.make_async_copy(x_hbm.at[:, 2:4], buf, sems.at[0])
-    copy.start()
-    small = pltpu.make_async_copy(valid_hbm, valid_buf, sems.at[1])
-    small.start()
-    block = buf.shape[0]
-    rows = 4 * block
-    half = rows // 2
-    spread = (iota((block, rows), 1) // 4 == iota((block, rows), 0)).astype(BF16)
-    to, frm = iota((rows, rows), 0), iota((rows, rows), 1)
-    source = jnp.where(to < half, 2 * to, 2 * (to - half) + 1)
-    small.wait()
-    valid = jnp.broadcast_to(valid_buf[...], row_ref.shape).astype(F32).astype(BF16)
-    row_ref[...] = valid
-    valid = jnp.dot(valid, spread, preferred_element_type=F32)[:1]
-    pick = jnp.where(frm == source, jnp.broadcast_to(valid, (rows, rows)), 0.0).astype(BF16)
-    copy.wait()
-    full = jnp.dot(pick, buf[...].reshape(rows, buf.shape[-1]), preferred_element_type=F32).astype(BF16)
-    full_ref[...] = full
-    width = half // CHUNKS
-    for k, chunk_ref in enumerate(chunk_refs):
-        for part in range(2):
-            at = part * half + k * width
-            chunk_ref[part * width : (part + 1) * width] = full[at : at + width]
 
 
 def store_tiles(g_ref, value):
@@ -96,13 +69,45 @@
         )
 
 
-def own_kernel(members, x_ref, valid_ref, full_ref, a_ref, keep_ref, send_ref, g_ref):
-    block = x_ref.shape[0]
-    rows = a_ref.shape[0]
-    pick = (iota((rows, block), 0) // (rows // block) == iota((rows, block), 1)).astype(BF16)
-    valid = dot_t(pick, valid_ref[...])[:, :1].astype(BF16)
-    a_ref[...] = x_ref[...].reshape(a_ref.shape) * valid
-    store_tiles(g_ref, dot_t(a_ref[...], full_ref[...]))
+def first_kernel(members, x_hbm, valid_hbm, *refs):
+    row_ref, *chunk_refs, a_ref, keep_ref, send_ref, buf, valid_buf, b_ref, g_ref, sems = refs
+    copies = [
+        pltpu.make_async_copy(valid_hbm, valid_buf, sems.at[0]),
+        pltpu.make_async_copy(x_hbm.at[:, 2:4], buf.at[:, 2:4], sems.at[1]),
+        pltpu.make_async_copy(x_hbm.at[:, :2], buf.at[:, :2], sems.at[2]),
+        pltpu.make_async_copy(x_hbm.at[:, 4:], buf.at[:, 4:], sems.at[3]),
+    ]
+    for copy in copies:
+        copy.start()
+    block = buf.shape[0]
+    stations = block // len(chunk_refs)
+    rows = 4 * stations
+    half = rows // 2
+    station, lane = iota((block, rows), 0), iota((block, rows), 1)
+    to, frm = iota((rows, rows), 0), iota((rows, rows), 1)
+    source = jnp.where(to < half, 2 * to, 2 * (to - half) + 1)
+    copies[0].wait()
+    valid = jnp.broadcast_to(valid_buf[...], row_ref.shape).astype(F32).astype(BF16)
+    row_ref[...] = valid
+    picks = []
+    for k in range(len(chunk_refs)):
+        spread = (lane // 4 + k * stations == station).astype(BF16)
+        mask = jnp.dot(valid, spread, preferred_element_type=F32)[:1]
+        picks.append(jnp.where(frm == source, jnp.broadcast_to(mask, (rows, rows)), 0.0).astype(BF16))
+    pick = (iota((a_ref.shape[0], block), 0) // (a_ref.shape[0] // block) == iota((a_ref.shape[0], block), 1)).astype(BF16)
+    mask = dot_t(pick, valid)[:, :1].astype(BF16)
+    copies[1].wait()
+    for k, chunk_ref in enumerate(chunk_refs):
+        some = buf[k * stations : (k + 1) * stations, 2:4].reshape(rows, buf.shape[-1])
+        chunk = jnp.dot(picks[k], some, preferred_element_type=F32).astype(BF16)
+        chunk_ref[...] = chunk
+        for part in range(2):
+            at = part * b_ref.shape[0] // 2 + k * half
+            b_ref[at : at + half] = chunk[part * half : (part + 1) * half]
+    copies[2].wait()
+    copies[3].wait()
+    a_ref[...] = buf[...].reshape(a_ref.shape) * mask
+    store_tiles(g_ref, dot_t(a_ref[...], b_ref[...]))
 
     def finish(even, odd, out, slot):
         out[slot, :, :LANES] = even[0] + odd[1]
@@ -170,38 +175,48 @@
 
 
 def final_kernel(factor, units, live_ref, *refs):
-    own_keep_ref, own_got_ref, *in_refs, early_ref, late_ref, out_ref = refs
-    own = own_keep_ref[...] + own_got_ref[...]
-    second = jnp.broadcast_to(lax.axis_index("stn") & 1, own[:, :LANES].shape) == 1
-    theirs = [r[i] for r in (early_ref, late_ref) for i in range(r.shape[0])]
+    own_keep_ref, own_got_ref, *in_refs, early_ref, late_ref, out_hbm, out_ref, sems = refs
+    places = [(r, i) for r in (early_ref, late_ref) for i in range(r.shape[0])]
     width = LANES // CHUNKS
-    columns = {}
-    for u, unit in enumerate(units):
-        tiles = in_refs[2 * u].shape[0]
-        mine = in_refs[2 * u][0] + in_refs[2 * u + 1][0]
-        for i, (kind, k) in enumerate(unit):
-            for part in range(2):
-                at = (part * len(unit) + i) * width
-                columns[kind, k, part] = mine[:, at : at + width]
-                at += LANES // 2 if tiles == 1 else 0
-                columns[kind + "s", k, part] = theirs[u][:, at : at + width]
-    rows = out_ref.shape[0] // (2 * PAIRS)
-
-    def joined(kind, part):
-        return jnp.concatenate([columns[kind, k, part] for k in range(CHUNKS)], axis=1)
-
-    for part in range(2):
-        four, two = joined("Fs", part), joined("Xs", part)
-        values = [
-            own[:, part * LANES : (part + 1) * LANES],
-            jnp.where(second, four, two),
-            joined("X", part),
-            jnp.where(second, two, four),
-            joined("F", part),
-        ]
-        for offset, value in enumerate(values):
-            scale = live_ref[0, offset].astype(F32) * factor
-            out_ref[pl.ds(2 * offset + part, rows, stride=2 * PAIRS), :] = value * scale
+    steps = sems.shape[0]
+    rows = out_ref.shape[0] // (2 * PAIRS * steps)
+    copies = []
+    for step in range(steps):
+        some = pl.ds(step * rows, rows)
+        own = own_keep_ref[some, :] + own_got_ref[some, :]
+        second = jnp.broadcast_to(lax.axis_index("stn") & 1, own[:, :LANES].shape) == 1
+        columns = {}
+        for u, unit in enumerate(units):
+            tiles = in_refs[2 * u].shape[0]
+            mine = in_refs[2 * u][0, some, :] + in_refs[2 * u + 1][0, some, :]
+            theirs = places[u][0][places[u][1], some, :]
+            for i, (kind, k) in enumerate(unit):
+                for part in range(2):
+                    at = (part * len(unit) + i) * width
+                    columns[kind, k, part] = mine[:, at : at + width]
+                    at += LANES // 2 if tiles == 1 else 0
+                    columns[kind + "s", k, part] = theirs[:, at : at + width]
+        for part in range(2):
+            four, two, mine_two, mine_four = (
+                jnp.concatenate([columns[kind, k, part] for k in range(CHUNKS)], axis=1)
+                for kind in ("Fs", "Xs", "X", "F")
+            )
+            values = [
+                own[:, part * LANES : (part + 1) * LANES],
+                jnp.where(second, four, two),
+                mine_two,
+                jnp.where(second, two, four),
+                mine_four,
+            ]
+            for offset, value in enumerate(values):
+                scale = live_ref[0, offset].astype(F32) * factor
+                to = step * rows * 2 * PAIRS + 2 * offset + part
+                out_ref[pl.ds(to, rows, stride=2 * PAIRS), :] = value * scale
+        slab = pl.ds(step * rows * 2 * PAIRS, rows * 2 * PAIRS)
+        copies.append(pltpu.make_async_copy(out_ref.at[slab], out_hbm.at[slab], sems.at[step]))
+        copies[-1].start()
+    for copy in copies:
+        copy.wait()
 
 
 def tie(values, *others):
@@ -216,26 +231,30 @@
     width = 2 * block // CHUNKS
     ids = range(blocks)
 
-    def call(kernel, outs, operands, mib, scratch=(), specs=None, cost=COST):
+    def call(kernel, outs, operands, mib, scratch=(), specs=None, out_spec=VMEM):
         return pl.pallas_call(
             kernel,
             in_specs=specs or [VMEM] * len(operands),
-            out_specs=[VMEM] * len(outs),
+            out_specs=[out_spec] * len(outs),
             out_shape=[jax.ShapeDtypeStruct(*out) for out in outs],
             scratch_shapes=list(scratch),
             compiler_params=params(mib),
-            cost_estimate=cost and pl.CostEstimate(flops=cost, bytes_accessed=cost, transcendentals=0),
         )(*operands)
 
-    full, valid, *own = call(
-        extract_kernel,
-        [((4 * block, freq), BF16), ((8, block), BF16)] + [((2 * width, freq), BF16)] * CHUNKS,
+    valid, *own, a, keep, send = call(
+        functools.partial(first_kernel, members),
+        [((8, block), BF16)]
+        + [((2 * width, freq), BF16)] * CHUNKS
+        + [((rows, freq), BF16)]
+        + [((half, per, 4 * block), F32)] * 2,
         [pltpu.with_memory_space_constraint(v, pltpu.HBM) for v in (spectra, segment_valid.reshape(1, block))],
-        12,
+        16,
         [
-            pltpu.VMEM((block, 2, 1, 2, freq), BF16),
+            pltpu.VMEM((block, channels, 1, 2, freq), BF16),
             pltpu.VMEM((1, block), jnp.int32),
-            pltpu.SemaphoreType.DMA((2,)),
+            pltpu.VMEM((4 * block, freq), BF16),
+            pltpu.VMEM((4 * block // LANES, rows, LANES), F32),
+            pltpu.SemaphoreType.DMA((4,)),
         ],
         [HBM] * 2,
     )
@@ -263,14 +282,6 @@
             distance *= 2
         return keep, send
 
-    a, keep, send = call(
-        functools.partial(own_kernel, members),
-        [((rows, freq), BF16)] + [((half, per, 4 * block), F32)] * 2,
-        [spectra, valid, full],
-        16,
-        [pltpu.VMEM((4 * block // LANES, rows, LANES), F32)],
-    )
-    sibling = exchange(a, 1)
     done = {}
 
     def after(name):
@@ -330,7 +341,12 @@
         [((2 * PAIRS * per, 2 * block), F32)],
         operands,
         12,
-        specs=[SMEM] + [VMEM] * (len(operands) - 1),
+        [
+            pltpu.VMEM((2 * PAIRS * per, 2 * block), F32),
+            pltpu.SemaphoreType.DMA((STEPS if per % (8 * STEPS) == 0 else 1,)),
+        ],
+        [SMEM] + [VMEM] * (len(operands) - 1),
+        HBM,
     )
     return out.reshape(block // members, channels, PAIRS, 2, 2 * block)
 

time: 60.2 us -> 59.8 us (level)
  starting transfers between devices: 32 us -> 34.2 us
  waiting for transfers between devices: 15.8 us -> 13.6 us
    ppermute x10, starting transfers between devices: 19.5 us -> 22 us  [halve(): got = lax.ppermute(send, 'seg', [(i ^ distance, i) for i in range(members)])]
    ppermute x4, waiting for transfers between devices: 4.36 us -> 3.09 us  [four_of(): lax.ppermute(value, 'stn', [((i - 4) % blocks, i) for i in ids])]
    ppermute x7, starting transfers between devices: 7.35 us -> 6.31 us  [exchange(): return lax.ppermute(c, 'stn', [(i ^ distance, i) for i in ids])]
    ppermute x10, waiting for transfers between devices: 10.2 us -> 9.3 us  [halve(): got = lax.ppermute(send, 'seg', [(i ^ distance, i) for i in range(members)])]
    ppermute x4, starting transfers between devices: 5.12 us -> 5.96 us  [four_of(): lax.ppermute(value, 'stn', [((i - 4) % blocks, i) for i in ids])]
    pallas_call x18 -> x17, Pallas kernels: 11.9 us -> 11.6 us  [call(): pl.pallas_call(kernel, in_specs=specs or [VMEM] * len(operands), out_spec...]
  transfers between devices with their start and end apart: 21 -> 21, of which waited for: 11 -> 9; matrix products, arithmetic and copies ran while one was open for 0% -> 0% of each run, Pallas kernels for 12% -> 12%
where the time goes in v4:
time: 59.8 us; the launch traced here: 59.6 us
  starting transfers between devices  34.2 us (57%)
  waiting for transfers between devices  13.6 us (23%)
  Pallas kernels  11.6 us (19%)
    ppermute x10, starting transfers between devices, halve(): got = lax.ppermute(send, 'seg', [(i ^ distance, i) for i in range(members)])  22 us
    pallas_call x17, Pallas kernels, call(): pl.pallas_call(kernel, in_specs=specs or [VMEM] * len(operands), out_spec...  11.6 us
    ppermute x10, waiting for transfers between devices, halve(): got = lax.ppermute(send, 'seg', [(i ^ distance, i) for i in range(members)])  9.3 us
    ppermute x7, starting transfers between devices, exchange(): return lax.ppermute(c, 'stn', [(i ^ distance, i) for i in ids])  6.31 us
    ppermute x4, starting transfers between devices, four_of(): lax.ppermute(value, 'stn', [((i - 4) % blocks, i) for i in ids])  5.96 us
    ppermute x4, waiting for transfers between devices, four_of(): lax.ppermute(value, 'stn', [((i - 4) % blocks, i) for i in ids])  3.09 us
    ppermute x7, waiting for transfers between devices, exchange(): return lax.ppermute(c, 'stn', [(i ^ distance, i) for i in ids])  1.22 us
  transfers between devices with their start and end apart: 21, of which 9 were waited for; matrix products, arithmetic and copies ran while one was open for 0% of the time, Pallas kernels for 12%

profile of v4, /device:TPU:0, one launch (start us, length us, event | category | flops | bytes accessed | tf_op | source)
XLA Modules:
  0.0 59.6 jit_solution(16014111556150459022)
XLA Ops:
  0.0 3.1 %shard_map.37 = (bf16[8,64]{1,0:T(8,128)(2,1)S(1)}, bf16[64,2048]{1,0:T(8,128)(2,1)S(1)}, bf16[64,2048]{1,0:T(8,128)(2,1)S(1)}, bf16[64,2048]{1,0:T(8,128)(2,1)S...) custom-call(bf16[64,5,1,2,2048]{4,3,2,1,0:T(2,128)(2,1)} %x_hbm.1, ...), custom_call_target="tpu_custom_call" | custom-call | tf_op jit(solution)/shard_map/pallas_call | solution.py:235
  3.1 0.5 collective-permute-start.2
  3.6 2.6 %collective-permute-start.4 = (bf16[64,2048]{1,0:T(8,128)(2,1)S(1)}, bf16[64,2048]{1,0:T(8,128)(2,1)S(1)}, u32[]{:S(2)}, u32[]{:S(2)}) collective-permute-start(bf16[64,2048]{1,0:T(8,128)(2,1)S(1)} %get-tuple-element.46.refs_3_.own_ref), channel_id=1, source_target_pairs={{16,0},{20,4},{24,8},{28,12},{0,16},{4,20},{8,24},{12,28},{17,1},{... | collective-permute-start | bytes 786440 | tf_op jit(solution)/shard_map/ppermute | solution.py:295
  6.2 0.1 collective-permute-start.3
  6.3 2.0 %collective-permute-start = (f32[2,80,256]{2,1,0:T(8,128)S(1)}, f32[2,80,256]{2,1,0:T(8,128)S(1)}, u32[]{:S(2)}, u32[]{:S(2)}) collective-permute-start(f32[2,80,256]{2,1,0:T(8,128)S(1)} %get-tuple-element.41), channel_id=1, source_target_pairs={{1,0},{0,1},{3,2},{2,3},{5,4},{4,5},{7,6},{6,7},{9,8},{8,9},{11,10... | collective-permute-start | bytes 491528 | tf_op jit(solution)/shard_map/ppermute | solution.py:266
  8.3 4.2 %collective-permute-done.got_ref = f32[2,80,256]{2,1,0:T(8,128)S(1)} collective-permute-done((f32[2,80,256]{2,1,0:T(8,128)S(1)}, f32[2,80,256]{2,1,0:T(8,128)S(1)}, u32[]{:S(2)}, u32[]{:S(2)}) %collective-permute-start) | collective-permute-done | bytes 163872 | tf_op jit(solution)/shard_map/ppermute | solution.py:266
  12.5 1.8 %collective-permute-start.9 = (bf16[64,2048]{1,0:T(8,128)(2,1)S(1)}, bf16[64,2048]{1,0:T(8,128)(2,1)S(1)}, u32[]{:S(2)}, u32[]{:S(2)}) collective-permute-start(bf16[64,2048]{1,0:T(8,128)(2,1)S(1)} %get-tuple-element.69.refs_2_.own_ref), channel_id=1, source_target_pairs={{16,0},{20,4},{24,8},{28,12},{0,16},{4,20},{8,24},{12,28},{17,1},{... | collective-permute-start | bytes 786440 | tf_op jit(solution)/shard_map/ppermute | solution.py:295
  14.3 0.0 collective-permute-done.4.refs_1_.four_ref
  14.3 1.6 %collective-permute-start.6 = (bf16[64,2048]{1,0:T(8,128)(2,1)S(1)}, bf16[64,2048]{1,0:T(8,128)(2,1)S(1)}, u32[]{:S(2)}, u32[]{:S(2)}) collective-permute-start(bf16[64,2048]{1,0:T(8,128)(2,1)S(1)} %shard_map.41), channel_id=1, source_target_pairs={{8,0},{12,4},{0,8},{4,12},{24,16},{28,20},{16,24},{20,28},{9,1},{1... | collective-permute-start | bytes 786440 | tf_op jit(solution)/shard_map/ppermute | solution.py:263
  15.9 0.0 collective-permute-done.2.sib_ref
  15.9 3.1 %collective-permute-done.3.refs_0_.four_ref = bf16[64,2048]{1,0:T(8,128)(2,1)S(1)} collective-permute-done((bf16[64,2048]{1,0:T(8,128)(2,1)S(1)}, bf16[64,2048]{1,0:T(8,128)(2,1)S(1)}, u32[]{:S(2)}, u32[]{:S(2)}) %collective-permute-start.3) | collective-permute-done | bytes 262176 | tf_op jit(solution)/shard_map/ppermute | solution.py:295
  19.0 2.0 %collective-permute-start.8 = (bf16[64,2048]{1,0:T(8,128)(2,1)S(1)}, bf16[64,2048]{1,0:T(8,128)(2,1)S(1)}, u32[]{:S(2)}, u32[]{:S(2)}) collective-permute-start(bf16[64,2048]{1,0:T(8,128)(2,1)S(1)} %shard_map.42), channel_id=1, source_target_pairs={{8,0},{12,4},{0,8},{4,12},{24,16},{28,20},{16,24},{20,28},{9,1},{1... | collective-permute-start | bytes 786440 | tf_op jit(solution)/shard_map/ppermute | solution.py:263
  21.0 1.5 %collective-permute-start.11 = (bf16[64,2048]{1,0:T(8,128)(2,1)S(1)}, bf16[64,2048]{1,0:T(8,128)(2,1)S(1)}, u32[]{:S(2)}, u32[]{:S(2)}) collective-permute-start(bf16[64,2048]{1,0:T(8,128)(2,1)S(1)} %get-tuple-element.70.refs_3_.own_ref), channel_id=1, source_target_pairs={{16,0},{20,4},{24,8},{28,12},{0,16},{4,20},{8,24},{12,28},{17,1},{... | collective-permute-start | bytes 786440 | tf_op jit(solution)/shard_map/ppermute | solution.py:295
  22.5 2.6 %collective-permute-start.1 = (f32[1,80,256]{2,1,0:T(8,128)S(1)}, f32[1,80,256]{2,1,0:T(8,128)S(1)}, u32[]{:S(2)}, u32[]{:S(2)}) collective-permute-start(f32[1,80,256]{2,1,0:T(8,128)S(1)} %get-tuple-element.43), channel_id=1, source_target_pairs={{2,0},{3,1},{0,2},{1,3},{6,4},{7,5},{4,6},{5,7},{10,8},{11,9},{8,1... | collective-permute-start | bytes 245768 | tf_op jit(solution)/shard_map/ppermute | solution.py:266
  25.1 1.8 %shard_map.39 = (f32[2,2,80,128]{3,2,1,0:T(8,128)S(1)}, f32[2,2,80,128]{3,2,1,0:T(8,128)S(1)}) custom-call(bf16[640,2048]{1,0:T(8,128)(2,1)S(1)} %get-tuple-element.44.a_ref, bf16[640,2048]{1,0:T(8,128)(2,1)S(1)} %collective-permute-done.2.sib_ref, bf16[64,2048]{1,0:T(8,128)(2,1)S(1)} %collective-permute-done.3.refs_0_.four_ref, ...), custom_call_target="tpu_custom_call" | custom-call | tf_op jit(solution)/shard_map/pallas_call | solution.py:235
  26.9 1.0 %collective-permute-done.1 = f32[1,80,256]{2,1,0:T(8,128)S(1)} collective-permute-done((f32[1,80,256]{2,1,0:T(8,128)S(1)}, f32[1,80,256]{2,1,0:T(8,128)S(1)}, u32[]{:S(2)}, u32[]{:S(2)}) %collective-permute-start.1) | collective-permute-done | bytes 81952 | tf_op jit(solution)/shard_map/ppermute | solution.py:266
  27.8 1.6 %collective-permute-start.5 = (f32[2,2,80,128]{3,2,1,0:T(8,128)S(1)}, f32[2,2,80,128]{3,2,1,0:T(8,128)S(1)}, u32[]{:S(2)}, u32[]{:S(2)}) collective-permute-start(f32[2,2,80,128]{3,2,1,0:T(8,128)S(1)} %get-tuple-element.49), channel_id=1, source_target_pairs={{1,0},{0,1},{3,2},{2,3},{5,4},{4,5},{7,6},{6,7},{9,8},{8,9},{11,10... | collective-permute-start | bytes 491528 | tf_op jit(solution)/shard_map/ppermute | solution.py:266
  29.4 0.0 collective-permute-done.9.refs_0_.four_ref
  29.4 0.6 %collective-permute-start.15 = (bf16[64,2048]{1,0:T(8,128)(2,1)S(1)}, bf16[64,2048]{1,0:T(8,128)(2,1)S(1)}, u32[]{:S(2)}, u32[]{:S(2)}) collective-permute-start(bf16[64,2048]{1,0:T(8,128)(2,1)S(1)} %shard_map.47), channel_id=1, source_target_pairs={{8,0},{12,4},{0,8},{4,12},{24,16},{28,20},{16,24},{20,28},{9,1},{1... | collective-permute-start | bytes 786440 | tf_op jit(solution)/shard_map/ppermute | solution.py:263
  30.0 0.0 collective-permute-done.6.refs_1_
  30.0 0.0 collective-permute-done.8.refs_0_
  30.1 1.7 %shard_map.43 = (f32[2,2,80,128]{3,2,1,0:T(8,128)S(1)}, f32[2,2,80,128]{3,2,1,0:T(8,128)S(1)}) custom-call(bf16[640,2048]{1,0:T(8,128)(2,1)S(1)} %get-tuple-element.44.a_ref, bf16[640,2048]{1,0:T(8,128)(2,1)S(1)} %collective-permute-done.2.sib_ref, bf16[64,2048]{1,0:T(8,128)(2,1)S(1)} %collective-permute-done.8.refs_0_, ...), custom_call_target="tpu_custom_call" | custom-call | tf_op jit(solution)/shard_map/pallas_call | solution.py:235
  31.7 0.0 collective-permute-done.11.refs_1_.four_ref
  31.8 1.6 %collective-permute-start.16 = (bf16[64,2048]{1,0:T(8,128)(2,1)S(1)}, bf16[64,2048]{1,0:T(8,128)(2,1)S(1)}, u32[]{:S(2)}, u32[]{:S(2)}) collective-permute-start(bf16[64,2048]{1,0:T(8,128)(2,1)S(1)} %shard_map.48), channel_id=1, source_target_pairs={{8,0},{12,4},{0,8},{4,12},{24,16},{28,20},{16,24},{20,28},{9,1},{1... | collective-permute-start | bytes 786440 | tf_op jit(solution)/shard_map/ppermute | solution.py:263
  33.4 0.0 collective-permute-done.5
  33.4 3.4 %collective-permute-start.7 = (f32[2,1,80,128]{3,2,0,1:T(8,128)S(1)}, f32[2,1,80,128]{3,2,0,1:T(8,128)S(1)}, u32[]{:S(2)}, u32[]{:S(2)}) collective-permute-start(f32[2,1,80,128]{3,2,0,1:T(8,128)S(1)} %bitcast.41), channel_id=1, source_target_pairs={{2,0},{3,1},{0,2},{1,3},{6,4},{7,5},{4,6},{5,7},{10,8},{11,9},{8,1... | collective-permute-start | bytes 245768 | tf_op jit(solution)/shard_map/ppermute | solution.py:266
  36.8 1.4 %collective-permute-start.10 = (f32[2,2,80,128]{3,2,1,0:T(8,128)S(1)}, f32[2,2,80,128]{3,2,1,0:T(8,128)S(1)}, u32[]{:S(2)}, u32[]{:S(2)}) collective-permute-start(f32[2,2,80,128]{3,2,1,0:T(8,128)S(1)} %get-tuple-element.58), channel_id=1, source_target_pairs={{1,0},{0,1},{3,2},{2,3},{5,4},{4,5},{7,6},{6,7},{9,8},{8,9},{11,10... | collective-permute-start | bytes 491528 | tf_op jit(solution)/shard_map/ppermute | solution.py:266
  38.2 1.0 %collective-permute-done.7 = f32[2,1,80,128]{3,2,0,1:T(8,128)S(1)} collective-permute-done((f32[2,1,80,128]{3,2,0,1:T(8,128)S(1)}, f32[2,1,80,128]{3,2,0,1:T(8,128)S(1)}, u32[]{:S(2)}, u32[]{:S(2)}) %collective-permute-start.7) | collective-permute-done | bytes 81952 | tf_op jit(solution)/shard_map/ppermute | solution.py:266
  39.2 1.8 %shard_map.45 = (f32[2,2,80,128]{3,2,1,0:T(8,128)S(1)}, f32[2,2,80,128]{3,2,1,0:T(8,128)S(1)}) custom-call(bf16[640,2048]{1,0:T(8,128)(2,1)S(1)} %get-tuple-element.44.a_ref, bf16[640,2048]{1,0:T(8,128)(2,1)S(1)} %collective-permute-done.2.sib_ref, bf16[64,2048]{1,0:T(8,128)(2,1)S(1)} %collective-permute-done.9.refs_0_.four_ref, ...), custom_call_target="tpu_custom_call" | custom-call | tf_op jit(solution)/shard_map/pallas_call | solution.py:235
  41.0 0.0 copy-start
  41.0 1.9 %collective-permute-start.13 = (f32[2,2,80,128]{3,2,1,0:T(8,128)S(1)}, f32[2,2,80,128]{3,2,1,0:T(8,128)S(1)}, u32[]{:S(2)}, u32[]{:S(2)}) collective-permute-start(f32[2,2,80,128]{3,2,1,0:T(8,128)S(1)} %get-tuple-element.66), channel_id=1, source_target_pairs={{1,0},{0,1},{3,2},{2,3},{5,4},{4,5},{7,6},{6,7},{9,8},{8,9},{11,10... | collective-permute-start | bytes 491528 | tf_op jit(solution)/shard_map/ppermute | solution.py:266
  42.9 0.0 collective-permute-done.15.refs_0_
  42.9 0.0 collective-permute-done.16.refs_1_
  42.9 1.7 %shard_map.49 = (f32[2,2,80,128]{3,2,1,0:T(8,128)S(1)}, f32[2,2,80,128]{3,2,1,0:T(8,128)S(1)}) custom-call(bf16[640,2048]{1,0:T(8,128)(2,1)S(1)} %get-tuple-element.44.a_ref, bf16[640,2048]{1,0:T(8,128)(2,1)S(1)} %collective-permute-done.2.sib_ref, bf16[64,2048]{1,0:T(8,128)(2,1)S(1)} %collective-permute-done.15.refs_0_, ...), custom_call_target="tpu_custom_call" | custom-call | tf_op jit(solution)/shard_map/pallas_call | solution.py:235
  44.6 0.3 collective-permute-start.17
  44.9 0.0 collective-permute-done.10
  44.9 3.3 %collective-permute-start.12 = (f32[2,1,80,128]{3,2,0,1:T(8,128)S(1)}, f32[2,1,80,128]{3,2,0,1:T(8,128)S(1)}, u32[]{:S(2)}, u32[]{:S(2)}) collective-permute-start(f32[2,1,80,128]{3,2,0,1:T(8,128)S(1)} %bitcast.38), channel_id=1, source_target_pairs={{2,0},{3,1},{0,2},{1,3},{6,4},{7,5},{4,6},{5,7},{10,8},{11,9},{8,1... | collective-permute-start | bytes 245768 | tf_op jit(solution)/shard_map/ppermute | solution.py:266
  48.2 0.6 collective-permute-done.13
  48.8 2.7 %collective-permute-start.14 = (f32[2,1,80,128]{3,2,0,1:T(8,128)S(1)}, f32[2,1,80,128]{3,2,0,1:T(8,128)S(1)}, u32[]{:S(2)}, u32[]{:S(2)}) collective-permute-start(f32[2,1,80,128]{3,2,0,1:T(8,128)S(1)} %bitcast.39), channel_id=1, source_target_pairs={{2,0},{3,1},{0,2},{1,3},{6,4},{7,5},{4,6},{5,7},{10,8},{11,9},{8,1... | collective-permute-start | bytes 245768 | tf_op jit(solution)/shard_map/ppermute | solution.py:266
  51.5 0.0 collective-permute-done.17
  51.6 2.8 %collective-permute-start.18 = (f32[2,1,80,128]{3,2,0,1:T(8,128)S(1)}, f32[2,1,80,128]{3,2,0,1:T(8,128)S(1)}, u32[]{:S(2)}, u32[]{:S(2)}) collective-permute-start(f32[2,1,80,128]{3,2,0,1:T(8,128)S(1)} %bitcast.40), channel_id=1, source_target_pairs={{2,0},{3,1},{0,2},{1,3},{6,4},{7,5},{4,6},{5,7},{10,8},{11,9},{8,1... | collective-permute-start | bytes 245768 | tf_op jit(solution)/shard_map/ppermute | solution.py:266
  54.4 0.0 collective-permute-done.12
  54.4 1.6 %collective-permute-done.14 = f32[2,1,80,128]{3,2,0,1:T(8,128)S(1)} collective-permute-done((f32[2,1,80,128]{3,2,0,1:T(8,128)S(1)}, f32[2,1,80,128]{3,2,0,1:T(8,128)S(1)}, u32[]{:S(2)}, u32[]{:S(2)}) %collective-permute-start.14) | collective-permute-done | bytes 81952 | tf_op jit(solution)/shard_map/ppermute | solution.py:266
  56.0 0.1 collective-permute-start.19
  56.1 0.9 %collective-permute-done.18 = f32[2,1,80,128]{3,2,0,1:T(8,128)S(1)} collective-permute-done((f32[2,1,80,128]{3,2,0,1:T(8,128)S(1)}, f32[2,1,80,128]{3,2,0,1:T(8,128)S(1)}, u32[]{:S(2)}, u32[]{:S(2)}) %collective-permute-start.18) | collective-permute-done | bytes 81952 | tf_op jit(solution)/shard_map/ppermute | solution.py:266
  57.0 0.0 collective-permute-start.20
  57.0 0.4 collective-permute-done.19.refs_10_
  57.4 0.8 %collective-permute-done.20.refs_11_ = f32[1,80,128]{2,1,0:T(8,128)S(1)} collective-permute-done((f32[1,80,128]{2,1,0:T(8,128)S(1)}, f32[1,80,128]{2,1,0:T(8,128)S(1)}, u32[]{:S(2)}, u32[]{:S(2)}) %collective-permute-start.20) | collective-permute-done | bytes 40992 | tf_op jit(solution)/shard_map/ppermute | solution.py:263
  58.2 0.0 copy-done
  58.2 1.4 %shard_map.53 = f32[800,128]{1,0:T(8,128)} custom-call(s32[1,5]{1,0:T(1,128)S(1)} %copy-done, f32[80,256]{1,0:T(8,128)S(1)} %bitcast.36, f32[80,256]{1,0:T(8,128)S(1)} %bitcast.37, f32[2,80,128]{2,1,0:T(8,128)S(1)} %get-tuple-element.50.refs_0_.refs_2_, f32[2,80,128]{2,1,0:T(8,128)S(1)} %bitcast.21, f32[2,80,128]{2,1,0:T(8,128)S(1)} %get-tuple-element.59.refs_2_.refs_4_, ...), custom_call_target="tpu_custom_call" | custom-call | tf_op jit(solution)/shard_map/pallas_call | solution.py:235
  (11 shorter events, 0.2 us)
Async XLA Ops:
  3.1 12.8 %collective-permute-start.2 = (bf16[640,2048]{1,0:T(8,128)(2,1)S(1)}, bf16[640,2048]{1,0:T(8,128)(2,1)S(1)}, u32[]{:S(2)}, u32[]{:S(2)}) collective-permute-start(bf16[640,2048]{1,0:T(8,128)(2,1)S(1)} %get-tuple-element.44.a_ref), channel_id=1, source_target_pairs={{4,0},{0,4},{12,8},{8,12},{20,16},{16,20},{28,24},{24,28},{5,1},{1... | collective-permute-start | bytes 7864328 | tf_op jit(solution)/shard_map/ppermute | solution.py:263
  3.6 10.7 %collective-permute-start.4 = (bf16[64,2048]{1,0:T(8,128)(2,1)S(1)}, bf16[64,2048]{1,0:T(8,128)(2,1)S(1)}, u32[]{:S(2)}, u32[]{:S(2)}) collective-permute-start(bf16[64,2048]{1,0:T(8,128)(2,1)S(1)} %get-tuple-element.46.refs_3_.own_ref), channel_id=1, source_target_pairs={{16,0},{20,4},{24,8},{28,12},{0,16},{4,20},{8,24},{12,28},{17,1},{... | collective-permute-start | bytes 786440 | tf_op jit(solution)/shard_map/ppermute | solution.py:295
  6.2 12.8 %collective-permute-start.3 = (bf16[64,2048]{1,0:T(8,128)(2,1)S(1)}, bf16[64,2048]{1,0:T(8,128)(2,1)S(1)}, u32[]{:S(2)}, u32[]{:S(2)}) collective-permute-start(bf16[64,2048]{1,0:T(8,128)(2,1)S(1)} %get-tuple-element.53.refs_2_.own_ref), channel_id=1, source_target_pairs={{16,0},{20,4},{24,8},{28,12},{0,16},{4,20},{8,24},{12,28},{17,1},{... | collective-permute-start | bytes 786440 | tf_op jit(solution)/shard_map/ppermute | solution.py:295
  6.3 6.2 %collective-permute-start = (f32[2,80,256]{2,1,0:T(8,128)S(1)}, f32[2,80,256]{2,1,0:T(8,128)S(1)}, u32[]{:S(2)}, u32[]{:S(2)}) collective-permute-start(f32[2,80,256]{2,1,0:T(8,128)S(1)} %get-tuple-element.41), channel_id=1, source_target_pairs={{1,0},{0,1},{3,2},{2,3},{5,4},{4,5},{7,6},{6,7},{9,8},{8,9},{11,10... | collective-permute-start | bytes 491528 | tf_op jit(solution)/shard_map/ppermute | solution.py:266
  12.5 16.9 %collective-permute-start.9 = (bf16[64,2048]{1,0:T(8,128)(2,1)S(1)}, bf16[64,2048]{1,0:T(8,128)(2,1)S(1)}, u32[]{:S(2)}, u32[]{:S(2)}) collective-permute-start(bf16[64,2048]{1,0:T(8,128)(2,1)S(1)} %get-tuple-element.69.refs_2_.own_ref), channel_id=1, source_target_pairs={{16,0},{20,4},{24,8},{28,12},{0,16},{4,20},{8,24},{12,28},{17,1},{... | collective-permute-start | bytes 786440 | tf_op jit(solution)/shard_map/ppermute | solution.py:295
  14.3 15.7 %collective-permute-start.6 = (bf16[64,2048]{1,0:T(8,128)(2,1)S(1)}, bf16[64,2048]{1,0:T(8,128)(2,1)S(1)}, u32[]{:S(2)}, u32[]{:S(2)}) collective-permute-start(bf16[64,2048]{1,0:T(8,128)(2,1)S(1)} %shard_map.41), channel_id=1, source_target_pairs={{8,0},{12,4},{0,8},{4,12},{24,16},{28,20},{16,24},{20,28},{9,1},{1... | collective-permute-start | bytes 786440 | tf_op jit(solution)/shard_map/ppermute | solution.py:263
  19.0 11.1 %collective-permute-start.8 = (bf16[64,2048]{1,0:T(8,128)(2,1)S(1)}, bf16[64,2048]{1,0:T(8,128)(2,1)S(1)}, u32[]{:S(2)}, u32[]{:S(2)}) collective-permute-start(bf16[64,2048]{1,0:T(8,128)(2,1)S(1)} %shard_map.42), channel_id=1, source_target_pairs={{8,0},{12,4},{0,8},{4,12},{24,16},{28,20},{16,24},{20,28},{9,1},{1... | collective-permute-start | bytes 786440 | tf_op jit(solution)/shard_map/ppermute | solution.py:263
  21.0 10.8 %collective-permute-start.11 = (bf16[64,2048]{1,0:T(8,128)(2,1)S(1)}, bf16[64,2048]{1,0:T(8,128)(2,1)S(1)}, u32[]{:S(2)}, u32[]{:S(2)}) collective-permute-start(bf16[64,2048]{1,0:T(8,128)(2,1)S(1)} %get-tuple-element.70.refs_3_.own_ref), channel_id=1, source_target_pairs={{16,0},{20,4},{24,8},{28,12},{0,16},{4,20},{8,24},{12,28},{17,1},{... | collective-permute-start | bytes 786440 | tf_op jit(solution)/shard_map/ppermute | solution.py:295
  22.5 5.3 %collective-permute-start.1 = (f32[1,80,256]{2,1,0:T(8,128)S(1)}, f32[1,80,256]{2,1,0:T(8,128)S(1)}, u32[]{:S(2)}, u32[]{:S(2)}) collective-permute-start(f32[1,80,256]{2,1,0:T(8,128)S(1)} %get-tuple-element.43), channel_id=1, source_target_pairs={{2,0},{3,1},{0,2},{1,3},{6,4},{7,5},{4,6},{5,7},{10,8},{11,9},{8,1... | collective-permute-start | bytes 245768 | tf_op jit(solution)/shard_map/ppermute | solution.py:266
  27.8 5.5 %collective-permute-start.5 = (f32[2,2,80,128]{3,2,1,0:T(8,128)S(1)}, f32[2,2,80,128]{3,2,1,0:T(8,128)S(1)}, u32[]{:S(2)}, u32[]{:S(2)}) collective-permute-start(f32[2,2,80,128]{3,2,1,0:T(8,128)S(1)} %get-tuple-element.49), channel_id=1, source_target_pairs={{1,0},{0,1},{3,2},{2,3},{5,4},{4,5},{7,6},{6,7},{9,8},{8,9},{11,10... | collective-permute-start | bytes 491528 | tf_op jit(solution)/shard_map/ppermute | solution.py:266
  29.4 13.5 %collective-permute-start.15 = (bf16[64,2048]{1,0:T(8,128)(2,1)S(1)}, bf16[64,2048]{1,0:T(8,128)(2,1)S(1)}, u32[]{:S(2)}, u32[]{:S(2)}) collective-permute-start(bf16[64,2048]{1,0:T(8,128)(2,1)S(1)} %shard_map.47), channel_id=1, source_target_pairs={{8,0},{12,4},{0,8},{4,12},{24,16},{28,20},{16,24},{20,28},{9,1},{1... | collective-permute-start | bytes 786440 | tf_op jit(solution)/shard_map/ppermute | solution.py:263
  31.8 11.1 %collective-permute-start.16 = (bf16[64,2048]{1,0:T(8,128)(2,1)S(1)}, bf16[64,2048]{1,0:T(8,128)(2,1)S(1)}, u32[]{:S(2)}, u32[]{:S(2)}) collective-permute-start(bf16[64,2048]{1,0:T(8,128)(2,1)S(1)} %shard_map.48), channel_id=1, source_target_pairs={{8,0},{12,4},{0,8},{4,12},{24,16},{28,20},{16,24},{20,28},{9,1},{1... | collective-permute-start | bytes 786440 | tf_op jit(solution)/shard_map/ppermute | solution.py:263
  33.4 5.8 %collective-permute-start.7 = (f32[2,1,80,128]{3,2,0,1:T(8,128)S(1)}, f32[2,1,80,128]{3,2,0,1:T(8,128)S(1)}, u32[]{:S(2)}, u32[]{:S(2)}) collective-permute-start(f32[2,1,80,128]{3,2,0,1:T(8,128)S(1)} %bitcast.41), channel_id=1, source_target_pairs={{2,0},{3,1},{0,2},{1,3},{6,4},{7,5},{4,6},{5,7},{10,8},{11,9},{8,1... | collective-permute-start | bytes 245768 | tf_op jit(solution)/shard_map/ppermute | solution.py:266
  36.8 8.1 %collective-permute-start.10 = (f32[2,2,80,128]{3,2,1,0:T(8,128)S(1)}, f32[2,2,80,128]{3,2,1,0:T(8,128)S(1)}, u32[]{:S(2)}, u32[]{:S(2)}) collective-permute-start(f32[2,2,80,128]{3,2,1,0:T(8,128)S(1)} %get-tuple-element.58), channel_id=1, source_target_pairs={{1,0},{0,1},{3,2},{2,3},{5,4},{4,5},{7,6},{6,7},{9,8},{8,9},{11,10... | collective-permute-start | bytes 491528 | tf_op jit(solution)/shard_map/ppermute | solution.py:266
  41.0 17.2 %copy-start = (s32[1,5]{1,0:T(1,128)S(1)}, s32[1,5]{1,0:T(1,128)}, u32[]{:S(2)}) copy-start(s32[1,5]{1,0:T(1,128)} %live_ref.1) | copy-start | bytes 64
  41.0 7.7 %collective-permute-start.13 = (f32[2,2,80,128]{3,2,1,0:T(8,128)S(1)}, f32[2,2,80,128]{3,2,1,0:T(8,128)S(1)}, u32[]{:S(2)}, u32[]{:S(2)}) collective-permute-start(f32[2,2,80,128]{3,2,1,0:T(8,128)S(1)} %get-tuple-element.66), channel_id=1, source_target_pairs={{1,0},{0,1},{3,2},{2,3},{5,4},{4,5},{7,6},{6,7},{9,8},{8,9},{11,10... | collective-permute-start | bytes 491528 | tf_op jit(solution)/shard_map/ppermute | solution.py:266
  44.6 7.0 %collective-permute-start.17 = (f32[2,2,80,128]{3,2,1,0:T(8,128)S(1)}, f32[2,2,80,128]{3,2,1,0:T(8,128)S(1)}, u32[]{:S(2)}, u32[]{:S(2)}) collective-permute-start(f32[2,2,80,128]{3,2,1,0:T(8,128)S(1)} %get-tuple-element.72), channel_id=1, source_target_pairs={{1,0},{0,1},{3,2},{2,3},{5,4},{4,5},{7,6},{6,7},{9,8},{8,9},{11,10... | collective-permute-start | bytes 491528 | tf_op jit(solution)/shard_map/ppermute | solution.py:266
  44.9 9.5 %collective-permute-start.12 = (f32[2,1,80,128]{3,2,0,1:T(8,128)S(1)}, f32[2,1,80,128]{3,2,0,1:T(8,128)S(1)}, u32[]{:S(2)}, u32[]{:S(2)}) collective-permute-start(f32[2,1,80,128]{3,2,0,1:T(8,128)S(1)} %bitcast.38), channel_id=1, source_target_pairs={{2,0},{3,1},{0,2},{1,3},{6,4},{7,5},{4,6},{5,7},{10,8},{11,9},{8,1... | collective-permute-start | bytes 245768 | tf_op jit(solution)/shard_map/ppermute | solution.py:266
  48.8 7.2 %collective-permute-start.14 = (f32[2,1,80,128]{3,2,0,1:T(8,128)S(1)}, f32[2,1,80,128]{3,2,0,1:T(8,128)S(1)}, u32[]{:S(2)}, u32[]{:S(2)}) collective-permute-start(f32[2,1,80,128]{3,2,0,1:T(8,128)S(1)} %bitcast.39), channel_id=1, source_target_pairs={{2,0},{3,1},{0,2},{1,3},{6,4},{7,5},{4,6},{5,7},{10,8},{11,9},{8,1... | collective-permute-start | bytes 245768 | tf_op jit(solution)/shard_map/ppermute | solution.py:266
  51.6 5.4 %collective-permute-start.18 = (f32[2,1,80,128]{3,2,0,1:T(8,128)S(1)}, f32[2,1,80,128]{3,2,0,1:T(8,128)S(1)}, u32[]{:S(2)}, u32[]{:S(2)}) collective-permute-start(f32[2,1,80,128]{3,2,0,1:T(8,128)S(1)} %bitcast.40), channel_id=1, source_target_pairs={{2,0},{3,1},{0,2},{1,3},{6,4},{7,5},{4,6},{5,7},{10,8},{11,9},{8,1... | collective-permute-start | bytes 245768 | tf_op jit(solution)/shard_map/ppermute | solution.py:266
  56.0 1.4 %collective-permute-start.19 = (f32[3,80,128]{2,1,0:T(8,128)S(1)}, f32[3,80,128]{2,1,0:T(8,128)S(1)}, u32[]{:S(2)}, u32[]{:S(2)}) collective-permute-start(f32[3,80,128]{2,1,0:T(8,128)S(1)} %shard_map.51), channel_id=1, source_target_pairs={{4,0},{0,4},{12,8},{8,12},{20,16},{16,20},{28,24},{24,28},{5,1},{1... | collective-permute-start | bytes 368648 | tf_op jit(solution)/shard_map/ppermute | solution.py:263
  57.0 1.2 %collective-permute-start.20 = (f32[1,80,128]{2,1,0:T(8,128)S(1)}, f32[1,80,128]{2,1,0:T(8,128)S(1)}, u32[]{:S(2)}, u32[]{:S(2)}) collective-permute-start(f32[1,80,128]{2,1,0:T(8,128)S(1)} %shard_map.52), channel_id=1, source_target_pairs={{4,0},{0,4},{12,8},{8,12},{20,16},{16,20},{28,24},{24,28},{5,1},{1... | collective-permute-start | bytes 122888 | tf_op jit(solution)/shard_map/ppermute | solution.py:263

commit v5 on v4

--- a/solution.py
+++ b/solution.py
@@ -11,19 +11,19 @@
 PAIRS = 5
 CHUNKS = 4
 STEPS = 5
-ORDER = ("F0", "F1", "U", "F2", "F3", "X0", "X1", "F0F1", "X2", "X0X1", "X3", "F2F3", "X2X3")
+ORDER = ("F0", "F1", "U", "F2", "F3", "X0", "F0F1", "X1", "F2X0", "X2", "F3X1", "X3", "X2X3")
 TIES = {
-    "F0F1b": ("X1",),
-    "F2": ("Ua",),
-    "F2F3": ("F0F1b",),
-    "F3": ("F1", "S"),
+    "F2": ("S",),
+    "F2X0": ("F0F1a", "Ub"),
+    "F3": ("F0", "S", "Ub"),
+    "F3X1": ("F2X0a",),
     "X0": ("S", "Ua"),
-    "X0X1": ("F0F1k", "F2", "Ub"),
-    "X0X1b": ("F3",),
-    "X2": ("F0F1k",),
-    "X2X3": ("X0X1a",),
-    "X3": ("F0F1a", "Ub", "X0X1k"),
+    "X1": ("F0F1k",),
+    "X2": ("F0F1a", "Ua"),
+    "X2X3": ("F0F1b",),
+    "X3": ("F2X0k",),
 }
+JOINT = ("F2X0", "F3X1")
 LANES = 128
 VMEM = pl.BlockSpec(memory_space=pltpu.VMEM)
 HBM = pl.BlockSpec(memory_space=pltpu.HBM)
@@ -167,14 +167,21 @@
         out[slot // 2] = keep_ref[slot] + got_ref[slot]
 
 
-def home_kernel(*refs):
+def joint_add_kernel(*refs):
+    *in_refs, keep_ref, send_ref = refs
+    for u in range(len(in_refs) // 2):
+        for t in range(2):
+            keep_ref[2 * u + t] = in_refs[2 * u][t, 0] + in_refs[2 * u + 1][t, 0]
+            send_ref[2 * u + t] = in_refs[2 * u][t, 1] + in_refs[2 * u + 1][t, 1]
+
+
+def home_kernel(bases, *refs):
     *in_refs, out_ref = refs
-    for k in range(out_ref.shape[0]):
-        last = in_refs[2 * k].shape[0] - 1
-        out_ref[k] = in_refs[2 * k][last] + in_refs[2 * k + 1][last]
-
-
-def final_kernel(factor, units, live_ref, *refs):
+    for k, base in enumerate(bases):
+        out_ref[k] = in_refs[2 * k][base + 1] + in_refs[2 * k + 1][base + 1]
+
+
+def final_kernel(factor, units, bases, live_ref, *refs):
     own_keep_ref, own_got_ref, *in_refs, early_ref, late_ref, out_hbm, out_ref, sems = refs
     places = [(r, i) for r in (early_ref, late_ref) for i in range(r.shape[0])]
     width = LANES // CHUNKS
@@ -187,14 +194,12 @@
         second = jnp.broadcast_to(lax.axis_index("stn") & 1, own[:, :LANES].shape) == 1
         columns = {}
         for u, unit in enumerate(units):
-            tiles = in_refs[2 * u].shape[0]
-            mine = in_refs[2 * u][0, some, :] + in_refs[2 * u + 1][0, some, :]
+            mine = in_refs[2 * u][bases[u], some, :] + in_refs[2 * u + 1][bases[u], some, :]
             theirs = places[u][0][places[u][1], some, :]
             for i, (kind, k) in enumerate(unit):
                 for part in range(2):
                     at = (part * len(unit) + i) * width
                     columns[kind, k, part] = mine[:, at : at + width]
-                    at += LANES // 2 if tiles == 1 else 0
                     columns[kind + "s", k, part] = theirs[:, at : at + width]
         for part in range(2):
             four, two, mine_two, mine_four = (
@@ -316,9 +321,24 @@
             [pltpu.VMEM((2, columns, freq), BF16), pltpu.VMEM((tiles, rows, LANES), F32)],
         )
         done[name + "k"] = keep
-        return pieces, reduce(keep, send, tiles, name)
-
-    four, two = [], []
+        if name not in JOINT:
+            return pieces, reduce(keep, send, tiles, name), 0
+        distance = 1
+        while 4 * distance < members:
+            keep, send = halve(keep, send, distance, tiles)
+            distance *= 2
+        got = lax.ppermute(send, "seg", [(i ^ distance, i) for i in range(members)])
+        done[name + "a"] = got
+        held.extend([keep, got])
+        if len(held) == 2 * len(JOINT):
+            shape = (2 * len(JOINT), per, LANES)
+            kept, sent = call(joint_add_kernel, [(shape, F32)] * 2, held, 8)
+            distance = members // 2
+            done["J"] = lax.ppermute(sent, "seg", [(i ^ distance, i) for i in range(members)])
+            joint.extend([kept, done["J"]])
+        return pieces, joint, 2 * (len(held) // 2 - 1)
+
+    four, two, held, joint = [], [], [], []
     units = []
     for name in ORDER:
         if name == "U":
@@ -329,15 +349,16 @@
             two.append(two_of(int(name[1])))
         else:
             units.append(unit(name))
-    pieces = [piece for _, piece in units]
-    units = [names for names, _ in units]
+    bases = [base for _, _, base in units]
+    pieces = [piece for _, piece, _ in units]
+    units = [names for names, _, _ in units]
     early = [v for piece in pieces[:-1] for v in piece]
-    (early_home,) = call(home_kernel, [((len(pieces) - 1, per, LANES), F32)], early, 8)
-    (late_home,) = call(home_kernel, [((1, per, LANES), F32)], pieces[-1], 8)
+    (early_home,) = call(functools.partial(home_kernel, bases[:-1]), [((len(pieces) - 1, per, LANES), F32)], early, 8)
+    (late_home,) = call(functools.partial(home_kernel, bases[-1:]), [((1, per, LANES), F32)], pieces[-1], 8)
     sums = [v for piece in pieces for v in piece]
     operands = [pair_live, own_keep, own_got, *sums, exchange(early_home, 1), exchange(late_home, 1)]
     (out,) = call(
-        functools.partial(final_kernel, factor, units),
+        functools.partial(final_kernel, factor, units, bases),
         [((2 * PAIRS * per, 2 * block), F32)],
         operands,
         12,

time: 59.8 us -> 58.5 us (0.978)
  starting transfers between devices: 34.2 us -> 27.7 us
  waiting for transfers between devices: 13.6 us -> 18.8 us
    ppermute x10 -> x6, starting transfers between devices: 22 us -> 13.4 us  [halve(): got = lax.ppermute(send, 'seg', [(i ^ distance, i) for i in range(members)])]
    ppermute x10 -> x6, waiting for transfers between devices: 9.3 us -> 14.5 us  [halve(): got = lax.ppermute(send, 'seg', [(i ^ distance, i) for i in range(members)])]
    ppermute x0 -> x3, starting transfers between devices: none -> 4.34 us  [the longest x2 3 us: unit(): got = lax.ppermute(send, 'seg', [(i ^ distance, i) for i in range(members)])]
    ppermute x4, waiting for transfers between devices: 3.09 us -> 0.01 us  [four_of(): lax.ppermute(value, 'stn', [((i - 4) % blocks, i) for i in ids])]
    ppermute x0 -> x3, waiting for transfers between devices: none -> 3.01 us  [the longest x2 1.68 us: unit(): got = lax.ppermute(send, 'seg', [(i ^ distance, i) for i in range(members)])]
    ppermute x4, starting transfers between devices: 5.96 us -> 4.11 us  [four_of(): lax.ppermute(value, 'stn', [((i - 4) % blocks, i) for i in ids])]
    pallas_call x17 -> x16, Pallas kernels: 11.6 us -> 11.6 us  [call(): pl.pallas_call(kernel, in_specs=specs or [VMEM] * len(operands), out_spec...]
  transfers between devices with their start and end apart: 21 -> 20, of which waited for: 9 -> 9; matrix products, arithmetic and copies ran while one was open for 0% -> 0% of each run, Pallas kernels for 12% -> 12%
where the time goes in v5:
time: 58.5 us; the launch traced here: 58.2 us
  starting transfers between devices  27.7 us (47%)
  waiting for transfers between devices  18.8 us (32%)
  Pallas kernels  11.6 us (20%)
    ppermute x6, waiting for transfers between devices, halve(): got = lax.ppermute(send, 'seg', [(i ^ distance, i) for i in range(members)])  14.5 us
    ppermute x6, starting transfers between devices, halve(): got = lax.ppermute(send, 'seg', [(i ^ distance, i) for i in range(members)])  13.4 us
    pallas_call x16, Pallas kernels, call(): pl.pallas_call(kernel, in_specs=specs or [VMEM] * len(operands), out_spec...  11.6 us
    ppermute x7, starting transfers between devices, exchange(): return lax.ppermute(c, 'stn', [(i ^ distance, i) for i in ids])  5.87 us
    ppermute x4, starting transfers between devices, four_of(): lax.ppermute(value, 'stn', [((i - 4) % blocks, i) for i in ids])  4.11 us
    ppermute x2, starting transfers between devices, unit(): got = lax.ppermute(send, 'seg', [(i ^ distance, i) for i in range(members)])  3 us
    ppermute x2, waiting for transfers between devices, unit(): got = lax.ppermute(send, 'seg', [(i ^ distance, i) for i in range(members)])  1.68 us
    ppermute x1, starting transfers between devices, unit(): lax.ppermute(sent, 'seg', [(i ^ distance, i) for i in range(members)])  1.34 us
  transfers between devices with their start and end apart: 20, of which 9 were waited for; matrix products, arithmetic and copies ran while one was open for 0% of the time, Pallas kernels for 12%

profile of v5, /device:TPU:0, one launch (start us, length us, event | category | flops | bytes accessed | tf_op | source)
XLA Modules:
  0.0 58.2 jit_solution(6183620189581632783)
XLA Ops:
  0.0 3.1 %shard_map.37 = (bf16[8,64]{1,0:T(8,128)(2,1)S(1)}, bf16[64,2048]{1,0:T(8,128)(2,1)S(1)}, bf16[64,2048]{1,0:T(8,128)(2,1)S(1)}, bf16[64,2048]{1,0:T(8,128)(2,1)S...) custom-call(bf16[64,5,1,2,2048]{4,3,2,1,0:T(2,128)(2,1)} %x_hbm.1, ...), custom_call_target="tpu_custom_call" | custom-call | tf_op jit(solution)/shard_map/pallas_call | solution.py:240
  3.1 0.5 collective-permute-start.2
  3.6 2.6 %collective-permute-start.3 = (bf16[64,2048]{1,0:T(8,128)(2,1)S(1)}, bf16[64,2048]{1,0:T(8,128)(2,1)S(1)}, u32[]{:S(2)}, u32[]{:S(2)}) collective-permute-start(bf16[64,2048]{1,0:T(8,128)(2,1)S(1)} %get-tuple-element.52.refs_2_.own_ref.refs_3_), channel_id=1, source_target_pairs={{16,0},{20,4},{24,8},{28,12},{0,16},{4,20},{8,24},{12,28},{17,1},{... | collective-permute-start | bytes 786440 | tf_op jit(solution)/shard_map/ppermute | solution.py:300
  6.2 1.6 %collective-permute-start = (f32[2,80,256]{2,1,0:T(8,128)S(1)}, f32[2,80,256]{2,1,0:T(8,128)S(1)}, u32[]{:S(2)}, u32[]{:S(2)}) collective-permute-start(f32[2,80,256]{2,1,0:T(8,128)S(1)} %get-tuple-element.39), channel_id=1, source_target_pairs={{1,0},{0,1},{3,2},{2,3},{5,4},{4,5},{7,6},{6,7},{9,8},{8,9},{11,10... | collective-permute-start | bytes 491528 | tf_op jit(solution)/shard_map/ppermute | solution.py:271
  7.8 0.5 collective-permute-start.4
  8.3 4.2 %collective-permute-done.got_ref = f32[2,80,256]{2,1,0:T(8,128)S(1)} collective-permute-done((f32[2,80,256]{2,1,0:T(8,128)S(1)}, f32[2,80,256]{2,1,0:T(8,128)S(1)}, u32[]{:S(2)}, u32[]{:S(2)}) %collective-permute-start) | collective-permute-done | bytes 163872 | tf_op jit(solution)/shard_map/ppermute | solution.py:271
  12.5 2.7 %collective-permute-start.1 = (f32[1,80,256]{2,1,0:T(8,128)S(1)}, f32[1,80,256]{2,1,0:T(8,128)S(1)}, u32[]{:S(2)}, u32[]{:S(2)}) collective-permute-start(f32[1,80,256]{2,1,0:T(8,128)S(1)} %get-tuple-element.41), channel_id=1, source_target_pairs={{2,0},{3,1},{0,2},{1,3},{6,4},{7,5},{4,6},{5,7},{10,8},{11,9},{8,1... | collective-permute-start | bytes 245768 | tf_op jit(solution)/shard_map/ppermute | solution.py:271
  15.1 0.0 collective-permute-done.2.sib_ref
  15.1 0.0 collective-permute-done.3.refs_0_.four_ref
  15.2 1.6 %collective-permute-start.8 = (bf16[64,2048]{1,0:T(8,128)(2,1)S(1)}, bf16[64,2048]{1,0:T(8,128)(2,1)S(1)}, u32[]{:S(2)}, u32[]{:S(2)}) collective-permute-start(bf16[64,2048]{1,0:T(8,128)(2,1)S(1)} %shard_map.41), channel_id=1, source_target_pairs={{8,0},{12,4},{0,8},{4,12},{24,16},{28,20},{16,24},{20,28},{9,1},{1... | collective-permute-start | bytes 786440 | tf_op jit(solution)/shard_map/ppermute | solution.py:268
  16.7 0.5 collective-permute-start.7
  17.2 1.8 %collective-permute-done.1 = f32[1,80,256]{2,1,0:T(8,128)S(1)} collective-permute-done((f32[1,80,256]{2,1,0:T(8,128)S(1)}, f32[1,80,256]{2,1,0:T(8,128)S(1)}, u32[]{:S(2)}, u32[]{:S(2)}) %collective-permute-start.1) | collective-permute-done | bytes 81952 | tf_op jit(solution)/shard_map/ppermute | solution.py:271
  19.0 0.5 collective-permute-start.10
  19.5 0.0 collective-permute-done.4.refs_1_.four_ref
  19.5 1.8 %shard_map.39 = (f32[2,2,80,128]{3,2,1,0:T(8,128)S(1)}, f32[2,2,80,128]{3,2,1,0:T(8,128)S(1)}) custom-call(bf16[640,2048]{1,0:T(8,128)(2,1)S(1)} %get-tuple-element.42.a_ref, bf16[640,2048]{1,0:T(8,128)(2,1)S(1)} %collective-permute-done.2.sib_ref, bf16[64,2048]{1,0:T(8,128)(2,1)S(1)} %collective-permute-done.3.refs_0_.four_ref, ...), custom_call_target="tpu_custom_call" | custom-call | tf_op jit(solution)/shard_map/pallas_call | solution.py:240
  21.3 1.5 %collective-permute-start.5 = (f32[2,2,80,128]{3,2,1,0:T(8,128)S(1)}, f32[2,2,80,128]{3,2,1,0:T(8,128)S(1)}, u32[]{:S(2)}, u32[]{:S(2)}) collective-permute-start(f32[2,2,80,128]{3,2,1,0:T(8,128)S(1)} %get-tuple-element.47), channel_id=1, source_target_pairs={{1,0},{0,1},{3,2},{2,3},{5,4},{4,5},{7,6},{6,7},{9,8},{8,9},{11,10... | collective-permute-start | bytes 491528 | tf_op jit(solution)/shard_map/ppermute | solution.py:271
  22.9 1.6 %collective-permute-start.11 = (bf16[64,2048]{1,0:T(8,128)(2,1)S(1)}, bf16[64,2048]{1,0:T(8,128)(2,1)S(1)}, u32[]{:S(2)}, u32[]{:S(2)}) collective-permute-start(bf16[64,2048]{1,0:T(8,128)(2,1)S(1)} %shard_map.43), channel_id=1, source_target_pairs={{8,0},{12,4},{0,8},{4,12},{24,16},{28,20},{16,24},{20,28},{9,1},{1... | collective-permute-start | bytes 786440 | tf_op jit(solution)/shard_map/ppermute | solution.py:268
  24.4 2.3 %collective-permute-done.5 = f32[2,2,80,128]{3,2,1,0:T(8,128)S(1)} collective-permute-done((f32[2,2,80,128]{3,2,1,0:T(8,128)S(1)}, f32[2,2,80,128]{3,2,1,0:T(8,128)S(1)}, u32[]{:S(2)}, u32[]{:S(2)}) %collective-permute-start.5) | collective-permute-done | bytes 163872 | tf_op jit(solution)/shard_map/ppermute | solution.py:271
  26.7 0.0 collective-permute-done.8.refs_1_
  26.8 0.0 collective-permute-done.7.refs_0_.four_ref
  26.8 1.7 %shard_map.42 = (f32[2,2,80,128]{3,2,1,0:T(8,128)S(1)}, f32[2,2,80,128]{3,2,1,0:T(8,128)S(1)}) custom-call(bf16[640,2048]{1,0:T(8,128)(2,1)S(1)} %get-tuple-element.42.a_ref, bf16[640,2048]{1,0:T(8,128)(2,1)S(1)} %collective-permute-done.2.sib_ref, bf16[64,2048]{1,0:T(8,128)(2,1)S(1)} %collective-permute-done.7.refs_0_.four_ref, ...), custom_call_target="tpu_custom_call" | custom-call | tf_op jit(solution)/shard_map/pallas_call | solution.py:240
  28.5 1.5 %collective-permute-start.9 = (f32[2,2,80,128]{3,2,1,0:T(8,128)S(1)}, f32[2,2,80,128]{3,2,1,0:T(8,128)S(1)}, u32[]{:S(2)}, u32[]{:S(2)}) collective-permute-start(f32[2,2,80,128]{3,2,1,0:T(8,128)S(1)} %get-tuple-element.55), channel_id=1, source_target_pairs={{1,0},{0,1},{3,2},{2,3},{5,4},{4,5},{7,6},{6,7},{9,8},{8,9},{11,10... | collective-permute-start | bytes 491528 | tf_op jit(solution)/shard_map/ppermute | solution.py:330
  30.0 1.6 %collective-permute-start.14 = (bf16[64,2048]{1,0:T(8,128)(2,1)S(1)}, bf16[64,2048]{1,0:T(8,128)(2,1)S(1)}, u32[]{:S(2)}, u32[]{:S(2)}) collective-permute-start(bf16[64,2048]{1,0:T(8,128)(2,1)S(1)} %shard_map.46), channel_id=1, source_target_pairs={{8,0},{12,4},{0,8},{4,12},{24,16},{28,20},{16,24},{20,28},{9,1},{1... | collective-permute-start | bytes 786440 | tf_op jit(solution)/shard_map/ppermute | solution.py:268
  31.6 0.0 collective-permute-done.10.refs_0_.four_ref
  31.6 0.6 %collective-permute-start.15 = (bf16[64,2048]{1,0:T(8,128)(2,1)S(1)}, bf16[64,2048]{1,0:T(8,128)(2,1)S(1)}, u32[]{:S(2)}, u32[]{:S(2)}) collective-permute-start(bf16[64,2048]{1,0:T(8,128)(2,1)S(1)} %shard_map.47), channel_id=1, source_target_pairs={{8,0},{12,4},{0,8},{4,12},{24,16},{28,20},{16,24},{20,28},{9,1},{1... | collective-permute-start | bytes 786440 | tf_op jit(solution)/shard_map/ppermute | solution.py:268
  32.2 1.7 %collective-permute-done.9.refs_1_ = f32[2,2,80,128]{3,2,1,0:T(8,128)S(1)} collective-permute-done((f32[2,2,80,128]{3,2,1,0:T(8,128)S(1)}, f32[2,2,80,128]{3,2,1,0:T(8,128)S(1)}, u32[]{:S(2)}, u32[]{:S(2)}) %collective-permute-start.9) | collective-permute-done | bytes 163872 | tf_op jit(solution)/shard_map/ppermute | solution.py:330
  33.9 0.0 collective-permute-done.11.refs_1_
  33.9 1.7 %shard_map.44 = (f32[2,2,80,128]{3,2,1,0:T(8,128)S(1)}, f32[2,2,80,128]{3,2,1,0:T(8,128)S(1)}) custom-call(bf16[640,2048]{1,0:T(8,128)(2,1)S(1)} %get-tuple-element.42.a_ref, bf16[640,2048]{1,0:T(8,128)(2,1)S(1)} %collective-permute-done.2.sib_ref, bf16[64,2048]{1,0:T(8,128)(2,1)S(1)} %collective-permute-done.10.refs_0_.four_ref, ...), custom_call_target="tpu_custom_call" | custom-call | tf_op jit(solution)/shard_map/pallas_call | solution.py:240
  35.6 1.5 %collective-permute-start.12 = (f32[2,2,80,128]{3,2,1,0:T(8,128)S(1)}, f32[2,2,80,128]{3,2,1,0:T(8,128)S(1)}, u32[]{:S(2)}, u32[]{:S(2)}) collective-permute-start(f32[2,2,80,128]{3,2,1,0:T(8,128)S(1)} %get-tuple-element.61), channel_id=1, source_target_pairs={{1,0},{0,1},{3,2},{2,3},{5,4},{4,5},{7,6},{6,7},{9,8},{8,9},{11,10... | collective-permute-start | bytes 491528 | tf_op jit(solution)/shard_map/ppermute | solution.py:330
  37.1 2.6 %collective-permute-start.6 = (f32[2,1,80,128]{3,2,0,1:T(8,128)S(1)}, f32[2,1,80,128]{3,2,0,1:T(8,128)S(1)}, u32[]{:S(2)}, u32[]{:S(2)}) collective-permute-start(f32[2,1,80,128]{3,2,0,1:T(8,128)S(1)} %bitcast.23), channel_id=1, source_target_pairs={{2,0},{3,1},{0,2},{1,3},{6,4},{7,5},{4,6},{5,7},{10,8},{11,9},{8,1... | collective-permute-start | bytes 245768 | tf_op jit(solution)/shard_map/ppermute | solution.py:271
  39.7 2.7 %collective-permute-done.6 = f32[2,1,80,128]{3,2,0,1:T(8,128)S(1)} collective-permute-done((f32[2,1,80,128]{3,2,0,1:T(8,128)S(1)}, f32[2,1,80,128]{3,2,0,1:T(8,128)S(1)}, u32[]{:S(2)}, u32[]{:S(2)}) %collective-permute-start.6) | collective-permute-done | bytes 81952 | tf_op jit(solution)/shard_map/ppermute | solution.py:271
  42.5 0.0 copy-start
  42.5 0.0 collective-permute-done.14.refs_0_
  42.5 0.0 collective-permute-done.15.refs_1_
  42.5 1.7 %shard_map.48 = (f32[2,2,80,128]{3,2,1,0:T(8,128)S(1)}, f32[2,2,80,128]{3,2,1,0:T(8,128)S(1)}) custom-call(bf16[640,2048]{1,0:T(8,128)(2,1)S(1)} %get-tuple-element.42.a_ref, bf16[640,2048]{1,0:T(8,128)(2,1)S(1)} %collective-permute-done.2.sib_ref, bf16[64,2048]{1,0:T(8,128)(2,1)S(1)} %collective-permute-done.14.refs_0_, ...), custom_call_target="tpu_custom_call" | custom-call | tf_op jit(solution)/shard_map/pallas_call | solution.py:240
  44.2 1.9 %collective-permute-start.16 = (f32[2,2,80,128]{3,2,1,0:T(8,128)S(1)}, f32[2,2,80,128]{3,2,1,0:T(8,128)S(1)}, u32[]{:S(2)}, u32[]{:S(2)}) collective-permute-start(f32[2,2,80,128]{3,2,1,0:T(8,128)S(1)} %get-tuple-element.68), channel_id=1, source_target_pairs={{1,0},{0,1},{3,2},{2,3},{5,4},{4,5},{7,6},{6,7},{9,8},{8,9},{11,10... | collective-permute-start | bytes 491528 | tf_op jit(solution)/shard_map/ppermute | solution.py:271
  46.1 0.0 collective-permute-done.12.refs_3_
  46.1 1.3 %collective-permute-start.13 = (f32[4,80,128]{2,1,0:T(8,128)S(1)}, f32[4,80,128]{2,1,0:T(8,128)S(1)}, u32[]{:S(2)}, u32[]{:S(2)}) collective-permute-start(f32[4,80,128]{2,1,0:T(8,128)S(1)} %get-tuple-element.63), channel_id=1, source_target_pairs={{2,0},{3,1},{0,2},{1,3},{6,4},{7,5},{4,6},{5,7},{10,8},{11,9},{8,1... | collective-permute-start | bytes 491528 | tf_op jit(solution)/shard_map/ppermute | solution.py:337
  47.5 2.5 %collective-permute-done.16 = f32[2,2,80,128]{3,2,1,0:T(8,128)S(1)} collective-permute-done((f32[2,2,80,128]{3,2,1,0:T(8,128)S(1)}, f32[2,2,80,128]{3,2,1,0:T(8,128)S(1)}, u32[]{:S(2)}, u32[]{:S(2)}) %collective-permute-start.16) | collective-permute-done | bytes 163872 | tf_op jit(solution)/shard_map/ppermute | solution.py:271
  50.0 3.1 %collective-permute-start.17 = (f32[2,1,80,128]{3,2,0,1:T(8,128)S(1)}, f32[2,1,80,128]{3,2,0,1:T(8,128)S(1)}, u32[]{:S(2)}, u32[]{:S(2)}) collective-permute-start(f32[2,1,80,128]{3,2,0,1:T(8,128)S(1)} %bitcast.24), channel_id=1, source_target_pairs={{2,0},{3,1},{0,2},{1,3},{6,4},{7,5},{4,6},{5,7},{10,8},{11,9},{8,1... | collective-permute-start | bytes 245768 | tf_op jit(solution)/shard_map/ppermute | solution.py:271
  53.1 1.3 %collective-permute-done.13.refs_3_.refs_5_.refs_7_ = f32[4,80,128]{2,1,0:T(8,128)S(1)} collective-permute-done((f32[4,80,128]{2,1,0:T(8,128)S(1)}, f32[4,80,128]{2,1,0:T(8,128)S(1)}, u32[]{:S(2)}, u32[]{:S(2)}) %collective-permute-start.13) | collective-permute-done | bytes 163872 | tf_op jit(solution)/shard_map/ppermute | solution.py:337
  54.5 0.1 collective-permute-start.18
  54.5 1.0 %collective-permute-done.17 = f32[2,1,80,128]{3,2,0,1:T(8,128)S(1)} collective-permute-done((f32[2,1,80,128]{3,2,0,1:T(8,128)S(1)}, f32[2,1,80,128]{3,2,0,1:T(8,128)S(1)}, u32[]{:S(2)}, u32[]{:S(2)}) %collective-permute-start.17) | collective-permute-done | bytes 81952 | tf_op jit(solution)/shard_map/ppermute | solution.py:271
  55.5 0.0 collective-permute-start.19
  55.6 1.2 %collective-permute-done.19.refs_11_ = f32[1,80,128]{2,1,0:T(8,128)S(1)} collective-permute-done((f32[1,80,128]{2,1,0:T(8,128)S(1)}, f32[1,80,128]{2,1,0:T(8,128)S(1)}, u32[]{:S(2)}, u32[]{:S(2)}) %collective-permute-start.19) | collective-permute-done | bytes 40992 | tf_op jit(solution)/shard_map/ppermute | solution.py:268
  56.8 0.0 collective-permute-done.18.refs_10_
  56.8 0.0 copy-done
  56.8 1.5 %shard_map.52 = f32[800,128]{1,0:T(8,128)} custom-call(s32[1,5]{1,0:T(1,128)S(1)} %copy-done, f32[80,256]{1,0:T(8,128)S(1)} %bitcast.21, f32[80,256]{1,0:T(8,128)S(1)} %bitcast.22, f32[2,80,128]{2,1,0:T(8,128)S(1)} %get-tuple-element.48.refs_0_.refs_2_, f32[2,80,128]{2,1,0:T(8,128)S(1)} %bitcast.14, ...), custom_call_target="tpu_custom_call" | custom-call | tf_op jit(solution)/shard_map/pallas_call | solution.py:240
  (10 shorter events, 0.2 us)
Async XLA Ops:
  3.1 12.1 %collective-permute-start.2 = (bf16[640,2048]{1,0:T(8,128)(2,1)S(1)}, bf16[640,2048]{1,0:T(8,128)(2,1)S(1)}, u32[]{:S(2)}, u32[]{:S(2)}) collective-permute-start(bf16[640,2048]{1,0:T(8,128)(2,1)S(1)} %get-tuple-element.42.a_ref), channel_id=1, source_target_pairs={{4,0},{0,4},{12,8},{8,12},{20,16},{16,20},{28,24},{24,28},{5,1},{1... | collective-permute-start | bytes 7864328 | tf_op jit(solution)/shard_map/ppermute | solution.py:268
  3.6 11.5 %collective-permute-start.3 = (bf16[64,2048]{1,0:T(8,128)(2,1)S(1)}, bf16[64,2048]{1,0:T(8,128)(2,1)S(1)}, u32[]{:S(2)}, u32[]{:S(2)}) collective-permute-start(bf16[64,2048]{1,0:T(8,128)(2,1)S(1)} %get-tuple-element.52.refs_2_.own_ref.refs_3_), channel_id=1, source_target_pairs={{16,0},{20,4},{24,8},{28,12},{0,16},{4,20},{8,24},{12,28},{17,1},{... | collective-permute-start | bytes 786440 | tf_op jit(solution)/shard_map/ppermute | solution.py:300
  6.2 6.3 %collective-permute-start = (f32[2,80,256]{2,1,0:T(8,128)S(1)}, f32[2,80,256]{2,1,0:T(8,128)S(1)}, u32[]{:S(2)}, u32[]{:S(2)}) collective-permute-start(f32[2,80,256]{2,1,0:T(8,128)S(1)} %get-tuple-element.39), channel_id=1, source_target_pairs={{1,0},{0,1},{3,2},{2,3},{5,4},{4,5},{7,6},{6,7},{9,8},{8,9},{11,10... | collective-permute-start | bytes 491528 | tf_op jit(solution)/shard_map/ppermute | solution.py:271
  7.8 11.8 %collective-permute-start.4 = (bf16[64,2048]{1,0:T(8,128)(2,1)S(1)}, bf16[64,2048]{1,0:T(8,128)(2,1)S(1)}, u32[]{:S(2)}, u32[]{:S(2)}) collective-permute-start(bf16[64,2048]{1,0:T(8,128)(2,1)S(1)} %get-tuple-element.58.refs_3_.own_ref), channel_id=1, source_target_pairs={{16,0},{20,4},{24,8},{28,12},{0,16},{4,20},{8,24},{12,28},{17,1},{... | collective-permute-start | bytes 786440 | tf_op jit(solution)/shard_map/ppermute | solution.py:300
  12.5 6.5 %collective-permute-start.1 = (f32[1,80,256]{2,1,0:T(8,128)S(1)}, f32[1,80,256]{2,1,0:T(8,128)S(1)}, u32[]{:S(2)}, u32[]{:S(2)}) collective-permute-start(f32[1,80,256]{2,1,0:T(8,128)S(1)} %get-tuple-element.41), channel_id=1, source_target_pairs={{2,0},{3,1},{0,2},{1,3},{6,4},{7,5},{4,6},{5,7},{10,8},{11,9},{8,1... | collective-permute-start | bytes 245768 | tf_op jit(solution)/shard_map/ppermute | solution.py:271
  15.2 11.6 %collective-permute-start.8 = (bf16[64,2048]{1,0:T(8,128)(2,1)S(1)}, bf16[64,2048]{1,0:T(8,128)(2,1)S(1)}, u32[]{:S(2)}, u32[]{:S(2)}) collective-permute-start(bf16[64,2048]{1,0:T(8,128)(2,1)S(1)} %shard_map.41), channel_id=1, source_target_pairs={{8,0},{12,4},{0,8},{4,12},{24,16},{28,20},{16,24},{20,28},{9,1},{1... | collective-permute-start | bytes 786440 | tf_op jit(solution)/shard_map/ppermute | solution.py:268
  16.7 10.0 %collective-permute-start.7 = (bf16[64,2048]{1,0:T(8,128)(2,1)S(1)}, bf16[64,2048]{1,0:T(8,128)(2,1)S(1)}, u32[]{:S(2)}, u32[]{:S(2)}) collective-permute-start(bf16[64,2048]{1,0:T(8,128)(2,1)S(1)} %get-tuple-element.64.refs_2_.own_ref), channel_id=1, source_target_pairs={{16,0},{20,4},{24,8},{28,12},{0,16},{4,20},{8,24},{12,28},{17,1},{... | collective-permute-start | bytes 786440 | tf_op jit(solution)/shard_map/ppermute | solution.py:300
  19.0 12.6 %collective-permute-start.10 = (bf16[64,2048]{1,0:T(8,128)(2,1)S(1)}, bf16[64,2048]{1,0:T(8,128)(2,1)S(1)}, u32[]{:S(2)}, u32[]{:S(2)}) collective-permute-start(bf16[64,2048]{1,0:T(8,128)(2,1)S(1)} %get-tuple-element.65.refs_2_.own_ref.refs_3_), channel_id=1, source_target_pairs={{16,0},{20,4},{24,8},{28,12},{0,16},{4,20},{8,24},{12,28},{17,1},{... | collective-permute-start | bytes 786440 | tf_op jit(solution)/shard_map/ppermute | solution.py:300
  21.3 5.4 %collective-permute-start.5 = (f32[2,2,80,128]{3,2,1,0:T(8,128)S(1)}, f32[2,2,80,128]{3,2,1,0:T(8,128)S(1)}, u32[]{:S(2)}, u32[]{:S(2)}) collective-permute-start(f32[2,2,80,128]{3,2,1,0:T(8,128)S(1)} %get-tuple-element.47), channel_id=1, source_target_pairs={{1,0},{0,1},{3,2},{2,3},{5,4},{4,5},{7,6},{6,7},{9,8},{8,9},{11,10... | collective-permute-start | bytes 491528 | tf_op jit(solution)/shard_map/ppermute | solution.py:271
  22.9 11.0 %collective-permute-start.11 = (bf16[64,2048]{1,0:T(8,128)(2,1)S(1)}, bf16[64,2048]{1,0:T(8,128)(2,1)S(1)}, u32[]{:S(2)}, u32[]{:S(2)}) collective-permute-start(bf16[64,2048]{1,0:T(8,128)(2,1)S(1)} %shard_map.43), channel_id=1, source_target_pairs={{8,0},{12,4},{0,8},{4,12},{24,16},{28,20},{16,24},{20,28},{9,1},{1... | collective-permute-start | bytes 786440 | tf_op jit(solution)/shard_map/ppermute | solution.py:268
  28.5 5.4 %collective-permute-start.9 = (f32[2,2,80,128]{3,2,1,0:T(8,128)S(1)}, f32[2,2,80,128]{3,2,1,0:T(8,128)S(1)}, u32[]{:S(2)}, u32[]{:S(2)}) collective-permute-start(f32[2,2,80,128]{3,2,1,0:T(8,128)S(1)} %get-tuple-element.55), channel_id=1, source_target_pairs={{1,0},{0,1},{3,2},{2,3},{5,4},{4,5},{7,6},{6,7},{9,8},{8,9},{11,10... | collective-permute-start | bytes 491528 | tf_op jit(solution)/shard_map/ppermute | solution.py:330
  30.0 12.4 %collective-permute-start.14 = (bf16[64,2048]{1,0:T(8,128)(2,1)S(1)}, bf16[64,2048]{1,0:T(8,128)(2,1)S(1)}, u32[]{:S(2)}, u32[]{:S(2)}) collective-permute-start(bf16[64,2048]{1,0:T(8,128)(2,1)S(1)} %shard_map.46), channel_id=1, source_target_pairs={{8,0},{12,4},{0,8},{4,12},{24,16},{28,20},{16,24},{20,28},{9,1},{1... | collective-permute-start | bytes 786440 | tf_op jit(solution)/shard_map/ppermute | solution.py:268
  31.6 10.9 %collective-permute-start.15 = (bf16[64,2048]{1,0:T(8,128)(2,1)S(1)}, bf16[64,2048]{1,0:T(8,128)(2,1)S(1)}, u32[]{:S(2)}, u32[]{:S(2)}) collective-permute-start(bf16[64,2048]{1,0:T(8,128)(2,1)S(1)} %shard_map.47), channel_id=1, source_target_pairs={{8,0},{12,4},{0,8},{4,12},{24,16},{28,20},{16,24},{20,28},{9,1},{1... | collective-permute-start | bytes 786440 | tf_op jit(solution)/shard_map/ppermute | solution.py:268
  35.6 10.5 %collective-permute-start.12 = (f32[2,2,80,128]{3,2,1,0:T(8,128)S(1)}, f32[2,2,80,128]{3,2,1,0:T(8,128)S(1)}, u32[]{:S(2)}, u32[]{:S(2)}) collective-permute-start(f32[2,2,80,128]{3,2,1,0:T(8,128)S(1)} %get-tuple-element.61), channel_id=1, source_target_pairs={{1,0},{0,1},{3,2},{2,3},{5,4},{4,5},{7,6},{6,7},{9,8},{8,9},{11,10... | collective-permute-start | bytes 491528 | tf_op jit(solution)/shard_map/ppermute | solution.py:330
  37.1 5.3 %collective-permute-start.6 = (f32[2,1,80,128]{3,2,0,1:T(8,128)S(1)}, f32[2,1,80,128]{3,2,0,1:T(8,128)S(1)}, u32[]{:S(2)}, u32[]{:S(2)}) collective-permute-start(f32[2,1,80,128]{3,2,0,1:T(8,128)S(1)} %bitcast.23), channel_id=1, source_target_pairs={{2,0},{3,1},{0,2},{1,3},{6,4},{7,5},{4,6},{5,7},{10,8},{11,9},{8,1... | collective-permute-start | bytes 245768 | tf_op jit(solution)/shard_map/ppermute | solution.py:271
  42.5 14.3 %copy-start = (s32[1,5]{1,0:T(1,128)S(1)}, s32[1,5]{1,0:T(1,128)}, u32[]{:S(2)}) copy-start(s32[1,5]{1,0:T(1,128)} %live_ref.1) | copy-start | bytes 64
  44.2 5.8 %collective-permute-start.16 = (f32[2,2,80,128]{3,2,1,0:T(8,128)S(1)}, f32[2,2,80,128]{3,2,1,0:T(8,128)S(1)}, u32[]{:S(2)}, u32[]{:S(2)}) collective-permute-start(f32[2,2,80,128]{3,2,1,0:T(8,128)S(1)} %get-tuple-element.68), channel_id=1, source_target_pairs={{1,0},{0,1},{3,2},{2,3},{5,4},{4,5},{7,6},{6,7},{9,8},{8,9},{11,10... | collective-permute-start | bytes 491528 | tf_op jit(solution)/shard_map/ppermute | solution.py:271
  46.1 8.3 %collective-permute-start.13 = (f32[4,80,128]{2,1,0:T(8,128)S(1)}, f32[4,80,128]{2,1,0:T(8,128)S(1)}, u32[]{:S(2)}, u32[]{:S(2)}) collective-permute-start(f32[4,80,128]{2,1,0:T(8,128)S(1)} %get-tuple-element.63), channel_id=1, source_target_pairs={{2,0},{3,1},{0,2},{1,3},{6,4},{7,5},{4,6},{5,7},{10,8},{11,9},{8,1... | collective-permute-start | bytes 491528 | tf_op jit(solution)/shard_map/ppermute | solution.py:337
  50.0 5.5 %collective-permute-start.17 = (f32[2,1,80,128]{3,2,0,1:T(8,128)S(1)}, f32[2,1,80,128]{3,2,0,1:T(8,128)S(1)}, u32[]{:S(2)}, u32[]{:S(2)}) collective-permute-start(f32[2,1,80,128]{3,2,0,1:T(8,128)S(1)} %bitcast.24), channel_id=1, source_target_pairs={{2,0},{3,1},{0,2},{1,3},{6,4},{7,5},{4,6},{5,7},{10,8},{11,9},{8,1... | collective-permute-start | bytes 245768 | tf_op jit(solution)/shard_map/ppermute | solution.py:271
  54.5 2.3 %collective-permute-start.18 = (f32[3,80,128]{2,1,0:T(8,128)S(1)}, f32[3,80,128]{2,1,0:T(8,128)S(1)}, u32[]{:S(2)}, u32[]{:S(2)}) collective-permute-start(f32[3,80,128]{2,1,0:T(8,128)S(1)} %shard_map.50), channel_id=1, source_target_pairs={{4,0},{0,4},{12,8},{8,12},{20,16},{16,20},{28,24},{24,28},{5,1},{1... | collective-permute-start | bytes 368648 | tf_op jit(solution)/shard_map/ppermute | solution.py:268
  55.5 1.2 %collective-permute-start.19 = (f32[1,80,128]{2,1,0:T(8,128)S(1)}, f32[1,80,128]{2,1,0:T(8,128)S(1)}, u32[]{:S(2)}, u32[]{:S(2)}) collective-permute-start(f32[1,80,128]{2,1,0:T(8,128)S(1)} %shard_map.51), channel_id=1, source_target_pairs={{4,0},{0,4},{12,8},{8,12},{20,16},{16,20},{28,24},{24,28},{5,1},{1... | collective-permute-start | bytes 122888 | tf_op jit(solution)/shard_map/ppermute | solution.py:268

commit v6 on v5

--- a/solution.py
+++ b/solution.py
@@ -18,7 +18,6 @@
     "F3": ("F0", "S", "Ub"),
     "F3X1": ("F2X0a",),
     "X0": ("S", "Ua"),
-    "X1": ("F0F1k",),
     "X2": ("F0F1a", "Ua"),
     "X2X3": ("F0F1b",),
     "X3": ("F2X0k",),

time: 58.5 us -> 58.5 us (level)
  no operation moved by 1% of the time
where the time goes in v6:
time: 58.5 us; the launch traced here: 58.2 us
  starting transfers between devices  27.7 us (47%)
  waiting for transfers between devices  18.8 us (32%)
  Pallas kernels  11.6 us (20%)
    ppermute x6, waiting for transfers between devices, halve(): got = lax.ppermute(send, 'seg', [(i ^ distance, i) for i in range(members)])  14.5 us
    ppermute x6, starting transfers between devices, halve(): got = lax.ppermute(send, 'seg', [(i ^ distance, i) for i in range(members)])  13.4 us
    pallas_call x16, Pallas kernels, call(): pl.pallas_call(kernel, in_specs=specs or [VMEM] * len(operands), out_spec...  11.6 us
    ppermute x7, starting transfers between devices, exchange(): return lax.ppermute(c, 'stn', [(i ^ distance, i) for i in ids])  5.87 us
    ppermute x4, starting transfers between devices, four_of(): lax.ppermute(value, 'stn', [((i - 4) % blocks, i) for i in ids])  4.11 us
    ppermute x2, starting transfers between devices, unit(): got = lax.ppermute(send, 'seg', [(i ^ distance, i) for i in range(members)])  3 us
    ppermute x2, waiting for transfers between devices, unit(): got = lax.ppermute(send, 'seg', [(i ^ distance, i) for i in range(members)])  1.68 us
    ppermute x1, starting transfers between devices, unit(): lax.ppermute(sent, 'seg', [(i ^ distance, i) for i in range(members)])  1.34 us
  transfers between devices with their start and end apart: 20, of which 9 were waited for; matrix products, arithmetic and copies ran while one was open for 0% of the time, Pallas kernels for 12%

profile of v6, /device:TPU:0, one launch (start us, length us, event | category | flops | bytes accessed | tf_op | source)
XLA Modules:
  0.0 58.2 jit_solution(6183620189581632783)
XLA Ops:
  0.0 3.1 %shard_map.37 = (bf16[8,64]{1,0:T(8,128)(2,1)S(1)}, bf16[64,2048]{1,0:T(8,128)(2,1)S(1)}, bf16[64,2048]{1,0:T(8,128)(2,1)S(1)}, bf16[64,2048]{1,0:T(8,128)(2,1)S...) custom-call(bf16[64,5,1,2,2048]{4,3,2,1,0:T(2,128)(2,1)} %x_hbm.1, ...), custom_call_target="tpu_custom_call" | custom-call | tf_op jit(solution)/shard_map/pallas_call | solution.py:239
  3.1 0.5 collective-permute-start.2
  3.6 2.6 %collective-permute-start.3 = (bf16[64,2048]{1,0:T(8,128)(2,1)S(1)}, bf16[64,2048]{1,0:T(8,128)(2,1)S(1)}, u32[]{:S(2)}, u32[]{:S(2)}) collective-permute-start(bf16[64,2048]{1,0:T(8,128)(2,1)S(1)} %get-tuple-element.51.refs_2_.own_ref.refs_3_), channel_id=1, source_target_pairs={{16,0},{20,4},{24,8},{28,12},{0,16},{4,20},{8,24},{12,28},{17,1},{... | collective-permute-start | bytes 786440 | tf_op jit(solution)/shard_map/ppermute | solution.py:299
  6.2 1.6 %collective-permute-start = (f32[2,80,256]{2,1,0:T(8,128)S(1)}, f32[2,80,256]{2,1,0:T(8,128)S(1)}, u32[]{:S(2)}, u32[]{:S(2)}) collective-permute-start(f32[2,80,256]{2,1,0:T(8,128)S(1)} %get-tuple-element.38), channel_id=1, source_target_pairs={{1,0},{0,1},{3,2},{2,3},{5,4},{4,5},{7,6},{6,7},{9,8},{8,9},{11,10... | collective-permute-start | bytes 491528 | tf_op jit(solution)/shard_map/ppermute | solution.py:270
  7.8 0.5 collective-permute-start.4
  8.3 4.2 %collective-permute-done.got_ref = f32[2,80,256]{2,1,0:T(8,128)S(1)} collective-permute-done((f32[2,80,256]{2,1,0:T(8,128)S(1)}, f32[2,80,256]{2,1,0:T(8,128)S(1)}, u32[]{:S(2)}, u32[]{:S(2)}) %collective-permute-start) | collective-permute-done | bytes 163872 | tf_op jit(solution)/shard_map/ppermute | solution.py:270
  12.5 2.7 %collective-permute-start.1 = (f32[1,80,256]{2,1,0:T(8,128)S(1)}, f32[1,80,256]{2,1,0:T(8,128)S(1)}, u32[]{:S(2)}, u32[]{:S(2)}) collective-permute-start(f32[1,80,256]{2,1,0:T(8,128)S(1)} %get-tuple-element.40), channel_id=1, source_target_pairs={{2,0},{3,1},{0,2},{1,3},{6,4},{7,5},{4,6},{5,7},{10,8},{11,9},{8,1... | collective-permute-start | bytes 245768 | tf_op jit(solution)/shard_map/ppermute | solution.py:270
  15.1 0.0 collective-permute-done.2.sib_ref
  15.1 0.0 collective-permute-done.3.refs_0_.four_ref
  15.2 1.6 %collective-permute-start.8 = (bf16[64,2048]{1,0:T(8,128)(2,1)S(1)}, bf16[64,2048]{1,0:T(8,128)(2,1)S(1)}, u32[]{:S(2)}, u32[]{:S(2)}) collective-permute-start(bf16[64,2048]{1,0:T(8,128)(2,1)S(1)} %shard_map.41), channel_id=1, source_target_pairs={{8,0},{12,4},{0,8},{4,12},{24,16},{28,20},{16,24},{20,28},{9,1},{1... | collective-permute-start | bytes 786440 | tf_op jit(solution)/shard_map/ppermute | solution.py:267
  16.7 0.5 collective-permute-start.7
  17.2 1.8 %collective-permute-done.1 = f32[1,80,256]{2,1,0:T(8,128)S(1)} collective-permute-done((f32[1,80,256]{2,1,0:T(8,128)S(1)}, f32[1,80,256]{2,1,0:T(8,128)S(1)}, u32[]{:S(2)}, u32[]{:S(2)}) %collective-permute-start.1) | collective-permute-done | bytes 81952 | tf_op jit(solution)/shard_map/ppermute | solution.py:270
  19.0 0.5 collective-permute-start.10
  19.5 0.0 collective-permute-done.4.refs_1_.four_ref
  19.5 1.8 %shard_map.39 = (f32[2,2,80,128]{3,2,1,0:T(8,128)S(1)}, f32[2,2,80,128]{3,2,1,0:T(8,128)S(1)}) custom-call(bf16[640,2048]{1,0:T(8,128)(2,1)S(1)} %get-tuple-element.41.a_ref, bf16[640,2048]{1,0:T(8,128)(2,1)S(1)} %collective-permute-done.2.sib_ref, bf16[64,2048]{1,0:T(8,128)(2,1)S(1)} %collective-permute-done.3.refs_0_.four_ref, ...), custom_call_target="tpu_custom_call" | custom-call | tf_op jit(solution)/shard_map/pallas_call | solution.py:239
  21.3 1.5 %collective-permute-start.5 = (f32[2,2,80,128]{3,2,1,0:T(8,128)S(1)}, f32[2,2,80,128]{3,2,1,0:T(8,128)S(1)}, u32[]{:S(2)}, u32[]{:S(2)}) collective-permute-start(f32[2,2,80,128]{3,2,1,0:T(8,128)S(1)} %get-tuple-element.46), channel_id=1, source_target_pairs={{1,0},{0,1},{3,2},{2,3},{5,4},{4,5},{7,6},{6,7},{9,8},{8,9},{11,10... | collective-permute-start | bytes 491528 | tf_op jit(solution)/shard_map/ppermute | solution.py:270
  22.9 1.6 %collective-permute-start.11 = (bf16[64,2048]{1,0:T(8,128)(2,1)S(1)}, bf16[64,2048]{1,0:T(8,128)(2,1)S(1)}, u32[]{:S(2)}, u32[]{:S(2)}) collective-permute-start(bf16[64,2048]{1,0:T(8,128)(2,1)S(1)} %shard_map.43), channel_id=1, source_target_pairs={{8,0},{12,4},{0,8},{4,12},{24,16},{28,20},{16,24},{20,28},{9,1},{1... | collective-permute-start | bytes 786440 | tf_op jit(solution)/shard_map/ppermute | solution.py:267
  24.4 2.3 %collective-permute-done.5 = f32[2,2,80,128]{3,2,1,0:T(8,128)S(1)} collective-permute-done((f32[2,2,80,128]{3,2,1,0:T(8,128)S(1)}, f32[2,2,80,128]{3,2,1,0:T(8,128)S(1)}, u32[]{:S(2)}, u32[]{:S(2)}) %collective-permute-start.5) | collective-permute-done | bytes 163872 | tf_op jit(solution)/shard_map/ppermute | solution.py:270
  26.7 0.0 collective-permute-done.8.refs_1_
  26.8 0.0 collective-permute-done.7.refs_0_.four_ref
  26.8 1.7 %shard_map.42 = (f32[2,2,80,128]{3,2,1,0:T(8,128)S(1)}, f32[2,2,80,128]{3,2,1,0:T(8,128)S(1)}) custom-call(bf16[640,2048]{1,0:T(8,128)(2,1)S(1)} %get-tuple-element.41.a_ref, bf16[640,2048]{1,0:T(8,128)(2,1)S(1)} %collective-permute-done.2.sib_ref, bf16[64,2048]{1,0:T(8,128)(2,1)S(1)} %collective-permute-done.7.refs_0_.four_ref, ...), custom_call_target="tpu_custom_call" | custom-call | tf_op jit(solution)/shard_map/pallas_call | solution.py:239
  28.5 1.5 %collective-permute-start.9 = (f32[2,2,80,128]{3,2,1,0:T(8,128)S(1)}, f32[2,2,80,128]{3,2,1,0:T(8,128)S(1)}, u32[]{:S(2)}, u32[]{:S(2)}) collective-permute-start(f32[2,2,80,128]{3,2,1,0:T(8,128)S(1)} %get-tuple-element.54), channel_id=1, source_target_pairs={{1,0},{0,1},{3,2},{2,3},{5,4},{4,5},{7,6},{6,7},{9,8},{8,9},{11,10... | collective-permute-start | bytes 491528 | tf_op jit(solution)/shard_map/ppermute | solution.py:329
  30.0 1.6 %collective-permute-start.14 = (bf16[64,2048]{1,0:T(8,128)(2,1)S(1)}, bf16[64,2048]{1,0:T(8,128)(2,1)S(1)}, u32[]{:S(2)}, u32[]{:S(2)}) collective-permute-start(bf16[64,2048]{1,0:T(8,128)(2,1)S(1)} %shard_map.46), channel_id=1, source_target_pairs={{8,0},{12,4},{0,8},{4,12},{24,16},{28,20},{16,24},{20,28},{9,1},{1... | collective-permute-start | bytes 786440 | tf_op jit(solution)/shard_map/ppermute | solution.py:267
  31.6 0.0 collective-permute-done.10.refs_0_.four_ref
  31.6 0.6 %collective-permute-start.15 = (bf16[64,2048]{1,0:T(8,128)(2,1)S(1)}, bf16[64,2048]{1,0:T(8,128)(2,1)S(1)}, u32[]{:S(2)}, u32[]{:S(2)}) collective-permute-start(bf16[64,2048]{1,0:T(8,128)(2,1)S(1)} %shard_map.47), channel_id=1, source_target_pairs={{8,0},{12,4},{0,8},{4,12},{24,16},{28,20},{16,24},{20,28},{9,1},{1... | collective-permute-start | bytes 786440 | tf_op jit(solution)/shard_map/ppermute | solution.py:267
  32.2 1.7 %collective-permute-done.9.refs_1_ = f32[2,2,80,128]{3,2,1,0:T(8,128)S(1)} collective-permute-done((f32[2,2,80,128]{3,2,1,0:T(8,128)S(1)}, f32[2,2,80,128]{3,2,1,0:T(8,128)S(1)}, u32[]{:S(2)}, u32[]{:S(2)}) %collective-permute-start.9) | collective-permute-done | bytes 163872 | tf_op jit(solution)/shard_map/ppermute | solution.py:329
  33.9 0.0 collective-permute-done.11.refs_1_
  33.9 1.7 %shard_map.44 = (f32[2,2,80,128]{3,2,1,0:T(8,128)S(1)}, f32[2,2,80,128]{3,2,1,0:T(8,128)S(1)}) custom-call(bf16[640,2048]{1,0:T(8,128)(2,1)S(1)} %get-tuple-element.41.a_ref, bf16[640,2048]{1,0:T(8,128)(2,1)S(1)} %collective-permute-done.2.sib_ref, bf16[64,2048]{1,0:T(8,128)(2,1)S(1)} %collective-permute-done.10.refs_0_.four_ref, ...), custom_call_target="tpu_custom_call" | custom-call | tf_op jit(solution)/shard_map/pallas_call | solution.py:239
  35.6 1.5 %collective-permute-start.12 = (f32[2,2,80,128]{3,2,1,0:T(8,128)S(1)}, f32[2,2,80,128]{3,2,1,0:T(8,128)S(1)}, u32[]{:S(2)}, u32[]{:S(2)}) collective-permute-start(f32[2,2,80,128]{3,2,1,0:T(8,128)S(1)} %get-tuple-element.59), channel_id=1, source_target_pairs={{1,0},{0,1},{3,2},{2,3},{5,4},{4,5},{7,6},{6,7},{9,8},{8,9},{11,10... | collective-permute-start | bytes 491528 | tf_op jit(solution)/shard_map/ppermute | solution.py:329
  37.1 2.6 %collective-permute-start.6 = (f32[2,1,80,128]{3,2,0,1:T(8,128)S(1)}, f32[2,1,80,128]{3,2,0,1:T(8,128)S(1)}, u32[]{:S(2)}, u32[]{:S(2)}) collective-permute-start(f32[2,1,80,128]{3,2,0,1:T(8,128)S(1)} %bitcast.23), channel_id=1, source_target_pairs={{2,0},{3,1},{0,2},{1,3},{6,4},{7,5},{4,6},{5,7},{10,8},{11,9},{8,1... | collective-permute-start | bytes 245768 | tf_op jit(solution)/shard_map/ppermute | solution.py:270
  39.7 2.7 %collective-permute-done.6 = f32[2,1,80,128]{3,2,0,1:T(8,128)S(1)} collective-permute-done((f32[2,1,80,128]{3,2,0,1:T(8,128)S(1)}, f32[2,1,80,128]{3,2,0,1:T(8,128)S(1)}, u32[]{:S(2)}, u32[]{:S(2)}) %collective-permute-start.6) | collective-permute-done | bytes 81952 | tf_op jit(solution)/shard_map/ppermute | solution.py:270
  42.5 0.0 copy-start
  42.5 0.0 collective-permute-done.14.refs_0_
  42.5 0.0 collective-permute-done.15.refs_1_
  42.5 1.7 %shard_map.48 = (f32[2,2,80,128]{3,2,1,0:T(8,128)S(1)}, f32[2,2,80,128]{3,2,1,0:T(8,128)S(1)}) custom-call(bf16[640,2048]{1,0:T(8,128)(2,1)S(1)} %get-tuple-element.41.a_ref, bf16[640,2048]{1,0:T(8,128)(2,1)S(1)} %collective-permute-done.2.sib_ref, bf16[64,2048]{1,0:T(8,128)(2,1)S(1)} %collective-permute-done.14.refs_0_, ...), custom_call_target="tpu_custom_call" | custom-call | tf_op jit(solution)/shard_map/pallas_call | solution.py:239
  44.2 1.9 %collective-permute-start.16 = (f32[2,2,80,128]{3,2,1,0:T(8,128)S(1)}, f32[2,2,80,128]{3,2,1,0:T(8,128)S(1)}, u32[]{:S(2)}, u32[]{:S(2)}) collective-permute-start(f32[2,2,80,128]{3,2,1,0:T(8,128)S(1)} %get-tuple-element.66), channel_id=1, source_target_pairs={{1,0},{0,1},{3,2},{2,3},{5,4},{4,5},{7,6},{6,7},{9,8},{8,9},{11,10... | collective-permute-start | bytes 491528 | tf_op jit(solution)/shard_map/ppermute | solution.py:270
  46.1 0.0 collective-permute-done.12.refs_3_
  46.1 1.3 %collective-permute-start.13 = (f32[4,80,128]{2,1,0:T(8,128)S(1)}, f32[4,80,128]{2,1,0:T(8,128)S(1)}, u32[]{:S(2)}, u32[]{:S(2)}) collective-permute-start(f32[4,80,128]{2,1,0:T(8,128)S(1)} %get-tuple-element.61), channel_id=1, source_target_pairs={{2,0},{3,1},{0,2},{1,3},{6,4},{7,5},{4,6},{5,7},{10,8},{11,9},{8,1... | collective-permute-start | bytes 491528 | tf_op jit(solution)/shard_map/ppermute | solution.py:336
  47.5 2.5 %collective-permute-done.16 = f32[2,2,80,128]{3,2,1,0:T(8,128)S(1)} collective-permute-done((f32[2,2,80,128]{3,2,1,0:T(8,128)S(1)}, f32[2,2,80,128]{3,2,1,0:T(8,128)S(1)}, u32[]{:S(2)}, u32[]{:S(2)}) %collective-permute-start.16) | collective-permute-done | bytes 163872 | tf_op jit(solution)/shard_map/ppermute | solution.py:270
  50.0 3.1 %collective-permute-start.17 = (f32[2,1,80,128]{3,2,0,1:T(8,128)S(1)}, f32[2,1,80,128]{3,2,0,1:T(8,128)S(1)}, u32[]{:S(2)}, u32[]{:S(2)}) collective-permute-start(f32[2,1,80,128]{3,2,0,1:T(8,128)S(1)} %bitcast.24), channel_id=1, source_target_pairs={{2,0},{3,1},{0,2},{1,3},{6,4},{7,5},{4,6},{5,7},{10,8},{11,9},{8,1... | collective-permute-start | bytes 245768 | tf_op jit(solution)/shard_map/ppermute | solution.py:270
  53.1 1.3 %collective-permute-done.13.refs_3_.refs_5_.refs_7_ = f32[4,80,128]{2,1,0:T(8,128)S(1)} collective-permute-done((f32[4,80,128]{2,1,0:T(8,128)S(1)}, f32[4,80,128]{2,1,0:T(8,128)S(1)}, u32[]{:S(2)}, u32[]{:S(2)}) %collective-permute-start.13) | collective-permute-done | bytes 163872 | tf_op jit(solution)/shard_map/ppermute | solution.py:336
  54.5 0.1 collective-permute-start.18
  54.5 1.0 %collective-permute-done.17 = f32[2,1,80,128]{3,2,0,1:T(8,128)S(1)} collective-permute-done((f32[2,1,80,128]{3,2,0,1:T(8,128)S(1)}, f32[2,1,80,128]{3,2,0,1:T(8,128)S(1)}, u32[]{:S(2)}, u32[]{:S(2)}) %collective-permute-start.17) | collective-permute-done | bytes 81952 | tf_op jit(solution)/shard_map/ppermute | solution.py:270
  55.5 0.0 collective-permute-start.19
  55.6 1.2 %collective-permute-done.19.refs_11_ = f32[1,80,128]{2,1,0:T(8,128)S(1)} collective-permute-done((f32[1,80,128]{2,1,0:T(8,128)S(1)}, f32[1,80,128]{2,1,0:T(8,128)S(1)}, u32[]{:S(2)}, u32[]{:S(2)}) %collective-permute-start.19) | collective-permute-done | bytes 40992 | tf_op jit(solution)/shard_map/ppermute | solution.py:267
  56.8 0.0 collective-permute-done.18.refs_10_
  56.8 0.0 copy-done
  56.8 1.5 %shard_map.52 = f32[800,128]{1,0:T(8,128)} custom-call(s32[1,5]{1,0:T(1,128)S(1)} %copy-done, f32[80,256]{1,0:T(8,128)S(1)} %bitcast.21, f32[80,256]{1,0:T(8,128)S(1)} %bitcast.22, f32[2,80,128]{2,1,0:T(8,128)S(1)} %get-tuple-element.47.refs_0_.refs_2_, f32[2,80,128]{2,1,0:T(8,128)S(1)} %bitcast.14, ...), custom_call_target="tpu_custom_call" | custom-call | tf_op jit(solution)/shard_map/pallas_call | solution.py:239
  (10 shorter events, 0.2 us)
Async XLA Ops:
  3.1 12.1 %collective-permute-start.2 = (bf16[640,2048]{1,0:T(8,128)(2,1)S(1)}, bf16[640,2048]{1,0:T(8,128)(2,1)S(1)}, u32[]{:S(2)}, u32[]{:S(2)}) collective-permute-start(bf16[640,2048]{1,0:T(8,128)(2,1)S(1)} %get-tuple-element.41.a_ref), channel_id=1, source_target_pairs={{4,0},{0,4},{12,8},{8,12},{20,16},{16,20},{28,24},{24,28},{5,1},{1... | collective-permute-start | bytes 7864328 | tf_op jit(solution)/shard_map/ppermute | solution.py:267
  3.6 11.5 %collective-permute-start.3 = (bf16[64,2048]{1,0:T(8,128)(2,1)S(1)}, bf16[64,2048]{1,0:T(8,128)(2,1)S(1)}, u32[]{:S(2)}, u32[]{:S(2)}) collective-permute-start(bf16[64,2048]{1,0:T(8,128)(2,1)S(1)} %get-tuple-element.51.refs_2_.own_ref.refs_3_), channel_id=1, source_target_pairs={{16,0},{20,4},{24,8},{28,12},{0,16},{4,20},{8,24},{12,28},{17,1},{... | collective-permute-start | bytes 786440 | tf_op jit(solution)/shard_map/ppermute | solution.py:299
  6.2 6.3 %collective-permute-start = (f32[2,80,256]{2,1,0:T(8,128)S(1)}, f32[2,80,256]{2,1,0:T(8,128)S(1)}, u32[]{:S(2)}, u32[]{:S(2)}) collective-permute-start(f32[2,80,256]{2,1,0:T(8,128)S(1)} %get-tuple-element.38), channel_id=1, source_target_pairs={{1,0},{0,1},{3,2},{2,3},{5,4},{4,5},{7,6},{6,7},{9,8},{8,9},{11,10... | collective-permute-start | bytes 491528 | tf_op jit(solution)/shard_map/ppermute | solution.py:270
  7.8 11.8 %collective-permute-start.4 = (bf16[64,2048]{1,0:T(8,128)(2,1)S(1)}, bf16[64,2048]{1,0:T(8,128)(2,1)S(1)}, u32[]{:S(2)}, u32[]{:S(2)}) collective-permute-start(bf16[64,2048]{1,0:T(8,128)(2,1)S(1)} %get-tuple-element.43.refs_3_.own_ref), channel_id=1, source_target_pairs={{16,0},{20,4},{24,8},{28,12},{0,16},{4,20},{8,24},{12,28},{17,1},{... | collective-permute-start | bytes 786440 | tf_op jit(solution)/shard_map/ppermute | solution.py:299
  12.5 6.5 %collective-permute-start.1 = (f32[1,80,256]{2,1,0:T(8,128)S(1)}, f32[1,80,256]{2,1,0:T(8,128)S(1)}, u32[]{:S(2)}, u32[]{:S(2)}) collective-permute-start(f32[1,80,256]{2,1,0:T(8,128)S(1)} %get-tuple-element.40), channel_id=1, source_target_pairs={{2,0},{3,1},{0,2},{1,3},{6,4},{7,5},{4,6},{5,7},{10,8},{11,9},{8,1... | collective-permute-start | bytes 245768 | tf_op jit(solution)/shard_map/ppermute | solution.py:270
  15.2 11.6 %collective-permute-start.8 = (bf16[64,2048]{1,0:T(8,128)(2,1)S(1)}, bf16[64,2048]{1,0:T(8,128)(2,1)S(1)}, u32[]{:S(2)}, u32[]{:S(2)}) collective-permute-start(bf16[64,2048]{1,0:T(8,128)(2,1)S(1)} %shard_map.41), channel_id=1, source_target_pairs={{8,0},{12,4},{0,8},{4,12},{24,16},{28,20},{16,24},{20,28},{9,1},{1... | collective-permute-start | bytes 786440 | tf_op jit(solution)/shard_map/ppermute | solution.py:267
  16.7 10.0 %collective-permute-start.7 = (bf16[64,2048]{1,0:T(8,128)(2,1)S(1)}, bf16[64,2048]{1,0:T(8,128)(2,1)S(1)}, u32[]{:S(2)}, u32[]{:S(2)}) collective-permute-start(bf16[64,2048]{1,0:T(8,128)(2,1)S(1)} %get-tuple-element.62.refs_2_.own_ref), channel_id=1, source_target_pairs={{16,0},{20,4},{24,8},{28,12},{0,16},{4,20},{8,24},{12,28},{17,1},{... | collective-permute-start | bytes 786440 | tf_op jit(solution)/shard_map/ppermute | solution.py:299
  19.0 12.6 %collective-permute-start.10 = (bf16[64,2048]{1,0:T(8,128)(2,1)S(1)}, bf16[64,2048]{1,0:T(8,128)(2,1)S(1)}, u32[]{:S(2)}, u32[]{:S(2)}) collective-permute-start(bf16[64,2048]{1,0:T(8,128)(2,1)S(1)} %get-tuple-element.63.refs_2_.own_ref.refs_3_), channel_id=1, source_target_pairs={{16,0},{20,4},{24,8},{28,12},{0,16},{4,20},{8,24},{12,28},{17,1},{... | collective-permute-start | bytes 786440 | tf_op jit(solution)/shard_map/ppermute | solution.py:299
  21.3 5.4 %collective-permute-start.5 = (f32[2,2,80,128]{3,2,1,0:T(8,128)S(1)}, f32[2,2,80,128]{3,2,1,0:T(8,128)S(1)}, u32[]{:S(2)}, u32[]{:S(2)}) collective-permute-start(f32[2,2,80,128]{3,2,1,0:T(8,128)S(1)} %get-tuple-element.46), channel_id=1, source_target_pairs={{1,0},{0,1},{3,2},{2,3},{5,4},{4,5},{7,6},{6,7},{9,8},{8,9},{11,10... | collective-permute-start | bytes 491528 | tf_op jit(solution)/shard_map/ppermute | solution.py:270
  22.9 11.0 %collective-permute-start.11 = (bf16[64,2048]{1,0:T(8,128)(2,1)S(1)}, bf16[64,2048]{1,0:T(8,128)(2,1)S(1)}, u32[]{:S(2)}, u32[]{:S(2)}) collective-permute-start(bf16[64,2048]{1,0:T(8,128)(2,1)S(1)} %shard_map.43), channel_id=1, source_target_pairs={{8,0},{12,4},{0,8},{4,12},{24,16},{28,20},{16,24},{20,28},{9,1},{1... | collective-permute-start | bytes 786440 | tf_op jit(solution)/shard_map/ppermute | solution.py:267
  28.5 5.4 %collective-permute-start.9 = (f32[2,2,80,128]{3,2,1,0:T(8,128)S(1)}, f32[2,2,80,128]{3,2,1,0:T(8,128)S(1)}, u32[]{:S(2)}, u32[]{:S(2)}) collective-permute-start(f32[2,2,80,128]{3,2,1,0:T(8,128)S(1)} %get-tuple-element.54), channel_id=1, source_target_pairs={{1,0},{0,1},{3,2},{2,3},{5,4},{4,5},{7,6},{6,7},{9,8},{8,9},{11,10... | collective-permute-start | bytes 491528 | tf_op jit(solution)/shard_map/ppermute | solution.py:329
  30.0 12.4 %collective-permute-start.14 = (bf16[64,2048]{1,0:T(8,128)(2,1)S(1)}, bf16[64,2048]{1,0:T(8,128)(2,1)S(1)}, u32[]{:S(2)}, u32[]{:S(2)}) collective-permute-start(bf16[64,2048]{1,0:T(8,128)(2,1)S(1)} %shard_map.46), channel_id=1, source_target_pairs={{8,0},{12,4},{0,8},{4,12},{24,16},{28,20},{16,24},{20,28},{9,1},{1... | collective-permute-start | bytes 786440 | tf_op jit(solution)/shard_map/ppermute | solution.py:267
  31.6 10.9 %collective-permute-start.15 = (bf16[64,2048]{1,0:T(8,128)(2,1)S(1)}, bf16[64,2048]{1,0:T(8,128)(2,1)S(1)}, u32[]{:S(2)}, u32[]{:S(2)}) collective-permute-start(bf16[64,2048]{1,0:T(8,128)(2,1)S(1)} %shard_map.47), channel_id=1, source_target_pairs={{8,0},{12,4},{0,8},{4,12},{24,16},{28,20},{16,24},{20,28},{9,1},{1... | collective-permute-start | bytes 786440 | tf_op jit(solution)/shard_map/ppermute | solution.py:267
  35.6 10.5 %collective-permute-start.12 = (f32[2,2,80,128]{3,2,1,0:T(8,128)S(1)}, f32[2,2,80,128]{3,2,1,0:T(8,128)S(1)}, u32[]{:S(2)}, u32[]{:S(2)}) collective-permute-start(f32[2,2,80,128]{3,2,1,0:T(8,128)S(1)} %get-tuple-element.59), channel_id=1, source_target_pairs={{1,0},{0,1},{3,2},{2,3},{5,4},{4,5},{7,6},{6,7},{9,8},{8,9},{11,10... | collective-permute-start | bytes 491528 | tf_op jit(solution)/shard_map/ppermute | solution.py:329
  37.1 5.3 %collective-permute-start.6 = (f32[2,1,80,128]{3,2,0,1:T(8,128)S(1)}, f32[2,1,80,128]{3,2,0,1:T(8,128)S(1)}, u32[]{:S(2)}, u32[]{:S(2)}) collective-permute-start(f32[2,1,80,128]{3,2,0,1:T(8,128)S(1)} %bitcast.23), channel_id=1, source_target_pairs={{2,0},{3,1},{0,2},{1,3},{6,4},{7,5},{4,6},{5,7},{10,8},{11,9},{8,1... | collective-permute-start | bytes 245768 | tf_op jit(solution)/shard_map/ppermute | solution.py:270
  42.5 14.3 %copy-start = (s32[1,5]{1,0:T(1,128)S(1)}, s32[1,5]{1,0:T(1,128)}, u32[]{:S(2)}) copy-start(s32[1,5]{1,0:T(1,128)} %live_ref.1) | copy-start | bytes 64
  44.2 5.8 %collective-permute-start.16 = (f32[2,2,80,128]{3,2,1,0:T(8,128)S(1)}, f32[2,2,80,128]{3,2,1,0:T(8,128)S(1)}, u32[]{:S(2)}, u32[]{:S(2)}) collective-permute-start(f32[2,2,80,128]{3,2,1,0:T(8,128)S(1)} %get-tuple-element.66), channel_id=1, source_target_pairs={{1,0},{0,1},{3,2},{2,3},{5,4},{4,5},{7,6},{6,7},{9,8},{8,9},{11,10... | collective-permute-start | bytes 491528 | tf_op jit(solution)/shard_map/ppermute | solution.py:270
  46.1 8.3 %collective-permute-start.13 = (f32[4,80,128]{2,1,0:T(8,128)S(1)}, f32[4,80,128]{2,1,0:T(8,128)S(1)}, u32[]{:S(2)}, u32[]{:S(2)}) collective-permute-start(f32[4,80,128]{2,1,0:T(8,128)S(1)} %get-tuple-element.61), channel_id=1, source_target_pairs={{2,0},{3,1},{0,2},{1,3},{6,4},{7,5},{4,6},{5,7},{10,8},{11,9},{8,1... | collective-permute-start | bytes 491528 | tf_op jit(solution)/shard_map/ppermute | solution.py:336
  50.0 5.5 %collective-permute-start.17 = (f32[2,1,80,128]{3,2,0,1:T(8,128)S(1)}, f32[2,1,80,128]{3,2,0,1:T(8,128)S(1)}, u32[]{:S(2)}, u32[]{:S(2)}) collective-permute-start(f32[2,1,80,128]{3,2,0,1:T(8,128)S(1)} %bitcast.24), channel_id=1, source_target_pairs={{2,0},{3,1},{0,2},{1,3},{6,4},{7,5},{4,6},{5,7},{10,8},{11,9},{8,1... | collective-permute-start | bytes 245768 | tf_op jit(solution)/shard_map/ppermute | solution.py:270
  54.5 2.3 %collective-permute-start.18 = (f32[3,80,128]{2,1,0:T(8,128)S(1)}, f32[3,80,128]{2,1,0:T(8,128)S(1)}, u32[]{:S(2)}, u32[]{:S(2)}) collective-permute-start(f32[3,80,128]{2,1,0:T(8,128)S(1)} %shard_map.50), channel_id=1, source_target_pairs={{4,0},{0,4},{12,8},{8,12},{20,16},{16,20},{28,24},{24,28},{5,1},{1... | collective-permute-start | bytes 368648 | tf_op jit(solution)/shard_map/ppermute | solution.py:267
  55.5 1.2 %collective-permute-start.19 = (f32[1,80,128]{2,1,0:T(8,128)S(1)}, f32[1,80,128]{2,1,0:T(8,128)S(1)}, u32[]{:S(2)}, u32[]{:S(2)}) collective-permute-start(f32[1,80,128]{2,1,0:T(8,128)S(1)} %shard_map.51), channel_id=1, source_target_pairs={{4,0},{0,4},{12,8},{8,12},{20,16},{16,20},{28,24},{24,28},{5,1},{1... | collective-permute-start | bytes 122888 | tf_op jit(solution)/shard_map/ppermute | solution.py:267
